TPU v7x, 256 devices: a whole 4x4x8 slice. The times are simulated.
256 devices in a mesh: pix: 32 (over z, y), shell: 8 (over x, core).
Axes of the slice: x: 4, y: 4, z: 8, core: 2. Of those that a mesh axis runs over, the one named last changes fastest.
Arguments:
- field: float32 [128, 1048576], P('shell', 'pix'), may hold values from -3 to 3
- momentum: float32 [128, 1048576], P('shell', 'pix'), may hold values from -6 to 6
- kernels: float32 [4, 20, 128], P(None, None, 'shell'), may hold values from 0.002 to 0.02
- depth_class: int32 [1048576], P('pix'), may hold values from 0 to 3
- counts: int32 [20, 1048576], P(None, 'pix'), may hold values from 0 to 12
- mask: float32 [1048576], P('pix'), may hold values from 0.1 to 1.5, as said below
- mean_counts: float32 [20], replicated, may hold values from 1 to 8
- shell_scale: float32 [128], P('shell'), may hold values from 0.5 to 2
Outputs:
- gradient: float32 [128, 1048576], P('shell', 'pix')
- loglik: float32 [], replicated
Inputs may be any that keep to these rules, and one draw needn't show every extreme that they name: `mask`: mask weights are positive.
All inputs are finite; a program needn't handle non-finite values.
Results may differ from a plain program's by a relative error of at most 0.00005.
Values sent between devices are 32-bit elements; how exact they have to be, the bound alone decides.
No kernel may reach another device: no remote copies, remote signals or barrier semaphores. Data moves between devices by JAX's collectives and lax.ppermute only.
A program may use at most 128 MiB of HBM per device.

v0:
```python
import jax
import jax.numpy as jnp
from jax import lax
from jax.sharding import PartitionSpec as P

CYCLE = 2048


LEAP = 0.1
ANGULAR = 0.5
RADIAL = 0.5


def padded_2(cells, sides, width):
    for axis, dim in sides:
        count = lax.axis_size(axis)
        ends = count - 1
        head = lax.slice_in_dim(cells, 0, width, axis=dim)
        tail = lax.slice_in_dim(cells, cells.shape[dim] - width, cells.shape[dim], axis=dim)
        cells = jnp.concatenate(
            [
                lax.ppermute(tail, axis, [(i, (i + 1) % count) for i in range(ends)]),
                cells,
                lax.ppermute(head, axis, [((i + 1) % count, i) for i in range(ends)]),
            ],
            axis=dim,
        )
    return cells


def shards(field, momentum, kernels, depth_class, counts, mask, mean_counts, shell_scale):
    shells_here, pixels = field.shape
    classes, bins, _ = kernels.shape
    total_pix = pixels * lax.axis_size("pix")
    position = field + LEAP * momentum
    density = jnp.exp(position)
    flat = kernels.reshape(classes * bins, shells_here)
    onehot = (depth_class[None, :] == jnp.arange(classes, dtype=jnp.int32)[:, None]).astype(
        jnp.float32
    )
    every = jnp.dot(
        flat, density, precision=lax.Precision.HIGHEST, preferred_element_type=jnp.float32
    )
    partial_proj = jnp.sum(every.reshape(classes, bins, pixels) * onehot[:, None, :], axis=0)
    counted = counts.astype(jnp.float32)
    proj = lax.psum(partial_proj, "shell")
    weighted, total = lax.psum(
        (jnp.sum(mask[None, :] * proj, axis=1), jnp.sum(counted, axis=1)), "pix"
    )
    norm = weighted / total_pix
    rate = mean_counts[:, None] * mask[None, :] * proj / norm[:, None]
    local_sum = jnp.sum(counted * jnp.log(rate) - rate)
    loglik = lax.psum(local_sum, "pix") / (bins * total_pix)
    ratio = counted / proj - (total / (total_pix * norm))[:, None] * mask[None, :]
    padded = padded_2(position, (("pix", 1),), CYCLE)
    angular = (
        4.0 * position
        - padded[:, CYCLE - 1 : CYCLE - 1 + pixels]
        - padded[:, CYCLE + 1 : CYCLE + 1 + pixels]
    )
    angular = angular - padded[:, 0:pixels] - padded[:, 2 * CYCLE : 2 * CYCLE + pixels]
    stacked = padded_2(position, (("shell", 0),), 1)
    radial = 2.0 * position - stacked[:-2] - stacked[2:]
    spread = (onehot[:, None, :] * ratio[None, :, :]).reshape(classes * bins, pixels)
    back = lax.dot_general(
        flat,
        spread,
        (((0,), (0,)), ((), ())),
        precision=lax.Precision.HIGHEST,
        preferred_element_type=jnp.float32,
    )
    like = density * back
    gradient = (
        like
        - position / (shell_scale[:, None] * shell_scale[:, None])
        - ANGULAR * angular
        - RADIAL * radial
    )
    return (gradient, loglik)


def solution(mesh):
    placed = (
        P("shell", "pix"),
        P("shell", "pix"),
        P(None, None, "shell"),
        P("pix"),
        P(None, "pix"),
        P("pix"),
        P(),
        P("shell"),
    )
    return jax.shard_map(
        shards, mesh=mesh, in_specs=placed, out_specs=(P("shell", "pix"), P()), check_vma=False
    )
```

profile of v0, /device:TPU:8, one launch (start us, length us, event | category | flops | bytes accessed | tf_op | source)
XLA Modules:
  0.0 298.6 jit_solution(3591351216382486892)
XLA Ops:
  7.2 0.0 all-reduce.3.cloned.1.call-start
  7.2 0.8 copy.10
  8.0 0.1 reshape.36
  8.1 2.5 multiply_add_fusion
  10.5 10.9 %convolution_bitcast_fusion = f32[80,32768]{1,0:T(8,128)} fusion(f32[80,16]{0,1:T(8,128)S(1)} %reshape.36, f32[16,32768]{1,0:T(8,128)S(1)} %multiply_add_fusion), kind=kOutput, calls=%fused_computation | convolution fusion | flops 503316480 | bytes 12588032 | tf_op jit(solution)/shard_map/dot_general | solution.py:41
  21.4 11.4 %reshape.37 = f32[4,20,32768]{2,1,0:T(8,128)} reshape(f32[80,32768]{1,0:T(8,128)} %convolution_bitcast_fusion) | data formatting | bytes 20971520 | tf_op jit(solution)/shard_map/reshape | solution.py:44
  32.8 0.1 fusion.20
  32.9 0.8 copy-done.2
  33.7 8.0 %multiply_reduce_fusion = f32[20,32768]{1,0:T(8,128)} fusion(f32[4,20,32768]{2,1,0:T(8,128)} %reshape.37, f32[4,32768]{1,0:T(4,128)S(1)} %fusion.20), kind=kLoop, calls=%fused_computation.5 | loop fusion | flops 4587520 | bytes 13631488 | tf_op jit(solution)/shard_map/reduce_sum | solution.py:44
  41.7 0.0 all-reduce.3.cloned.1.call-update
  41.8 0.0 copy-start.6
  41.8 0.0 copy-start.5
  41.8 3.6 %collective-permute-start = (f32[16,2048]{1,0:T(8,128)S(1)}, f32[16,2048]{1,0:T(8,128)}, u32[]{:S(2)}, u32[]{:S(2)}) collective-permute-start(f32[16,2048]{1,0:T(8,128)S(1)} %get-tuple-element.8), channel_id=1, source_target_pairs={{0,8},{8,16},{16,24},{24,32},{32,40},{40,48},{48,56},{56,64},{64,7... | collective-permute-start | bytes 393224 | tf_op jit(solution)/shard_map/ppermute | solution.py:22
  45.4 3.0 %collective-permute-start.1 = (f32[16,2048]{1,0:T(8,128)S(1)}, f32[16,2048]{1,0:T(8,128)}, u32[]{:S(2)}, u32[]{:S(2)}) collective-permute-start(f32[16,2048]{1,0:T(8,128)S(1)} %get-tuple-element.9), channel_id=1, source_target_pairs={{8,0},{16,8},{24,16},{32,24},{40,32},{48,40},{56,48},{64,56},{72,6... | collective-permute-start | bytes 393224 | tf_op jit(solution)/shard_map/ppermute | solution.py:24
  48.5 0.9 fusion.21
  49.3 1.9 collective-permute-start.2
  51.3 1.3 collective-permute-start.3
  52.6 66.3 %all-reduce.3.cloned.1.call-done = f32[20,32768]{1,0:T(8,128)} async-done(((f32[20,32768]{1,0:T(8,128)}), f32[20,32768]{1,0:T(8,128)}) %all-reduce.3.cloned.1.call-update) | async-done | bytes 2621456 | tf_op jit(solution)/shard_map/psum | solution.py:46
  118.9 2.4 multiply_reduce_fusion.1
  121.3 71.1 %psum.30 = f32[20]{0:T(128)S(1)} all-reduce(f32[20]{0:T(128)S(1)} %multiply_reduce_fusion.1), channel_id=1, replica_groups=mesh['pix'=32,'shell'=8] {'pix'}, use_global_device_ids=true, to_apply=%region_5.0 | all-reduce | flops 20 | bytes 160 | tf_op jit(solution)/shard_map/psum | solution.py:47
  192.5 3.6 %subtract_reduce_fusion = (f32[]{:T(128)}, f32[20]{0:T(128)S(1)}) fusion(f32[20,32768]{1,0:T(8,128)S(1)} %copy-done, s32[20,32768]{1,0:T(8,128)} %param.12, f32[20]{0:T(128)S(1)} %broadcast_multiply_fusion, f32[20]{0:T(128)S(1)} %copy-done.5, f32[32768]{0:T(1024)S(1)} %copy-done.3), kind=kLoop, calls=%fused_computation.8 | loop fusion | flops 5242859 | bytes 5374196 | tf_op jit(solution)/shard_map/reduce_sum | solution.py:52
  196.1 74.9 %all-reduce = (f32[20]{0:T(128)S(1)}, f32[]{:T(128)}) all-reduce(f32[20]{0:T(128)S(1)} %get-tuple-element.3, f32[]{:T(128)} %get-tuple-element.2), channel_id=1, replica_groups=mesh['pix'=32,'shell'=8] {'pix'}, use_global_device_ids=true, to_apply=%region_3.0 | all-reduce | flops 21 | bytes 168 | tf_op jit(solution)/shard_map/psum | solution.py:47
  271.1 4.1 %multiply_subtract_fusion = f32[20,32768]{1,0:T(8,128)} fusion(f32[20,32768]{1,0:T(8,128)S(1)} %copy-done, s32[20,32768]{1,0:T(8,128)} %param.12, f32[20]{0:T(128)S(1)} %div.29, f32[32768]{0:T(1024)S(1)} %copy-done.3), kind=kLoop, calls=%fused_computation.9 | loop fusion | flops 2621440 | bytes 7995472 | tf_op jit(solution)/shard_map/sub | solution.py:54
  275.9 14.8 %fusion.11 = f32[16,32768]{1,0:T(8,128)} fusion(f32[16,32768]{1,0:T(8,128)} %copy-done.1, f32[16,2048]{1,0:T(8,128)} %collective-permute-done.1, f32[16,2048]{1,0:T(8,128)} %collective-permute-done, f32[1,32768]{1,0:T(1,128)} %collective-permute-done.3, f32[1,32768]{1,0:T(1,128)} %collective-permute-done.2, f32[4,20,16]{1,2,0:T(8,128)} %param.10, ...), kind=kOutput, calls=%fused_computation.22 | convolution fusion | flops 516947968 | bytes 7869504 | tf_op jit(solution)/shard_map/dot_general | solution.py:65
  (19 shorter events, 0.1 us)
Async XLA Ops:
  7.2 111.7 %all-reduce.3.cloned.1.call-start = ((), (), s32[]{:S(2)}) async-start(), calls=%async_computation | async-start | bytes 6291456 | tf_op jit(solution)/shard_map/psum | solution.py:46
  10.5 37.9 %copy-start.1 = (f32[16,32768]{1,0:T(8,128)}, f32[16,32768]{1,0:T(8,128)S(1)}, u32[]{:S(2)}) copy-start(f32[16,32768]{1,0:T(8,128)S(1)} %multiply_add_fusion) | copy-start | bytes 6291460
  21.4 11.4 %copy-start.4 = (s32[32768]{0:T(1024)S(1)}, s32[32768]{0:T(1024)}, u32[]{:S(2)}) copy-start(s32[32768]{0:T(1024)} %param.11) | copy-start | bytes 393220
  32.9 0.8 copy-start.2
  41.7 77.2 %copy-start.3 = (f32[32768]{0:T(1024)S(1)}, f32[32768]{0:T(1024)}, u32[]{:S(2)}) copy-start(f32[32768]{0:T(1024)} %param.13) | copy-start | bytes 393220
  41.8 79.6 %copy-start.6 = (f32[16]{0:T(128)S(1)}, f32[16]{0:T(128)}, u32[]{:S(2)}) copy-start(f32[16]{0:T(128)} %param.15) | copy-start | bytes 196
  41.8 150.7 %copy-start.5 = (f32[20]{0:T(128)S(1)}, f32[20]{0:T(128)}, u32[]{:S(2)}) copy-start(f32[20]{0:T(128)} %param.14) | copy-start | bytes 244
  41.8 234.0 %collective-permute-start = (f32[16,2048]{1,0:T(8,128)S(1)}, f32[16,2048]{1,0:T(8,128)}, u32[]{:S(2)}, u32[]{:S(2)}) collective-permute-start(f32[16,2048]{1,0:T(8,128)S(1)} %get-tuple-element.8), channel_id=1, source_target_pairs={{0,8},{8,16},{16,24},{24,32},{32,40},{40,48},{48,56},{56,64},{64,7... | collective-permute-start | bytes 393224 | tf_op jit(solution)/shard_map/ppermute | solution.py:22
  45.4 230.4 %collective-permute-start.1 = (f32[16,2048]{1,0:T(8,128)S(1)}, f32[16,2048]{1,0:T(8,128)}, u32[]{:S(2)}, u32[]{:S(2)}) collective-permute-start(f32[16,2048]{1,0:T(8,128)S(1)} %get-tuple-element.9), channel_id=1, source_target_pairs={{8,0},{16,8},{24,16},{32,24},{40,32},{48,40},{56,48},{64,56},{72,6... | collective-permute-start | bytes 393224 | tf_op jit(solution)/shard_map/ppermute | solution.py:24
  49.3 226.5 %collective-permute-start.2 = (f32[1,32768]{1,0:T(1,128)}, f32[1,32768]{1,0:T(1,128)}, u32[]{:S(2)}, u32[]{:S(2)}) collective-permute-start(f32[1,32768]{1,0:T(1,128)} %get-tuple-element.6), channel_id=1, source_target_pairs={{0,1},{1,2},{2,3},{3,4},{4,5},{5,6},{6,7},{8,9},{9,10},{10,11},{11... | collective-permute-start | bytes 393224 | tf_op jit(solution)/shard_map/ppermute | solution.py:22
  51.3 224.6 %collective-permute-start.3 = (f32[1,32768]{1,0:T(1,128)}, f32[1,32768]{1,0:T(1,128)}, u32[]{:S(2)}, u32[]{:S(2)}) collective-permute-start(f32[1,32768]{1,0:T(1,128)} %get-tuple-element.7), channel_id=1, source_target_pairs={{1,0},{2,1},{3,2},{4,3},{5,4},{6,5},{7,6},{9,8},{10,9},{11,10},{12... | collective-permute-start | bytes 393224 | tf_op jit(solution)/shard_map/ppermute | solution.py:24
  118.9 73.6 %copy-start = (f32[20,32768]{1,0:T(8,128)S(1)}, f32[20,32768]{1,0:T(8,128)}, u32[]{:S(2)}) copy-start(f32[20,32768]{1,0:T(8,128)} %all-reduce.3.cloned.1.call-done) | copy-start | bytes 7864324
Sparse Core Ops, SparseCore 0:
  41.9 76.9 all-reduce.2
where the time goes:
time: 299 us
  blocking collectives  146 us (49%)
  waiting for transfers between devices  66.4 us (22%)
  matrix products  25.7 us (9%)
  other arithmetic  20.8 us (7%)
  between operations  15.9 us (5%)
  local copies, waits for them, and re-layouts  14 us (5%)
  starting transfers between devices  9.87 us (3%)
    psum x2, blocking collectives, shards(): lax.psum((jnp.sum(mask[None, :] * proj, axis=1), jnp.sum(counted, axis=1)...  146 us
    psum x1, waiting for transfers between devices, shards(): proj = lax.psum(partial_proj, 'shell')  66.3 us
    dot_general x1, matrix products, shards(): lax.dot_general(flat, spread, (((0,), (0,)), ((), ())), precision=lax.Pre...  14.8 us
    reshape x1, local copies, waits for them, and re-layouts, shards(): every.reshape(classes, bins, pixels) * onehot[:, None, :]  11.4 us
    dot_general x1, matrix products, shards(): jnp.dot(flat, density, precision=lax.Precision.HIGHEST, preferred_element...  10.9 us
    reduce_sum x1, other arithmetic, shards(): jnp.sum(every.reshape(classes, bins, pixels) * onehot[:, None, :], axis=0)  8.02 us
  transfers between devices with their start and end apart: 5, of which 1 were waited for; matrix products, arithmetic and copies ran while one was open for 4% of the time, Pallas kernels for 0%

commit v1 on v0

v1 whole, which is shorter than its diff:
```python
import functools

import jax
import jax.numpy as jnp
from jax import lax
from jax.experimental import pallas as pl
from jax.experimental.pallas import tpu as pltpu
from jax.sharding import PartitionSpec as P


CYCLE = 2048
LEAP = 0.1
ANGULAR = 0.5
RADIAL = 0.5
WIDE = 256


def split(values):
    high = values.astype(jnp.bfloat16)
    low = (values - high.astype(jnp.float32)).astype(jnp.bfloat16)
    return high, low


def iota(shape, dim):
    return lax.broadcasted_iota(jnp.int32, shape, dim)


def dot_nt(a, b):
    return lax.dot_general(a, b, (((1,), (1,)), ((), ())), preferred_element_type=jnp.float32)


def forward_weights(table, classes, bins, shells):
    rows, cols = classes * 2 * bins, 6 * shells
    spread = (iota((rows, bins), 0) % bins == iota((rows, bins), 1)).astype(jnp.bfloat16)
    same_class = iota((rows, classes * shells), 0) // (2 * bins) == (
        iota((rows, classes * shells), 1) // shells
    )
    place = (iota((classes * shells, cols), 0) % shells == iota((classes * shells, cols), 1) % shells)
    place = place.astype(jnp.bfloat16)
    parts = []
    for part in split(table):
        wide = jnp.where(same_class, dot_nt(spread, part), 0.0).astype(jnp.bfloat16)
        parts.append(jnp.dot(wide, place, preferred_element_type=jnp.float32))
    row, col = iota((rows, cols), 0), iota((rows, cols), 1)
    picked = jnp.where(col // (2 * shells) == 2, parts[1], parts[0])
    same_sub = (row // bins) % 2 == (col // shells) % 2
    return jnp.where(same_sub, picked, 0.0).astype(jnp.bfloat16)


def backward_weights(table, classes, bins, shells, depth):
    half = classes * shells
    rows, cols = 2 * half, 3 * depth
    place = iota((bins, cols), 0) == (iota((bins, cols), 1) % depth) % bins
    place = place.astype(jnp.bfloat16)
    parts = []
    for part in split(table):
        once = jnp.dot(part, place, preferred_element_type=jnp.float32)
        parts.append(jnp.concatenate([once, once], axis=0))
    row, col = iota((rows, cols), 0), iota((rows, cols), 1)
    picked = jnp.where(col // depth == 2, parts[1], parts[0])
    same_sub = row // half == (col % depth) // bins
    return jnp.where(same_sub, picked, 0.0).astype(jnp.bfloat16)


def packed_row(row, start, width, bins):
    first = row[:, pl.ds(start, WIDE)]
    second = row[:, pl.ds(start + width, WIDE)]
    return jnp.where(iota((2 * bins, WIDE), 0) < bins, first, second)


def position_of():
    place = lax.axis_index("shell")
    return place // 2, place % 2


def offset_of(half, turn, chip, width):
    return pl.multiple_of((half * 4 + (chip + turn) % 4) * width, width)


def project_piece(
    d, base, field, momentum, depth, mask, weights, proj, density, position, weighted, classes, bins
):
    sub = field.shape[2] // 2
    total = jnp.zeros(weighted.shape, jnp.float32)
    for start in range(0, sub, WIDE):
        halves = []
        for begin in (start, start + sub):
            here = slice(begin, begin + WIDE)
            place = field[d, :, here] + LEAP * momentum[d, :, here]
            values = jnp.exp(place)
            position[d, :, here] = place
            density[d, :, here] = values
            halves.append(values)
        high, low = split(jnp.concatenate(halves, axis=0))
        every = jnp.dot(
            weights[...],
            jnp.concatenate([high, low, high], axis=0),
            preferred_element_type=jnp.float32,
        )
        chosen = packed_row(depth, base + start, sub, bins)
        picked = every[: 2 * bins]
        for k in range(1, classes):
            picked = jnp.where(chosen == k, every[2 * bins * k : 2 * bins * (k + 1)], picked)
        proj[d, :, start : start + WIDE] = picked
        scaled = picked * packed_row(mask, base + start, sub, bins)
        for lane in range(0, WIDE, 128):
            total = total + scaled[:, lane : lane + 128]
    weighted[...] += total


def project_given_body(
    field,
    momentum,
    depth,
    mask,
    table_away,
    proj,
    density,
    position,
    weighted,
    field_kept,
    momentum_kept,
    depth_here,
    mask_here,
    weights,
    field_given,
    momentum_given,
    stage,
    table,
    marks,
    classes,
    bins,
):
    _, shells, width = field_given.shape
    chip, core = position_of()
    copies = [
        pltpu.make_async_copy(depth, depth_here, marks.at[16]),
        pltpu.make_async_copy(mask, mask_here, marks.at[17]),
    ]
    load_table = pltpu.make_async_copy(table_away, table, marks.at[18])
    load_table.start()

    def fetch(half, d, source, target, mark):
        begin = offset_of(half, d, chip, width)
        return pltpu.make_async_copy(
            source.at[:, pl.ds(begin, width)], target.at[d], marks.at[mark]
        )

    for d in range(4):
        copies.append(fetch(1 - core, d, field, field_given, 2 * d))
        copies.append(fetch(1 - core, d, momentum, momentum_given, 2 * d + 1))
    for d in range(4):
        copies.append(fetch(core, d, field, field_kept, 8 + 2 * d))
        copies.append(fetch(core, d, momentum, momentum_kept, 9 + 2 * d))
    for copy in copies:
        copy.start()
    load_table.wait()
    weights[...] = forward_weights(table[...], classes, bins, shells)
    weighted[...] = jnp.zeros_like(weighted)
    copies[0].wait()
    copies[1].wait()
    for d in range(4):
        copies[2 + 2 * d].wait()
        copies[3 + 2 * d].wait()
        project_piece(
            d,
            offset_of(1 - core, d, chip, width),
            field_given,
            momentum_given,
            depth_here,
            mask_here,
            weights,
            proj,
            stage,
            position,
            weighted,
            classes,
            bins,
        )
        copies.append(
            pltpu.make_async_copy(stage.at[d], density.at[d], marks.at[19 + d])
        )
        copies[-1].start()
    for copy in copies[10:]:
        copy.wait()


def in_hbm(*values):
    return [pltpu.with_memory_space_constraint(v, pltpu.HBM) for v in values]


def in_vmem(*values):
    return [pltpu.with_memory_space_constraint(v, pltpu.VMEM) for v in values]


HERE = pl.BlockSpec(memory_space=pltpu.VMEM)
AWAY = pl.BlockSpec(memory_space=pltpu.HBM)


LIMIT = pltpu.CompilerParams(vmem_limit_bytes=16 << 20)


def vmem(*shape, dtype=jnp.float32):
    return pltpu.VMEM(shape, dtype)


def project_given(field, momentum, depth, mask, table, classes, bins):
    shells, pixels = field.shape
    width = pixels // 8
    outs = [
        vmem(4, 2 * bins, width // 2),
        pltpu.HBM((4, shells, width), jnp.float32),
        vmem(4, shells, width),
        vmem(2 * bins, 128),
        vmem(4, shells, width),
        vmem(4, shells, width),
        vmem(1, pixels, dtype=jnp.int32),
        vmem(1, pixels),
        vmem(classes * 2 * bins, 6 * shells, dtype=jnp.bfloat16),
    ]
    return pl.pallas_call(
        functools.partial(project_given_body, classes=classes, bins=bins),
        in_specs=[AWAY] * 5,
        out_specs=[HERE, AWAY] + [HERE] * (len(outs) - 2),
        out_shape=outs,
        scratch_shapes=[
            vmem(4, shells, width),
            vmem(4, shells, width),
            vmem(4, shells, width),
            vmem(*table.shape),
            pltpu.SemaphoreType.DMA((23,)),
        ],
        compiler_params=LIMIT,
        name="project_given",
    )(*in_hbm(field, momentum, depth, mask, table))


def project_kept_body(
    field,
    momentum,
    depth,
    mask,
    weights,
    before,
    proj,
    density,
    position,
    weighted,
    stage,
    marks,
    classes,
    bins,
):
    width = field.shape[2]
    chip, core = position_of()
    weighted[...] = before[...]
    copies = []
    for d in range(4):
        project_piece(
            d,
            offset_of(core, d, chip, width),
            field,
            momentum,
            depth,
            mask,
            weights,
            proj,
            stage,
            position,
            weighted,
            classes,
            bins,
        )
        copies.append(pltpu.make_async_copy(stage.at[d], density.at[d], marks.at[d]))
        copies[-1].start()
    for copy in copies:
        copy.wait()


def project_kept(field, momentum, depth, mask, weights, before, classes, bins):
    _, shells, width = field.shape
    outs = [
        vmem(4, 2 * bins, width // 2),
        pltpu.HBM((4, shells, width), jnp.float32),
        vmem(4, shells, width),
        vmem(2 * bins, 128),
    ]
    return pl.pallas_call(
        functools.partial(project_kept_body, classes=classes, bins=bins),
        in_specs=[HERE] * 6,
        out_specs=[HERE, AWAY, HERE, HERE],
        out_shape=outs,
        scratch_shapes=[vmem(4, shells, width), pltpu.SemaphoreType.DMA((4,))],
        compiler_params=LIMIT,
        name="project_kept",
    )(*in_vmem(field, momentum, depth, mask, weights, before))


def combine_body(kept, partner, given_place, kept_place, own, first, second, third, head, tail):
    chip, core = position_of()
    for d, out in enumerate((own, first, second, third)):
        out[...] = kept[d] + partner[d]
    front, back = (4 - chip) % 4, (7 - chip) % 4
    edge = given_place.shape[2] - CYCLE

    @pl.when(core == 0)
    def _():
        head[...] = kept_place[front, :, :CYCLE]
        tail[...] = given_place[back, :, edge:]

    @pl.when(core == 1)
    def _():
        head[...] = given_place[front, :, :CYCLE]
        tail[...] = kept_place[back, :, edge:]


def combine(kept, partner, given_place, kept_place):
    _, rows, sub = kept.shape
    shells = given_place.shape[1]
    outs = [vmem(rows, sub)] * 4 + [vmem(shells, CYCLE)] * 2
    return pl.pallas_call(
        combine_body,
        in_specs=[HERE] * 4,
        out_specs=[HERE] * 6,
        out_shape=outs,
        compiler_params=LIMIT,
        name="combine",
    )(*in_vmem(kept, partner, given_place, kept_place))


def column(row, count):
    width = row.shape[1]
    at = iota((count, width), 0) % width == iota((count, width), 1)
    wide = jnp.broadcast_to(row, (8, width))
    return exact_rows(wide, at.astype(jnp.bfloat16))[:, :1]


def tally_body(
    counts, after, table, scale, mean, totals, own, weights, square, means, here, marks, deep
):
    bins, pixels = here.shape
    shells = square.shape[0]
    chip, core = position_of()
    part = pixels // 8
    copies = []
    for i in range(8):
        piece = pl.ds(i * part, part)
        copies.append(
            pltpu.make_async_copy(counts.at[:, piece], here.at[:, piece], marks.at[i])
        )
        copies[-1].start()
    weights[...] = backward_weights(table[...], table.shape[0] // shells, bins, shells, deep)
    size = column(scale[...], shells)
    square[...] = jnp.broadcast_to(1.0 / (size * size), square.shape)
    means[...] = jnp.broadcast_to(column(mean[...], 2 * bins), means.shape)
    totals[...] = jnp.zeros_like(totals)
    for i in range(8):
        copies[i].wait()

        def step(j, carry):
            begin = pl.multiple_of(i * part + j * 512, 512)
            some = here[:, pl.ds(begin, 512)]
            return carry + (some[:, :128] + some[:, 128:256]) + (some[:, 256:384] + some[:, 384:])

        total = lax.fori_loop(0, part // 512, step, jnp.zeros((bins, 128), jnp.int32), unroll=2)
        totals[...] += total.astype(jnp.float32)
    base = offset_of(core, 0, chip, part)
    sub = part // 2
    for start in range(0, sub, 512):
        there = slice(start, start + 512)
        own[:bins, there] = here[:, pl.ds(base + start, 512)].astype(jnp.float32)
        own[bins:, there] = here[:, pl.ds(base + sub + start, 512)].astype(jnp.float32)


def tally(counts, after, table, scale, mean):
    bins, pixels = counts.shape
    shells = scale.shape[1]
    deep = -(-2 * bins // 16) * 16
    return pl.pallas_call(
        functools.partial(tally_body, deep=deep),
        in_specs=[AWAY, HERE, pl.BlockSpec(), pl.BlockSpec(), pl.BlockSpec()],
        out_specs=[HERE] * 5,
        out_shape=[
            vmem(bins, 128),
            vmem(2 * bins, pixels // 16),
            vmem(2 * table.shape[0], 3 * deep, dtype=jnp.bfloat16),
            vmem(shells, 128),
            vmem(2 * bins, 128),
        ],
        scratch_shapes=[vmem(bins, pixels, dtype=jnp.int32), pltpu.SemaphoreType.DMA((8,))],
        compiler_params=LIMIT,
        name="tally",
    )(*in_hbm(counts), *in_vmem(after), table, scale, mean)


def stencil_body(
    given, kept, before, after, scale, away, to_partner, to_side, position, out, marks
):
    _, shells, width = given.shape
    pixels = 8 * width
    chip, core = position_of()
    position[:, :CYCLE] = before[...]
    position[:, CYCLE + pixels :] = after[...]
    for d in range(4):
        for source, half in ((given, 1 - core), (kept, core)):
            base = offset_of(half, d, chip, width)
            for start in range(0, width, 1024):
                values = source[d, :, start : start + 1024]
                position[:, pl.ds(CYCLE + base + start, 1024)] = values
                first, last = values[:1], values[shells - 1 :]
                here = pl.ds(base + start, 1024)
                to_partner[:, here] = jnp.where(core == 0, last, first)
                to_side[:, here] = jnp.where(core == 0, first, last)
    inverse = jnp.concatenate([scale[...]] * 4, axis=1)
    row = iota((shells, 512), 0)

    def step(i, carry):
        start = pl.multiple_of(i * 512, 512)
        near = position[:, pl.ds(CYCLE + start - 128, 512 + 256)]
        middle = near[:, 128:640]
        left = pltpu.roll(near, 1, 1)[:, 128:640]
        right = pltpu.roll(near, 767, 1)[:, 128:640]
        early = position[:, pl.ds(start, 512)]
        late = position[:, pl.ds(2 * CYCLE + start, 512)]
        angular = 4.0 * middle - left - right - early - late
        up = jnp.where(row == 0, 0.0, pltpu.roll(middle, 1, 0))
        down = jnp.where(row == shells - 1, 0.0, pltpu.roll(middle, shells - 1, 0))
        radial = 2.0 * middle - up - down
        out[:, pl.ds(start, 512)] = -middle * inverse - ANGULAR * angular - RADIAL * radial
        return carry

    copies = []
    steps = pixels // 4096
    for i in range(8):
        lax.fori_loop(i * steps, (i + 1) * steps, step, 0, unroll=4)
        piece = pl.ds(i * steps * 512, steps * 512)
        copies.append(pltpu.make_async_copy(out.at[:, piece], away.at[:, piece], marks.at[i]))
        copies[-1].start()
    for copy in copies:
        copy.wait()


def stencil(given, kept, before, after, scale):
    _, shells, width = given.shape
    pixels = 8 * width
    return pl.pallas_call(
        stencil_body,
        in_specs=[HERE] * 5,
        out_specs=[AWAY, HERE, HERE],
        out_shape=[
            pltpu.HBM((shells, pixels), jnp.float32), vmem(1, pixels), vmem(1, pixels)
        ],
        scratch_shapes=[
            vmem(shells, pixels + 2 * CYCLE),
            vmem(shells, pixels),
            pltpu.SemaphoreType.DMA((8,)),
        ],
        compiler_params=LIMIT,
        name="stencil",
    )(*in_vmem(given, kept, before, after, scale))


def exact_rows(values, ones):
    total = 0.0
    for _ in range(3):
        part = values.astype(jnp.bfloat16)
        values = values - part.astype(jnp.float32)
        total = total + dot_nt(ones, part)
    return total


def ratio_body(
    own, first, second, third, counts, mask, weighted, totals, later, out, stats
):
    rows, sub = out.shape
    bins = rows // 2
    chip, core = position_of()
    base = offset_of(core, 0, chip, 2 * sub)
    logs = jnp.zeros((rows, 128), jnp.float32)
    for start in range(0, sub, WIDE):
        here = slice(start, start + WIDE)
        proj = own[:, here] + first[:, here] + second[:, here] + third[:, here]
        some = counts[:, here]
        out[:, here] = some / proj
        term = some * jnp.log(proj * packed_row(mask, base + start, sub, bins))
        for lane in range(0, WIDE, 128):
            logs = logs + term[:, lane : lane + 128]
    mine = jnp.where((chip == 0) & (core == 0), totals[...], 0.0)
    gap = jnp.zeros((128 - 2 * rows - bins, 128), jnp.float32)
    sums = jnp.concatenate(
        [weighted[...], logs, mine, gap], axis=0
    )
    row = exact_rows(sums, jnp.ones((8, 128), jnp.bfloat16))[:1]
    stats[...] = jnp.broadcast_to(row[:, None], stats.shape)


def ratio(own, first, second, third, counts, mask, weighted, totals, later, devices):
    return pl.pallas_call(
        ratio_body,
        in_specs=[HERE] * 9,
        out_specs=[HERE, HERE],
        out_shape=[vmem(*own.shape), vmem(devices, 1, 128)],
        compiler_params=LIMIT,
        name="ratio",
    )(*in_vmem(own, first, second, third, counts, mask, weighted, totals, later))


def reduce_body(gathered, mean, level, loglik, bins, total_pix):
    row = jnp.sum(gathered[...], axis=0)
    row = jnp.broadcast_to(row, (8, 128))
    at, lane = iota((2 * bins, 128), 0) % bins, iota((2 * bins, 128), 1)
    pick = jnp.where((lane < 2 * bins) & (lane % bins == at), 1.0, 0.0)
    weighted = exact_rows(row, pick.astype(jnp.bfloat16))[:, :1]
    pick = jnp.where(lane - 4 * bins == at, 1.0, 0.0)
    total = exact_rows(row, pick.astype(jnp.bfloat16))[:, :1]
    norm = weighted / total_pix
    level[...] = jnp.broadcast_to(total / (total_pix * norm), level.shape)
    average = mean[:, :1]
    terms = total * jnp.log(average / norm) - average * (weighted / norm)
    terms = jnp.where(iota(terms.shape, 0) < bins, terms, 0.0)
    lane = iota((8, 128), 1)
    logs = jnp.where((lane >= 2 * bins) & (lane < 4 * bins), row, 0.0)[:1]
    value = jnp.sum(terms, axis=0, keepdims=True) + jnp.sum(logs, axis=1, keepdims=True)
    loglik[...] = jnp.broadcast_to(value / (bins * total_pix), loglik.shape)


def gradient_body(*refs, classes, bins, total_pix, mine):
    quotients, refs = refs[:4], refs[4:]
    density_away, rest_away, depth, mask, weights, partner, side = refs[:7]
    density, rest, stage, marks = refs[-4:]
    _, shells, width = stage.shape
    sub = width // 2
    chip, core = position_of()
    half = core if mine else 1 - core
    loads = []
    for d in range(4):
        base = offset_of(half, d, chip, width)
        loads.append(
            (
                pltpu.make_async_copy(density_away.at[d], density.at[d], marks.at[4 + d]),
                pltpu.make_async_copy(
                    rest_away.at[:, pl.ds(base, width)], rest.at[d], marks.at[8 + d]
                ),
            )
        )
        for load in loads[-1]:
            load.start()
    if mine:
        gathered, mean, out, level, loglik = refs[7:12]
        reduce_body(gathered, mean, level, loglik, bins, total_pix)
    else:
        level, _, out = refs[7:10]
    row = iota((shells, WIDE), 0)
    beside_partner = (row == 0) & (core == 1) | (row == shells - 1) & (core == 0)
    outside = (row == 0) & (core == 0) | (row == shells - 1) & (core == 1)
    share = jnp.concatenate([level[...]] * (WIDE // 128), axis=1)
    filler = jnp.zeros((weights.shape[1] // 3 - 2 * bins, WIDE), jnp.float32)
    copies = []
    for d in range(4):
        base = offset_of(half, d, chip, width)
        for load in loads[d]:
            load.wait()
        for start in range(0, sub, WIDE):
            difference = quotients[d][:, start : start + WIDE]
            difference = difference - share * packed_row(mask, base + start, sub, bins)
            high, low = split(jnp.concatenate([difference, filler], axis=0))
            every = jnp.dot(
                weights[...],
                jnp.concatenate([high, low, high], axis=0),
                preferred_element_type=jnp.float32,
            )
            for k in range(2):
                here = slice(start + k * sub, start + k * sub + WIDE)
                away = pl.ds(base + (start + k * sub), WIDE)
                chosen = depth[:, away]
                begin = k * classes * shells
                back = every[begin : begin + shells]
                for c in range(1, classes):
                    begin += shells
                    back = jnp.where(chosen == c, every[begin : begin + shells], back)
                near = jnp.where(beside_partner, partner[:, away], 0.0)
                near = jnp.where(outside, side[:, away], near)
                stage[d, :, here] = density[d, :, here] * back + (rest[d, :, here] + RADIAL * near)
        copies.append(
            pltpu.make_async_copy(stage.at[d], out.at[:, pl.ds(base, width)], marks.at[d])
        )
        copies[-1].start()
    for copy in copies:
        copy.wait()


def gradient(
    quotients, density, rest, depth, mask, weights, partner, side, extra, previous,
    classes, bins, total_pix,
):
    shells, pixels = rest.shape
    width = pixels // 8
    mine = previous is None
    operands = in_vmem(*quotients) + in_hbm(density, rest)
    operands += in_vmem(depth, mask, weights, partner, side, *extra)
    specs = [HERE] * 4 + [AWAY] * 2 + [HERE] * (len(operands) - 6)
    outs, out_specs, aliases = [jax.ShapeDtypeStruct((shells, pixels), jnp.float32)], [AWAY], {}
    if mine:
        outs += [vmem(2 * bins, 128), jax.ShapeDtypeStruct((8, 128), jnp.float32)]
        out_specs += [HERE, pl.BlockSpec()]
    else:
        aliases = {len(operands): 0}
        operands.append(previous)
        specs.append(AWAY)
    return pl.pallas_call(
        functools.partial(
            gradient_body, classes=classes, bins=bins, total_pix=total_pix, mine=mine
        ),
        in_specs=specs,
        out_specs=out_specs,
        out_shape=outs,
        scratch_shapes=[
            vmem(4, shells, width),
            vmem(4, shells, width),
            vmem(4, shells, width),
            pltpu.SemaphoreType.DMA((12,)),
        ],
        input_output_aliases=aliases,
        compiler_params=LIMIT,
        name="gradient_kept" if mine else "gradient_given",
    )(*operands)


def swap(values):
    count = lax.axis_size("shell")
    return lax.ppermute(values, "shell", [(i, i ^ 1) for i in range(count)])


def beside(values):
    count = lax.axis_size("shell")
    pairs = [(i, i + 1) for i in range(1, count - 1, 2)]
    return lax.ppermute(values, "shell", pairs + [(b, a) for a, b in pairs])


def along(values, step):
    count = lax.axis_size("shell")
    return lax.ppermute(values, "shell", [(i, (i + 2 * step) % count) for i in range(count)])


def halo(values, axis, step):
    count = lax.axis_size(axis)
    pairs = [(i, i + step) for i in range(count) if 0 <= i + step < count]
    return lax.ppermute(values, axis, pairs)


def shards(field, momentum, kernels, depth_class, counts, mask, mean_counts, shell_scale):
    shells, pixels = field.shape
    classes, bins, _ = kernels.shape
    devices = lax.axis_size("pix") * lax.axis_size("shell")
    total_pix = pixels * lax.axis_size("pix")
    table = jnp.transpose(kernels, (0, 2, 1)).reshape(classes * shells, bins)

    given = project_given(
        field,
        momentum,
        depth_class.reshape(1, pixels),
        mask.reshape(1, pixels),
        table,
        classes,
        bins,
    )
    proj, density_given, place_given, weighted, field_kept, momentum_kept = given[:6]
    depth, cover, weights = given[6:]
    proj_partner = swap(proj)
    proj_kept, density_kept, place_kept, weighted = project_kept(
        field_kept, momentum_kept, depth, cover, weights, weighted, classes, bins
    )
    own, first, second, third, head, tail = combine(
        proj_kept, proj_partner, place_given, place_kept
    )
    second = along(second, 2)
    first = along(first, 1)
    third = along(third, 3)
    after = halo(head, "pix", -1)
    before = halo(tail, "pix", 1)
    totals, own_counts, weights, square, mean = tally(
        counts, head, table, shell_scale.reshape(1, shells), mean_counts.reshape(1, bins)
    )
    rest, to_partner, to_side = stencil(place_given, place_kept, before, after, square)
    partner_row = swap(to_partner)
    side_row = beside(to_side)
    quotient, stats = ratio(
        own, first, second, third, own_counts, cover, weighted, totals, to_side, devices
    )

    from_far = along(quotient, 2)
    from_back = along(quotient, 1)
    from_front = along(quotient, 3)
    gathered = lax.all_to_all(stats, ("pix", "shell"), 0, 0)
    mine = [quotient, from_front, from_far, from_back]
    theirs = [swap(q) for q in mine[1:]]
    theirs = [swap(quotient), *theirs]

    common = (rest, depth, cover, weights, partner_row, side_row)
    out, level, loglik = gradient(
        mine, density_kept, *common, (gathered, mean), None, classes, bins, total_pix
    )
    (out,) = gradient(
        theirs, density_given, *common, (level,), out, classes, bins, total_pix
    )
    return out, loglik[0, 0]


def solution(mesh):
    placed = (
        P("shell", "pix"),
        P("shell", "pix"),
        P(None, None, "shell"),
        P("pix"),
        P(None, "pix"),
        P("pix"),
        P(),
        P("shell"),
    )
    return jax.shard_map(
        shards,
        mesh=mesh,
        in_specs=placed,
        out_specs=(P("shell", "pix"), P()),
        check_vma=False,
    )
```

time: 299 us -> 82.9 us (0.28)
  the two profiles are of different devices: /device:TPU:8 before, /device:TPU:1 now
where the time goes in v1:
time: 82.9 us; the launch traced here: 82.6 us
  starting transfers between devices  36.8 us (44%)
  waiting for transfers between devices  25.1 us (30%)
  Pallas kernels  19.3 us (23%)
  between operations  0.95 us (1%)
    all_to_all x1, starting transfers between devices, shards(): gathered = lax.all_to_all(stats, ('pix', 'shell'), 0, 0)  13 us
    ppermute x6, waiting for transfers between devices, along(): lax.ppermute(values, 'shell', [(i, (i + 2 * step) % count) for i in range...  12.2 us
    ppermute x6, starting transfers between devices, swap(): return lax.ppermute(values, 'shell', [(i, i ^ 1) for i in range(count)])  7.99 us
    ppermute x6, starting transfers between devices, along(): lax.ppermute(values, 'shell', [(i, (i + 2 * step) % count) for i in range...  7.73 us
    pallas_call x2, Pallas kernels, gradient(): pl.pallas_call(functools.partial(gradient_body, classes=classes, bins=bin...  6.43 us
    all_to_all x1, waiting for transfers between devices, shards(): gathered = lax.all_to_all(stats, ('pix', 'shell'), 0, 0)  5.93 us
    ppermute x2, starting transfers between devices, halo(): return lax.ppermute(values, axis, pairs)  4.48 us
    pallas_call x1, Pallas kernels, stencil(): pl.pallas_call(stencil_body, in_specs=[HERE] * 5, out_specs=[AWAY, HERE,...  4.39 us
  transfers between devices with their start and end apart: 16, of which 7 were waited for; matrix products, arithmetic and copies ran while one was open for 1% of the time, Pallas kernels for 14%

profile of v1, /device:TPU:1, one launch (start us, length us, event | category | flops | bytes accessed | tf_op | source)
XLA Modules:
  0.0 82.6 jit_solution(8642008621726054756)
XLA Ops:
  0.6 3.4 %project_given.1 = (f32[4,40,2048]{2,1,0:T(8,128)S(1)}, f32[4,16,4096]{2,1,0:T(8,128)}, f32[4,16,4096]{2,1,0:T(8,128)S(1)}, f32[40,128]{1,0:T(8,128)S(1)}, f32[4...) custom-call(f32[16,32768]{1,0:T(8,128)} %field.1, ...), custom_call_target="tpu_custom_call" | custom-call | tf_op jit(solution)/shard_map/project_given/pallas_call | solution.py:221
  4.0 3.3 %collective-permute-start = (f32[4,40,2048]{2,1,0:T(8,128)S(1)}, f32[4,40,2048]{2,1,0:T(8,128)S(1)}, u32[]{:S(2)}, u32[]{:S(2)}) collective-permute-start(f32[4,40,2048]{2,1,0:T(8,128)S(1)} %get-tuple-element.41), channel_id=1, source_target_pairs={{0,1},{1,0},{2,3},{3,2},{4,5},{5,4},{6,7},{7,6},{8,9},{9,8},{10,11... | collective-permute-start | bytes 3932168 | tf_op jit(solution)/shard_map/ppermute | solution.py:631
  7.3 1.8 %project_kept.1 = (f32[4,40,2048]{2,1,0:T(8,128)S(1)}, f32[4,16,4096]{2,1,0:T(8,128)}, f32[4,16,4096]{2,1,0:T(8,128)S(1)}, f32[40,128]{1,0:T(8,128)S(1)}) custom-call(f32[4,16,4096]{2,1,0:T(8,128)S(1)} %get-tuple-element.34.field, f32[4,16,4096]{2,1,0:T(8,128)S(1)} %get-tuple-element.35.momentum, s32[1,32768]{1,0:T(1,128)S(1)} %get-tuple-element.36.depth.refs_6_, ...), custom_call_target="tpu_custom_call" | custom-call | tf_op jit(solution)/shard_map/project_kept/pallas_call | solution.py:288
  10.3 1.9 %collective-permute-start.2 = (f32[40,2048]{1,0:T(8,128)S(1)}, f32[40,2048]{1,0:T(8,128)S(1)}, u32[]{:S(2)}, u32[]{:S(2)}) collective-permute-start(f32[40,2048]{1,0:T(8,128)S(1)} %get-tuple-element.46), channel_id=1, source_target_pairs={{0,4},{1,5},{2,6},{3,7},{4,0},{5,1},{6,2},{7,3},{8,12},{9,13},{10,... | collective-permute-start | bytes 983048 | tf_op jit(solution)/shard_map/ppermute | solution.py:642
  12.2 1.2 %collective-permute-start.3 = (f32[40,2048]{1,0:T(8,128)S(1)}, f32[40,2048]{1,0:T(8,128)S(1)}, u32[]{:S(2)}, u32[]{:S(2)}) collective-permute-start(f32[40,2048]{1,0:T(8,128)S(1)} %get-tuple-element.47), channel_id=1, source_target_pairs={{0,6},{1,7},{2,0},{3,1},{4,2},{5,3},{6,4},{7,5},{8,14},{9,15},{10,... | collective-permute-start | bytes 983048 | tf_op jit(solution)/shard_map/ppermute | solution.py:642
  13.4 3.2 %collective-permute-start.4 = (f32[16,2048]{1,0:T(8,128)S(1)}, f32[16,2048]{1,0:T(8,128)S(1)}, u32[]{:S(2)}, u32[]{:S(2)}) collective-permute-start(f32[16,2048]{1,0:T(8,128)S(1)} %get-tuple-element.52), channel_id=1, source_target_pairs={{0,8},{8,16},{16,24},{24,32},{32,40},{40,48},{48,56},{56,64},{64,7... | collective-permute-start | bytes 393224 | tf_op jit(solution)/shard_map/ppermute | solution.py:648
  16.6 1.3 %collective-permute-start.5 = (f32[16,2048]{1,0:T(8,128)S(1)}, f32[16,2048]{1,0:T(8,128)S(1)}, u32[]{:S(2)}, u32[]{:S(2)}) collective-permute-start(f32[16,2048]{1,0:T(8,128)S(1)} %get-tuple-element.48.after), channel_id=1, source_target_pairs={{8,0},{16,8},{24,16},{32,24},{40,32},{48,40},{56,48},{64,56},{72,6... | collective-permute-start | bytes 393224 | tf_op jit(solution)/shard_map/ppermute | solution.py:648
  17.9 2.1 %tally.1 = (f32[20,128]{1,0:T(8,128)S(1)}, f32[40,2048]{1,0:T(8,128)S(1)}, bf16[128,144]{1,0:T(8,128)(2,1)S(1)}, f32[16,128]{1,0:T(8,128)S(1)}, f32[40,128]{1,0:T(8,128)S(1)}) custom-call(s32[20,32768]{1,0:T(8,128)} %counts.1, f32[16,2048]{1,0:T(8,128)S(1)} %get-tuple-element.48.after, f32[64,20]{1,0:T(8,128)S(1)} %bitcast.9, f32[1,16]{1,0:T(1,128)S(1)} %bitcast.10, ...), custom_call_target="tpu_custom_call" | custom-call | tf_op jit(solution)/shard_map/tally/pallas_call | solution.py:379
  20.0 2.6 %collective-permute-done.5.after = f32[16,2048]{1,0:T(8,128)S(1)} collective-permute-done((f32[16,2048]{1,0:T(8,128)S(1)}, f32[16,2048]{1,0:T(8,128)S(1)}, u32[]{:S(2)}, u32[]{:S(2)}) %collective-permute-start.5) | collective-permute-done | bytes 131104 | tf_op jit(solution)/shard_map/ppermute | solution.py:648
  22.6 4.4 %stencil.1 = (f32[16,32768]{1,0:T(8,128)}, f32[1,32768]{1,0:T(1,128)}, f32[1,32768]{1,0:T(1,128)S(1)}) custom-call(f32[4,16,4096]{2,1,0:T(8,128)S(1)} %get-tuple-element.42.given_place.given, f32[4,16,4096]{2,1,0:T(8,128)S(1)} %get-tuple-element.43.kept_place.kept, f32[16,2048]{1,0:T(8,128)S(1)} %collective-permute-done.4.before, ...), custom_call_target="tpu_custom_call" | custom-call | tf_op jit(solution)/shard_map/stencil/pallas_call | solution.py:446
  27.7 1.0 %ratio.1 = (f32[40,2048]{1,0:T(8,128)S(1)}, f32[256,1,128]{2,1,0:T(1,128)}) custom-call(f32[40,2048]{1,0:T(8,128)S(1)} %get-tuple-element.44.own, f32[40,2048]{1,0:T(8,128)S(1)} %collective-permute-done.1.first, f32[40,2048]{1,0:T(8,128)S(1)} %collective-permute-done.2.second, f32[40,2048]{1,0:T(8,128)S(1)} %collective-permute-done.3.third, ...), custom_call_target="tpu_custom_call" | custom-call | tf_op jit(solution)/shard_map/ratio/pallas_call | solution.py:498
  28.7 1.4 %collective-permute-start.11 = (f32[40,2048]{1,0:T(8,128)S(1)}, f32[40,2048]{1,0:T(8,128)S(1)}, u32[]{:S(2)}, u32[]{:S(2)}) collective-permute-start(f32[40,2048]{1,0:T(8,128)S(1)} %get-tuple-element.55.refs_0_), channel_id=1, source_target_pairs={{0,2},{1,3},{2,4},{3,5},{4,6},{5,7},{6,0},{7,1},{8,10},{9,11},{10,... | collective-permute-start | bytes 983048 | tf_op jit(solution)/shard_map/ppermute | solution.py:642
  30.2 3.1 %collective-permute-start.9 = (f32[40,2048]{1,0:T(8,128)S(1)}, f32[40,2048]{1,0:T(8,128)S(1)}, u32[]{:S(2)}, u32[]{:S(2)}) collective-permute-start(f32[40,2048]{1,0:T(8,128)S(1)} %get-tuple-element.55.refs_0_), channel_id=1, source_target_pairs={{0,4},{1,5},{2,6},{3,7},{4,0},{5,1},{6,2},{7,3},{8,12},{9,13},{10,... | collective-permute-start | bytes 983048 | tf_op jit(solution)/shard_map/ppermute | solution.py:642
  33.3 1.1 %collective-permute-start.6 = (f32[40,2048]{1,0:T(8,128)S(1)}, f32[40,2048]{1,0:T(8,128)S(1)}, u32[]{:S(2)}, u32[]{:S(2)}) collective-permute-start(f32[40,2048]{1,0:T(8,128)S(1)} %get-tuple-element.55.refs_0_), channel_id=1, source_target_pairs={{0,1},{1,0},{2,3},{3,2},{4,5},{5,4},{6,7},{7,6},{8,9},{9,8},{10,11... | collective-permute-start | bytes 983048 | tf_op jit(solution)/shard_map/ppermute | solution.py:631
  34.4 4.6 %collective-permute-done.11.refs_3_ = f32[40,2048]{1,0:T(8,128)S(1)} collective-permute-done((f32[40,2048]{1,0:T(8,128)S(1)}, f32[40,2048]{1,0:T(8,128)S(1)}, u32[]{:S(2)}, u32[]{:S(2)}) %collective-permute-start.11) | collective-permute-done | bytes 327712 | tf_op jit(solution)/shard_map/ppermute | solution.py:642
  39.0 1.8 %collective-permute-start.12 = (f32[40,2048]{1,0:T(8,128)S(1)}, f32[40,2048]{1,0:T(8,128)S(1)}, u32[]{:S(2)}, u32[]{:S(2)}) collective-permute-start(f32[40,2048]{1,0:T(8,128)S(1)} %collective-permute-done.11.refs_3_), channel_id=1, source_target_pairs={{0,1},{1,0},{2,3},{3,2},{4,5},{5,4},{6,7},{7,6},{8,9},{9,8},{10,11... | collective-permute-start | bytes 983048 | tf_op jit(solution)/shard_map/ppermute | solution.py:631
  40.8 6.9 %collective-permute-done.9.refs_2_ = f32[40,2048]{1,0:T(8,128)S(1)} collective-permute-done((f32[40,2048]{1,0:T(8,128)S(1)}, f32[40,2048]{1,0:T(8,128)S(1)}, u32[]{:S(2)}, u32[]{:S(2)}) %collective-permute-start.9) | collective-permute-done | bytes 327712 | tf_op jit(solution)/shard_map/ppermute | solution.py:642
  47.6 1.3 %collective-permute-start.10 = (f32[40,2048]{1,0:T(8,128)S(1)}, f32[40,2048]{1,0:T(8,128)S(1)}, u32[]{:S(2)}, u32[]{:S(2)}) collective-permute-start(f32[40,2048]{1,0:T(8,128)S(1)} %collective-permute-done.9.refs_2_), channel_id=1, source_target_pairs={{0,1},{1,0},{2,3},{3,2},{4,5},{5,4},{6,7},{7,6},{8,9},{9,8},{10,11... | collective-permute-start | bytes 983048 | tf_op jit(solution)/shard_map/ppermute | solution.py:631
  49.5 13.0 %all-to-all-start = ((f32[256,1,128]{2,1,0:T(1,128)}), f32[256,1,128]{2,1,0:T(1,128)S(1)}, u32[]{:S(2)}, u32[]{:S(2)}) async-start(f32[256,1,128]{2,1,0:T(1,128)} %get-tuple-element.61), calls=%async_computation | async-start | bytes 262144 | tf_op jit(solution)/shard_map/all_to_all | solution.py:694
  62.5 3.5 %collective-permute-start.14 = (f32[1,32768]{1,0:T(1,128)S(1)}, f32[1,32768]{1,0:T(1,128)S(1)}, u32[]{:S(2)}, u32[]{:S(2)}) collective-permute-start(f32[1,32768]{1,0:T(1,128)S(1)} %get-tuple-element.54.later), channel_id=1, source_target_pairs={{1,2},{3,4},{5,6},{2,1},{4,3},{6,5},{9,10},{11,12},{13,14},{10,9},... | collective-permute-start | bytes 393224 | tf_op jit(solution)/shard_map/ppermute | solution.py:637
  66.1 3.5 %collective-permute-done.14.refs_10_ = f32[1,32768]{1,0:T(1,128)S(1)} collective-permute-done((f32[1,32768]{1,0:T(1,128)S(1)}, f32[1,32768]{1,0:T(1,128)S(1)}, u32[]{:S(2)}, u32[]{:S(2)}) %collective-permute-start.14) | collective-permute-done | bytes 131104 | tf_op jit(solution)/shard_map/ppermute | solution.py:637
  69.6 5.9 %all-to-all-done.refs_11_ = f32[256,1,128]{2,1,0:T(1,128)S(1)} async-done(((f32[256,1,128]{2,1,0:T(1,128)}), f32[256,1,128]{2,1,0:T(1,128)S(1)}, u32[]{:S(2)}, u32[]{:S(2)}) %all-to-all-start) | async-done | bytes 131104 | tf_op jit(solution)/shard_map/all_to_all | solution.py:694
  75.5 3.3 %gradient_kept.1 = (f32[16,32768]{1,0:T(8,128)}, f32[40,128]{1,0:T(8,128)S(1)}, f32[8,128]{1,0:T(8,128)S(1)}) custom-call(f32[40,2048]{1,0:T(8,128)S(1)} %get-tuple-element.55.refs_0_, f32[40,2048]{1,0:T(8,128)S(1)} %collective-permute-done.7.refs_1_, f32[40,2048]{1,0:T(8,128)S(1)} %collective-permute-done.9.refs_2_, ...), custom_call_target="tpu_custom_call" | custom-call | tf_op jit(solution)/shard_map/gradient_kept/pallas_call | solution.py:610
  79.4 3.1 %gradient_given.1 = f32[16,32768]{1,0:T(8,128)} custom-call(f32[40,2048]{1,0:T(8,128)S(1)} %collective-permute-done.6.refs_0_, f32[40,2048]{1,0:T(8,128)S(1)} %collective-permute-done.8.refs_1_, f32[40,2048]{1,0:T(8,128)S(1)} %collective-permute-done.10.refs_2_, f32[40,2048]{1,0:T(8,128)S(1)} %collective-permute-done.12.refs_3_, ...), custom_call_target="tpu_custom_call", output_to_operand_aliasing={{}: (12, {})} | custom-call | tf_op jit(solution)/shard_map/gradient_given/pallas_call | solution.py:610
  (23 shorter events, 2.9 us)
Async XLA Ops:
  4.0 5.9 %collective-permute-start = (f32[4,40,2048]{2,1,0:T(8,128)S(1)}, f32[4,40,2048]{2,1,0:T(8,128)S(1)}, u32[]{:S(2)}, u32[]{:S(2)}) collective-permute-start(f32[4,40,2048]{2,1,0:T(8,128)S(1)} %get-tuple-element.41), channel_id=1, source_target_pairs={{0,1},{1,0},{2,3},{3,2},{4,5},{5,4},{6,7},{7,6},{8,9},{9,8},{10,11... | collective-permute-start | bytes 3932168 | tf_op jit(solution)/shard_map/ppermute | solution.py:631
  10.0 7.9 %copy-start = (f32[4,20,16]{1,2,0:T(8,128)S(1)}, f32[4,20,16]{1,2,0:T(8,128)}, u32[]{:S(2)}) copy-start(f32[4,20,16]{1,2,0:T(8,128)} %param.10) | copy-start | bytes 15364
  10.0 7.9 %copy-start.1 = (f32[16]{0:T(128)S(1)}, f32[16]{0:T(128)}, u32[]{:S(2)}) copy-start(f32[16]{0:T(128)} %param.15) | copy-start | bytes 196
  10.0 7.9 %copy-start.2 = (f32[20]{0:T(128)S(1)}, f32[20]{0:T(128)}, u32[]{:S(2)}) copy-start(f32[20]{0:T(128)} %param.14) | copy-start | bytes 244
  10.2 16.8 %collective-permute-start.1 = (f32[40,2048]{1,0:T(8,128)S(1)}, f32[40,2048]{1,0:T(8,128)S(1)}, u32[]{:S(2)}, u32[]{:S(2)}) collective-permute-start(f32[40,2048]{1,0:T(8,128)S(1)} %get-tuple-element.45), channel_id=1, source_target_pairs={{0,2},{1,3},{2,4},{3,5},{4,6},{5,7},{6,0},{7,1},{8,10},{9,11},{10,... | collective-permute-start | bytes 983048 | tf_op jit(solution)/shard_map/ppermute | solution.py:642
  10.3 16.7 %collective-permute-start.2 = (f32[40,2048]{1,0:T(8,128)S(1)}, f32[40,2048]{1,0:T(8,128)S(1)}, u32[]{:S(2)}, u32[]{:S(2)}) collective-permute-start(f32[40,2048]{1,0:T(8,128)S(1)} %get-tuple-element.46), channel_id=1, source_target_pairs={{0,4},{1,5},{2,6},{3,7},{4,0},{5,1},{6,2},{7,3},{8,12},{9,13},{10,... | collective-permute-start | bytes 983048 | tf_op jit(solution)/shard_map/ppermute | solution.py:642
  12.2 15.5 %collective-permute-start.3 = (f32[40,2048]{1,0:T(8,128)S(1)}, f32[40,2048]{1,0:T(8,128)S(1)}, u32[]{:S(2)}, u32[]{:S(2)}) collective-permute-start(f32[40,2048]{1,0:T(8,128)S(1)} %get-tuple-element.47), channel_id=1, source_target_pairs={{0,6},{1,7},{2,0},{3,1},{4,2},{5,3},{6,4},{7,5},{8,14},{9,15},{10,... | collective-permute-start | bytes 983048 | tf_op jit(solution)/shard_map/ppermute | solution.py:642
  13.4 6.6 %collective-permute-start.4 = (f32[16,2048]{1,0:T(8,128)S(1)}, f32[16,2048]{1,0:T(8,128)S(1)}, u32[]{:S(2)}, u32[]{:S(2)}) collective-permute-start(f32[16,2048]{1,0:T(8,128)S(1)} %get-tuple-element.52), channel_id=1, source_target_pairs={{0,8},{8,16},{16,24},{24,32},{32,40},{40,48},{48,56},{56,64},{64,7... | collective-permute-start | bytes 393224 | tf_op jit(solution)/shard_map/ppermute | solution.py:648
  16.6 6.0 %collective-permute-start.5 = (f32[16,2048]{1,0:T(8,128)S(1)}, f32[16,2048]{1,0:T(8,128)S(1)}, u32[]{:S(2)}, u32[]{:S(2)}) collective-permute-start(f32[16,2048]{1,0:T(8,128)S(1)} %get-tuple-element.48.after), channel_id=1, source_target_pairs={{8,0},{16,8},{24,16},{32,24},{40,32},{48,40},{56,48},{64,56},{72,6... | collective-permute-start | bytes 393224 | tf_op jit(solution)/shard_map/ppermute | solution.py:648
  28.7 10.2 %collective-permute-start.11 = (f32[40,2048]{1,0:T(8,128)S(1)}, f32[40,2048]{1,0:T(8,128)S(1)}, u32[]{:S(2)}, u32[]{:S(2)}) collective-permute-start(f32[40,2048]{1,0:T(8,128)S(1)} %get-tuple-element.55.refs_0_), channel_id=1, source_target_pairs={{0,2},{1,3},{2,4},{3,5},{4,6},{5,7},{6,0},{7,1},{8,10},{9,11},{10,... | collective-permute-start | bytes 983048 | tf_op jit(solution)/shard_map/ppermute | solution.py:642
  30.2 17.5 %collective-permute-start.9 = (f32[40,2048]{1,0:T(8,128)S(1)}, f32[40,2048]{1,0:T(8,128)S(1)}, u32[]{:S(2)}, u32[]{:S(2)}) collective-permute-start(f32[40,2048]{1,0:T(8,128)S(1)} %get-tuple-element.55.refs_0_), channel_id=1, source_target_pairs={{0,4},{1,5},{2,6},{3,7},{4,0},{5,1},{6,2},{7,3},{8,12},{9,13},{10,... | collective-permute-start | bytes 983048 | tf_op jit(solution)/shard_map/ppermute | solution.py:642
  33.3 15.7 %collective-permute-start.7 = (f32[40,2048]{1,0:T(8,128)S(1)}, f32[40,2048]{1,0:T(8,128)S(1)}, u32[]{:S(2)}, u32[]{:S(2)}) collective-permute-start(f32[40,2048]{1,0:T(8,128)S(1)} %get-tuple-element.55.refs_0_), channel_id=1, source_target_pairs={{0,6},{1,7},{2,0},{3,1},{4,2},{5,3},{6,4},{7,5},{8,14},{9,15},{10,... | collective-permute-start | bytes 983048 | tf_op jit(solution)/shard_map/ppermute | solution.py:642
  33.3 46.0 %collective-permute-start.6 = (f32[40,2048]{1,0:T(8,128)S(1)}, f32[40,2048]{1,0:T(8,128)S(1)}, u32[]{:S(2)}, u32[]{:S(2)}) collective-permute-start(f32[40,2048]{1,0:T(8,128)S(1)} %get-tuple-element.55.refs_0_), channel_id=1, source_target_pairs={{0,1},{1,0},{2,3},{3,2},{4,5},{5,4},{6,7},{7,6},{8,9},{9,8},{10,11... | collective-permute-start | bytes 983048 | tf_op jit(solution)/shard_map/ppermute | solution.py:631
  39.0 40.4 %collective-permute-start.12 = (f32[40,2048]{1,0:T(8,128)S(1)}, f32[40,2048]{1,0:T(8,128)S(1)}, u32[]{:S(2)}, u32[]{:S(2)}) collective-permute-start(f32[40,2048]{1,0:T(8,128)S(1)} %collective-permute-done.11.refs_3_), channel_id=1, source_target_pairs={{0,1},{1,0},{2,3},{3,2},{4,5},{5,4},{6,7},{7,6},{8,9},{9,8},{10,11... | collective-permute-start | bytes 983048 | tf_op jit(solution)/shard_map/ppermute | solution.py:631
  47.6 31.7 %collective-permute-start.10 = (f32[40,2048]{1,0:T(8,128)S(1)}, f32[40,2048]{1,0:T(8,128)S(1)}, u32[]{:S(2)}, u32[]{:S(2)}) collective-permute-start(f32[40,2048]{1,0:T(8,128)S(1)} %collective-permute-done.9.refs_2_), channel_id=1, source_target_pairs={{0,1},{1,0},{2,3},{3,2},{4,5},{5,4},{6,7},{7,6},{8,9},{9,8},{10,11... | collective-permute-start | bytes 983048 | tf_op jit(solution)/shard_map/ppermute | solution.py:631
  49.0 30.4 %collective-permute-start.8 = (f32[40,2048]{1,0:T(8,128)S(1)}, f32[40,2048]{1,0:T(8,128)S(1)}, u32[]{:S(2)}, u32[]{:S(2)}) collective-permute-start(f32[40,2048]{1,0:T(8,128)S(1)} %collective-permute-done.7.refs_1_), channel_id=1, source_target_pairs={{0,1},{1,0},{2,3},{3,2},{4,5},{5,4},{6,7},{7,6},{8,9},{9,8},{10,11... | collective-permute-start | bytes 983048 | tf_op jit(solution)/shard_map/ppermute | solution.py:631
  49.0 13.5 %collective-permute-start.13 = (f32[1,32768]{1,0:T(1,128)}, f32[1,32768]{1,0:T(1,128)S(1)}, u32[]{:S(2)}, u32[]{:S(2)}) collective-permute-start(f32[1,32768]{1,0:T(1,128)} %get-tuple-element.59), channel_id=1, source_target_pairs={{0,1},{1,0},{2,3},{3,2},{4,5},{5,4},{6,7},{7,6},{8,9},{9,8},{10,11... | collective-permute-start | bytes 393224 | tf_op jit(solution)/shard_map/ppermute | solution.py:631
  49.5 26.0 %all-to-all-start = ((f32[256,1,128]{2,1,0:T(1,128)}), f32[256,1,128]{2,1,0:T(1,128)S(1)}, u32[]{:S(2)}, u32[]{:S(2)}) async-start(f32[256,1,128]{2,1,0:T(1,128)} %get-tuple-element.61), calls=%async_computation | async-start | bytes 262144 | tf_op jit(solution)/shard_map/all_to_all | solution.py:694
  62.5 7.0 %collective-permute-start.14 = (f32[1,32768]{1,0:T(1,128)S(1)}, f32[1,32768]{1,0:T(1,128)S(1)}, u32[]{:S(2)}, u32[]{:S(2)}) collective-permute-start(f32[1,32768]{1,0:T(1,128)S(1)} %get-tuple-element.54.later), channel_id=1, source_target_pairs={{1,2},{3,4},{5,6},{2,1},{4,3},{6,5},{9,10},{11,12},{13,14},{10,9},... | collective-permute-start | bytes 393224 | tf_op jit(solution)/shard_map/ppermute | solution.py:637

commit v2 on v1

--- a/solution.py
+++ b/solution.py
@@ -78,10 +78,9 @@
 
 
 def project_piece(
-    d, base, field, momentum, depth, mask, weights, proj, density, position, weighted, classes, bins
+    d, base, field, momentum, depth, weights, proj, density, position, classes, bins
 ):
     sub = field.shape[2] // 2
-    total = jnp.zeros(weighted.shape, jnp.float32)
     for start in range(0, sub, WIDE):
         halves = []
         for begin in (start, start + sub):
@@ -102,10 +101,6 @@
         for k in range(1, classes):
             picked = jnp.where(chosen == k, every[2 * bins * k : 2 * bins * (k + 1)], picked)
         proj[d, :, start : start + WIDE] = picked
-        scaled = picked * packed_row(mask, base + start, sub, bins)
-        for lane in range(0, WIDE, 128):
-            total = total + scaled[:, lane : lane + 128]
-    weighted[...] += total
 
 
 def project_given_body(
@@ -117,7 +112,6 @@
     proj,
     density,
     position,
-    weighted,
     field_kept,
     momentum_kept,
     depth_here,
@@ -156,7 +150,6 @@
         copy.start()
     load_table.wait()
     weights[...] = forward_weights(table[...], classes, bins, shells)
-    weighted[...] = jnp.zeros_like(weighted)
     copies[0].wait()
     copies[1].wait()
     for d in range(4):
@@ -168,12 +161,10 @@
             field_given,
             momentum_given,
             depth_here,
-            mask_here,
             weights,
             proj,
             stage,
             position,
-            weighted,
             classes,
             bins,
         )
@@ -211,7 +202,6 @@
         vmem(4, 2 * bins, width // 2),
         pltpu.HBM((4, shells, width), jnp.float32),
         vmem(4, shells, width),
-        vmem(2 * bins, 128),
         vmem(4, shells, width),
         vmem(4, shells, width),
         vmem(1, pixels, dtype=jnp.int32),
@@ -236,24 +226,10 @@
 
 
 def project_kept_body(
-    field,
-    momentum,
-    depth,
-    mask,
-    weights,
-    before,
-    proj,
-    density,
-    position,
-    weighted,
-    stage,
-    marks,
-    classes,
-    bins,
+    field, momentum, depth, weights, proj, density, position, stage, marks, classes, bins
 ):
     width = field.shape[2]
     chip, core = position_of()
-    weighted[...] = before[...]
     copies = []
     for d in range(4):
         project_piece(
@@ -262,12 +238,10 @@
             field,
             momentum,
             depth,
-            mask,
             weights,
             proj,
             stage,
             position,
-            weighted,
             classes,
             bins,
         )
@@ -277,23 +251,22 @@
         copy.wait()
 
 
-def project_kept(field, momentum, depth, mask, weights, before, classes, bins):
+def project_kept(field, momentum, depth, weights, classes, bins):
     _, shells, width = field.shape
     outs = [
         vmem(4, 2 * bins, width // 2),
         pltpu.HBM((4, shells, width), jnp.float32),
         vmem(4, shells, width),
-        vmem(2 * bins, 128),
     ]
     return pl.pallas_call(
         functools.partial(project_kept_body, classes=classes, bins=bins),
-        in_specs=[HERE] * 6,
-        out_specs=[HERE, AWAY, HERE, HERE],
+        in_specs=[HERE] * 4,
+        out_specs=[HERE, AWAY, HERE],
         out_shape=outs,
         scratch_shapes=[vmem(4, shells, width), pltpu.SemaphoreType.DMA((4,))],
         compiler_params=LIMIT,
         name="project_kept",
-    )(*in_vmem(field, momentum, depth, mask, weights, before))
+    )(*in_vmem(field, momentum, depth, weights))
 
 
 def combine_body(kept, partner, given_place, kept_place, own, first, second, third, head, tail):
@@ -335,66 +308,78 @@
     return exact_rows(wide, at.astype(jnp.bfloat16))[:, :1]
 
 
-def tally_body(
-    counts, after, table, scale, mean, totals, own, weights, square, means, here, marks, deep
+def prepare_body(
+    counts,
+    given,
+    kept,
+    after,
+    table,
+    scale,
+    mean,
+    own,
+    weights,
+    square,
+    means,
+    kernels,
+    to_partner,
+    to_side,
+    here,
+    mark,
+    deep,
 ):
-    bins, pixels = here.shape
+    bins, part = here.shape
     shells = square.shape[0]
     chip, core = position_of()
-    part = pixels // 8
-    copies = []
-    for i in range(8):
-        piece = pl.ds(i * part, part)
-        copies.append(
-            pltpu.make_async_copy(counts.at[:, piece], here.at[:, piece], marks.at[i])
-        )
-        copies[-1].start()
+    base = offset_of(core, 0, chip, part)
+    copy = pltpu.make_async_copy(counts.at[:, pl.ds(base, part)], here, mark)
+    copy.start()
     weights[...] = backward_weights(table[...], table.shape[0] // shells, bins, shells, deep)
     size = column(scale[...], shells)
     square[...] = jnp.broadcast_to(1.0 / (size * size), square.shape)
-    means[...] = jnp.broadcast_to(column(mean[...], 2 * bins), means.shape)
-    totals[...] = jnp.zeros_like(totals)
-    for i in range(8):
-        copies[i].wait()
-
-        def step(j, carry):
-            begin = pl.multiple_of(i * part + j * 512, 512)
-            some = here[:, pl.ds(begin, 512)]
-            return carry + (some[:, :128] + some[:, 128:256]) + (some[:, 256:384] + some[:, 384:])
-
-        total = lax.fori_loop(0, part // 512, step, jnp.zeros((bins, 128), jnp.int32), unroll=2)
-        totals[...] += total.astype(jnp.float32)
-    base = offset_of(core, 0, chip, part)
+    means[...] = mean[...]
+    kernels[...] = table[...]
+    for d in range(4):
+        for source, half in ((given, 1 - core), (kept, core)):
+            begin = offset_of(half, d, chip, part)
+            for start in range(0, part, 1024):
+                first = source[d, :1, start : start + 1024]
+                last = source[d, shells - 1 :, start : start + 1024]
+                there = pl.ds(begin + start, 1024)
+                to_partner[:, there] = jnp.where(core == 0, last, first)
+                to_side[:, there] = jnp.where(core == 0, first, last)
+    copy.wait()
     sub = part // 2
     for start in range(0, sub, 512):
         there = slice(start, start + 512)
-        own[:bins, there] = here[:, pl.ds(base + start, 512)].astype(jnp.float32)
-        own[bins:, there] = here[:, pl.ds(base + sub + start, 512)].astype(jnp.float32)
-
-
-def tally(counts, after, table, scale, mean):
+        own[:bins, there] = here[:, there].astype(jnp.float32)
+        own[bins:, there] = here[:, start + sub : start + sub + 512].astype(jnp.float32)
+
+
+def prepare(counts, given, kept, after, table, scale, mean):
     bins, pixels = counts.shape
     shells = scale.shape[1]
     deep = -(-2 * bins // 16) * 16
     return pl.pallas_call(
-        functools.partial(tally_body, deep=deep),
-        in_specs=[AWAY, HERE, pl.BlockSpec(), pl.BlockSpec(), pl.BlockSpec()],
-        out_specs=[HERE] * 5,
+        functools.partial(prepare_body, deep=deep),
+        in_specs=[AWAY, HERE, HERE, HERE, pl.BlockSpec(), pl.BlockSpec(), pl.BlockSpec()],
+        out_specs=[HERE] * 7,
         out_shape=[
-            vmem(bins, 128),
             vmem(2 * bins, pixels // 16),
             vmem(2 * table.shape[0], 3 * deep, dtype=jnp.bfloat16),
             vmem(shells, 128),
-            vmem(2 * bins, 128),
+            vmem(1, bins),
+            vmem(*table.shape),
+            vmem(1, pixels),
+            vmem(1, pixels),
         ],
-        scratch_shapes=[vmem(bins, pixels, dtype=jnp.int32), pltpu.SemaphoreType.DMA((8,))],
+        scratch_shapes=[vmem(bins, pixels // 8, dtype=jnp.int32), pltpu.SemaphoreType.DMA],
         compiler_params=LIMIT,
-        name="tally",
-    )(*in_hbm(counts), *in_vmem(after), table, scale, mean)
+        name="prepare",
+    )(*in_hbm(counts), *in_vmem(given, kept, after), table, scale, mean)
 
 
 def stencil_body(
-    given, kept, before, after, scale, away, to_partner, to_side, position, out, marks
+    given, kept, before, after, scale, away, position, out, marks
 ):
     _, shells, width = given.shape
     pixels = 8 * width
@@ -407,10 +392,6 @@
             for start in range(0, width, 1024):
                 values = source[d, :, start : start + 1024]
                 position[:, pl.ds(CYCLE + base + start, 1024)] = values
-                first, last = values[:1], values[shells - 1 :]
-                here = pl.ds(base + start, 1024)
-                to_partner[:, here] = jnp.where(core == 0, last, first)
-                to_side[:, here] = jnp.where(core == 0, first, last)
     inverse = jnp.concatenate([scale[...]] * 4, axis=1)
     row = iota((shells, 512), 0)
 
@@ -446,10 +427,8 @@
     return pl.pallas_call(
         stencil_body,
         in_specs=[HERE] * 5,
-        out_specs=[AWAY, HERE, HERE],
-        out_shape=[
-            pltpu.HBM((shells, pixels), jnp.float32), vmem(1, pixels), vmem(1, pixels)
-        ],
+        out_specs=AWAY,
+        out_shape=pltpu.HBM((shells, pixels), jnp.float32),
         scratch_shapes=[
             vmem(shells, pixels + 2 * CYCLE),
             vmem(shells, pixels),
@@ -469,66 +448,148 @@
     return total
 
 
-def ratio_body(
-    own, first, second, third, counts, mask, weighted, totals, later, out, stats
-):
+def ratio_body(own, first, second, third, counts, mask, later, out, stats):
     rows, sub = out.shape
     bins = rows // 2
     chip, core = position_of()
     base = offset_of(core, 0, chip, 2 * sub)
-    logs = jnp.zeros((rows, 128), jnp.float32)
+    weighted = logs = totals = jnp.zeros((rows, 128), jnp.float32)
     for start in range(0, sub, WIDE):
         here = slice(start, start + WIDE)
         proj = own[:, here] + first[:, here] + second[:, here] + third[:, here]
         some = counts[:, here]
         out[:, here] = some / proj
-        term = some * jnp.log(proj * packed_row(mask, base + start, sub, bins))
+        covered = proj * packed_row(mask, base + start, sub, bins)
+        term = some * jnp.log(covered)
         for lane in range(0, WIDE, 128):
+            weighted = weighted + covered[:, lane : lane + 128]
             logs = logs + term[:, lane : lane + 128]
-    mine = jnp.where((chip == 0) & (core == 0), totals[...], 0.0)
-    gap = jnp.zeros((128 - 2 * rows - bins, 128), jnp.float32)
-    sums = jnp.concatenate(
-        [weighted[...], logs, mine, gap], axis=0
-    )
+            totals = totals + some[:, lane : lane + 128]
+    filler = jnp.zeros((128 - 3 * rows, 128), jnp.float32)
+    sums = jnp.concatenate([weighted, logs, totals, filler], axis=0)
     row = exact_rows(sums, jnp.ones((8, 128), jnp.bfloat16))[:1]
     stats[...] = jnp.broadcast_to(row[:, None], stats.shape)
 
 
-def ratio(own, first, second, third, counts, mask, weighted, totals, later, devices):
+def ratio(own, first, second, third, counts, mask, later):
     return pl.pallas_call(
         ratio_body,
-        in_specs=[HERE] * 9,
+        in_specs=[HERE] * 6 + [AWAY],
         out_specs=[HERE, HERE],
-        out_shape=[vmem(*own.shape), vmem(devices, 1, 128)],
+        out_shape=[
+            vmem(*own.shape),
+            vmem(lax.axis_size("pix") * lax.axis_size("shell"), 1, 128),
+        ],
         compiler_params=LIMIT,
         name="ratio",
-    )(*in_vmem(own, first, second, third, counts, mask, weighted, totals, later))
-
-
-def reduce_body(gathered, mean, level, loglik, bins, total_pix):
-    row = jnp.sum(gathered[...], axis=0)
-    row = jnp.broadcast_to(row, (8, 128))
-    at, lane = iota((2 * bins, 128), 0) % bins, iota((2 * bins, 128), 1)
-    pick = jnp.where((lane < 2 * bins) & (lane % bins == at), 1.0, 0.0)
-    weighted = exact_rows(row, pick.astype(jnp.bfloat16))[:, :1]
-    pick = jnp.where(lane - 4 * bins == at, 1.0, 0.0)
-    total = exact_rows(row, pick.astype(jnp.bfloat16))[:, :1]
+    )(*in_vmem(own, first, second, third, counts, mask), *in_hbm(later))
+
+
+def lanes_of(row, low, high, bins):
+    at, lane = iota((bins, 128), 0), iota((bins, 128), 1)
+    pick = (lane >= low) & (lane < high) & (lane % bins == at)
+    pick = jnp.where(pick, 1.0, 0.0).astype(jnp.bfloat16)
+    total = 0.0
+    for _ in range(3):
+        part = row.astype(jnp.bfloat16)
+        row = row - part.astype(jnp.float32)
+        total = total + dot_nt(part, pick)
+    return total
+
+
+def finish_body(
+    gathered,
+    mean,
+    table,
+    depth,
+    mask,
+    kept,
+    given,
+    density_kept,
+    density_given,
+    out,
+    loglik,
+    density,
+    stage,
+    marks,
+    classes,
+    bins,
+    total_pix,
+):
+    _, shells, width = kept.shape
+    chip, core = position_of()
+    pieces, copies = [], []
+    for d in range(4):
+        for k, (side, away, half) in enumerate(
+            ((kept, density_kept, core), (given, density_given, 1 - core))
+        ):
+            pieces.append((side, d, offset_of(half, d, chip, width)))
+            slot = 2 * d + k
+            copies.append(pltpu.make_async_copy(away.at[d], density.at[slot], marks.at[slot]))
+            copies[-1].start()
+    row = jnp.broadcast_to(jnp.sum(gathered[...], axis=0), (8, 128))
+    weighted = lanes_of(row, 0, 2 * bins, bins)[:1]
+    total = lanes_of(row, 4 * bins, 6 * bins, bins)[:1]
     norm = weighted / total_pix
-    level[...] = jnp.broadcast_to(total / (total_pix * norm), level.shape)
-    average = mean[:, :1]
+    level = total / (total_pix * norm)
+    average = mean[...]
     terms = total * jnp.log(average / norm) - average * (weighted / norm)
-    terms = jnp.where(iota(terms.shape, 0) < bins, terms, 0.0)
-    lane = iota((8, 128), 1)
-    logs = jnp.where((lane >= 2 * bins) & (lane < 4 * bins), row, 0.0)[:1]
-    value = jnp.sum(terms, axis=0, keepdims=True) + jnp.sum(logs, axis=1, keepdims=True)
-    loglik[...] = jnp.broadcast_to(value / (bins * total_pix), loglik.shape)
-
-
-def gradient_body(*refs, classes, bins, total_pix, mine):
+    lane = iota((1, 128), 1)
+    logs = jnp.where((lane >= 2 * bins) & (lane < 4 * bins), row[:1], 0.0)
+    value = jnp.sum(terms, axis=1, keepdims=True) + jnp.sum(logs, axis=1, keepdims=True)
+    loglik[...] = value / (bins * total_pix)
+    drop = jnp.sum(table[...] * level, axis=1, keepdims=True)
+    drop = jnp.broadcast_to(drop, (drop.shape[0], WIDE))
+    for slot, (side, d, base) in enumerate(pieces):
+        copies[slot].wait()
+        for start in range(0, width, WIDE):
+            here, away = slice(start, start + WIDE), pl.ds(base + start, WIDE)
+            chosen = depth[:, away]
+            less = drop[:shells]
+            for c in range(1, classes):
+                less = jnp.where(chosen == c, drop[c * shells : (c + 1) * shells], less)
+            less = density[slot, :, here] * (mask[:, away] * less)
+            stage[slot, :, here] = side[d, :, here] - less
+        copies.append(
+            pltpu.make_async_copy(
+                stage.at[slot], out.at[:, pl.ds(base, width)], marks.at[8 + slot]
+            )
+        )
+        copies[-1].start()
+    for copy in copies[8:]:
+        copy.wait()
+
+
+def finish(
+    gathered, mean, table, depth, mask, kept, given, density_kept, density_given, total_pix
+):
+    _, shells, width = kept.shape
+    pixels, bins = 8 * width, table.shape[1]
+    classes = table.shape[0] // shells
+    operands = in_vmem(gathered, mean, table, depth, mask, kept, given)
+    return pl.pallas_call(
+        functools.partial(finish_body, classes=classes, bins=bins, total_pix=total_pix),
+        in_specs=[HERE] * 7 + [AWAY] * 2,
+        out_specs=[AWAY, pl.BlockSpec()],
+        out_shape=[
+            jax.ShapeDtypeStruct((shells, pixels), jnp.float32),
+            jax.ShapeDtypeStruct((1, 1), jnp.float32),
+        ],
+        scratch_shapes=[
+            vmem(8, shells, width),
+            vmem(8, shells, width),
+            pltpu.SemaphoreType.DMA((16,)),
+        ],
+        compiler_params=LIMIT,
+        name="finish",
+    )(*operands, *in_hbm(density_kept, density_given))
+
+
+def gradient_body(*refs, classes, bins, mine):
     quotients, refs = refs[:4], refs[4:]
-    density_away, rest_away, depth, mask, weights, partner, side = refs[:7]
-    density, rest, stage, marks = refs[-4:]
-    _, shells, width = stage.shape
+    density_away, rest_away, depth, weights, partner, side = refs[:6]
+    out, density, rest, marks = refs[6:]
+    _, shells, width = out.shape
     sub = width // 2
     chip, core = position_of()
     half = core if mine else 1 - core
@@ -537,33 +598,25 @@
         base = offset_of(half, d, chip, width)
         loads.append(
             (
-                pltpu.make_async_copy(density_away.at[d], density.at[d], marks.at[4 + d]),
+                pltpu.make_async_copy(density_away.at[d], density.at[d], marks.at[d]),
                 pltpu.make_async_copy(
-                    rest_away.at[:, pl.ds(base, width)], rest.at[d], marks.at[8 + d]
+                    rest_away.at[:, pl.ds(base, width)], rest.at[d], marks.at[4 + d]
                 ),
             )
         )
         for load in loads[-1]:
             load.start()
-    if mine:
-        gathered, mean, out, level, loglik = refs[7:12]
-        reduce_body(gathered, mean, level, loglik, bins, total_pix)
-    else:
-        level, _, out = refs[7:10]
     row = iota((shells, WIDE), 0)
     beside_partner = (row == 0) & (core == 1) | (row == shells - 1) & (core == 0)
     outside = (row == 0) & (core == 0) | (row == shells - 1) & (core == 1)
-    share = jnp.concatenate([level[...]] * (WIDE // 128), axis=1)
     filler = jnp.zeros((weights.shape[1] // 3 - 2 * bins, WIDE), jnp.float32)
-    copies = []
     for d in range(4):
         base = offset_of(half, d, chip, width)
         for load in loads[d]:
             load.wait()
         for start in range(0, sub, WIDE):
-            difference = quotients[d][:, start : start + WIDE]
-            difference = difference - share * packed_row(mask, base + start, sub, bins)
-            high, low = split(jnp.concatenate([difference, filler], axis=0))
+            values = quotients[d][:, start : start + WIDE]
+            high, low = split(jnp.concatenate([values, filler], axis=0))
             every = jnp.dot(
                 weights[...],
                 jnp.concatenate([high, low, high], axis=0),
@@ -580,47 +633,24 @@
                     back = jnp.where(chosen == c, every[begin : begin + shells], back)
                 near = jnp.where(beside_partner, partner[:, away], 0.0)
                 near = jnp.where(outside, side[:, away], near)
-                stage[d, :, here] = density[d, :, here] * back + (rest[d, :, here] + RADIAL * near)
-        copies.append(
-            pltpu.make_async_copy(stage.at[d], out.at[:, pl.ds(base, width)], marks.at[d])
-        )
-        copies[-1].start()
-    for copy in copies:
-        copy.wait()
-
-
-def gradient(
-    quotients, density, rest, depth, mask, weights, partner, side, extra, previous,
-    classes, bins, total_pix,
-):
+                out[d, :, here] = density[d, :, here] * back + (rest[d, :, here] + RADIAL * near)
+
+
+def gradient(quotients, density, rest, depth, weights, partner, side, classes, bins, mine):
     shells, pixels = rest.shape
     width = pixels // 8
-    mine = previous is None
     operands = in_vmem(*quotients) + in_hbm(density, rest)
-    operands += in_vmem(depth, mask, weights, partner, side, *extra)
-    specs = [HERE] * 4 + [AWAY] * 2 + [HERE] * (len(operands) - 6)
-    outs, out_specs, aliases = [jax.ShapeDtypeStruct((shells, pixels), jnp.float32)], [AWAY], {}
-    if mine:
-        outs += [vmem(2 * bins, 128), jax.ShapeDtypeStruct((8, 128), jnp.float32)]
-        out_specs += [HERE, pl.BlockSpec()]
-    else:
-        aliases = {len(operands): 0}
-        operands.append(previous)
-        specs.append(AWAY)
+    operands += in_vmem(depth, weights, partner, side)
     return pl.pallas_call(
-        functools.partial(
-            gradient_body, classes=classes, bins=bins, total_pix=total_pix, mine=mine
-        ),
-        in_specs=specs,
-        out_specs=out_specs,
-        out_shape=outs,
+        functools.partial(gradient_body, classes=classes, bins=bins, mine=mine),
+        in_specs=[HERE] * 4 + [AWAY] * 2 + [HERE] * 4,
+        out_specs=HERE,
+        out_shape=vmem(4, shells, width),
         scratch_shapes=[
             vmem(4, shells, width),
             vmem(4, shells, width),
-            vmem(4, shells, width),
-            pltpu.SemaphoreType.DMA((12,)),
+            pltpu.SemaphoreType.DMA((8,)),
         ],
-        input_output_aliases=aliases,
         compiler_params=LIMIT,
         name="gradient_kept" if mine else "gradient_given",
     )(*operands)
@@ -651,7 +681,6 @@
 def shards(field, momentum, kernels, depth_class, counts, mask, mean_counts, shell_scale):
     shells, pixels = field.shape
     classes, bins, _ = kernels.shape
-    devices = lax.axis_size("pix") * lax.axis_size("shell")
     total_pix = pixels * lax.axis_size("pix")
     table = jnp.transpose(kernels, (0, 2, 1)).reshape(classes * shells, bins)
 
@@ -664,46 +693,47 @@
         classes,
         bins,
     )
-    proj, density_given, place_given, weighted, field_kept, momentum_kept = given[:6]
-    depth, cover, weights = given[6:]
+    proj, density_given, place_given, field_kept, momentum_kept, depth, cover, weights = given
     proj_partner = swap(proj)
-    proj_kept, density_kept, place_kept, weighted = project_kept(
-        field_kept, momentum_kept, depth, cover, weights, weighted, classes, bins
+    proj_kept, density_kept, place_kept = project_kept(
+        field_kept, momentum_kept, depth, weights, classes, bins
     )
     own, first, second, third, head, tail = combine(
         proj_kept, proj_partner, place_given, place_kept
     )
-    second = along(second, 2)
     first = along(first, 1)
     third = along(third, 3)
+    second = along(second, 2)
     after = halo(head, "pix", -1)
     before = halo(tail, "pix", 1)
-    totals, own_counts, weights, square, mean = tally(
-        counts, head, table, shell_scale.reshape(1, shells), mean_counts.reshape(1, bins)
+    own_counts, weights, square, mean, table, to_partner, to_side = prepare(
+        counts,
+        place_given,
+        place_kept,
+        head,
+        table,
+        shell_scale.reshape(1, shells),
+        mean_counts.reshape(1, bins),
     )
-    rest, to_partner, to_side = stencil(place_given, place_kept, before, after, square)
     partner_row = swap(to_partner)
     side_row = beside(to_side)
-    quotient, stats = ratio(
-        own, first, second, third, own_counts, cover, weighted, totals, to_side, devices
-    )
-
-    from_far = along(quotient, 2)
+    rest = stencil(place_given, place_kept, before, after, square)
+    quotient, stats = ratio(own, first, second, third, own_counts, cover, rest)
     from_back = along(quotient, 1)
     from_front = along(quotient, 3)
+    from_far = along(quotient, 2)
     gathered = lax.all_to_all(stats, ("pix", "shell"), 0, 0)
     mine = [quotient, from_front, from_far, from_back]
     theirs = [swap(q) for q in mine[1:]]
     theirs = [swap(quotient), *theirs]
 
-    common = (rest, depth, cover, weights, partner_row, side_row)
-    out, level, loglik = gradient(
-        mine, density_kept, *common, (gathered, mean), None, classes, bins, total_pix
+    common = (rest, depth, weights, partner_row, side_row, classes, bins)
+    kept = gradient(mine, density_kept, *common, True)
+    given = gradient(theirs, density_given, *common, False)
+    out, loglik = finish(
+        gathered, mean, table, depth, cover, kept, given, density_kept, density_given, total_pix
     )
-    (out,) = gradient(
-        theirs, density_given, *common, (level,), out, classes, bins, total_pix
-    )
-    return out, loglik[0, 0]
+    return out, loglik.reshape(())
 
 
 def solution(mesh):

time: 82.9 us -> 78.3 us (0.945)
  waiting for transfers between devices: 25.1 us -> 21.2 us
  starting transfers between devices: 36.8 us -> 35.8 us
    all_to_all x1, waiting for transfers between devices: 5.93 us -> 0.14 us  [shards(): gathered = lax.all_to_all(stats, ('pix', 'shell'), 0, 0)]
    pallas_call x3 -> x4, Pallas kernels: 7.47 us -> 8.96 us  [the longest x1 3.51 us: stencil(): pl.pallas_call(stencil_body, in_specs=[HERE] * 5, out_specs=AWAY, out_sha...]
    ppermute x6, waiting for transfers between devices: 12.2 us -> 13.2 us  [along(): lax.ppermute(values, 'shell', [(i, (i + 2 * step) % count) for i in range...]
    all_to_all x1, starting transfers between devices: 13 us -> 12.1 us  [shards(): gathered = lax.all_to_all(stats, ('pix', 'shell'), 0, 0)]
    ppermute x2, waiting for transfers between devices: 2.6 us -> 3.44 us  [halo(): return lax.ppermute(values, axis, pairs)]
  transfers between devices with their start and end apart: 16 -> 16, of which waited for: 7 -> 8; matrix products, arithmetic and copies ran while one was open for 1% -> 0% of each run, Pallas kernels for 14% -> 16%
where the time goes in v2:
time: 78.3 us; the launch traced here: 78 us
  starting transfers between devices  35.8 us (46%)
  waiting for transfers between devices  21.2 us (27%)
  Pallas kernels  20 us (26%)
  between operations  0.97 us (1%)
    ppermute x6, waiting for transfers between devices, along(): lax.ppermute(values, 'shell', [(i, (i + 2 * step) % count) for i in range...  13.2 us
    all_to_all x1, starting transfers between devices, shards(): gathered = lax.all_to_all(stats, ('pix', 'shell'), 0, 0)  12.1 us
    ppermute x6, starting transfers between devices, swap(): return lax.ppermute(values, 'shell', [(i, i ^ 1) for i in range(count)])  7.88 us
    ppermute x6, starting transfers between devices, along(): lax.ppermute(values, 'shell', [(i, (i + 2 * step) % count) for i in range...  7.73 us
    pallas_call x2, Pallas kernels, gradient(): pl.pallas_call(functools.partial(gradient_body, classes=classes, bins=bin...  5.74 us
    ppermute x2, starting transfers between devices, halo(): return lax.ppermute(values, axis, pairs)  4.49 us
    ppermute x1, starting transfers between devices, beside(): return lax.ppermute(values, 'shell', pairs + [(b, a) for a, b in pairs])  3.54 us
    pallas_call x1, Pallas kernels, stencil(): pl.pallas_call(stencil_body, in_specs=[HERE] * 5, out_specs=AWAY, out_sha...  3.51 us
  transfers between devices with their start and end apart: 16, of which 8 were waited for; matrix products, arithmetic and copies ran while one was open for 0% of the time, Pallas kernels for 16%

profile of v2, /device:TPU:1, one launch (start us, length us, event | category | flops | bytes accessed | tf_op | source)
XLA Modules:
  0.0 78.0 jit_solution(13468627924689512227)
XLA Ops:
  0.6 3.4 %project_given.1 = (f32[4,40,2048]{2,1,0:T(8,128)S(1)}, f32[4,16,4096]{2,1,0:T(8,128)}, f32[4,16,4096]{2,1,0:T(8,128)S(1)}, f32[4,16,4096]{2,1,0:T(8,128)S(1)}, ...) custom-call(f32[16,32768]{1,0:T(8,128)} %field.1, ...), custom_call_target="tpu_custom_call" | custom-call | tf_op jit(solution)/shard_map/project_given/pallas_call | solution.py:211
  4.0 3.3 %collective-permute-start = (f32[4,40,2048]{2,1,0:T(8,128)S(1)}, f32[4,40,2048]{2,1,0:T(8,128)S(1)}, u32[]{:S(2)}, u32[]{:S(2)}) collective-permute-start(f32[4,40,2048]{2,1,0:T(8,128)S(1)} %get-tuple-element.35), channel_id=1, source_target_pairs={{0,1},{1,0},{2,3},{3,2},{4,5},{5,4},{6,7},{7,6},{8,9},{9,8},{10,11... | collective-permute-start | bytes 3932168 | tf_op jit(solution)/shard_map/ppermute | solution.py:661
  7.3 1.8 %project_kept.1 = (f32[4,40,2048]{2,1,0:T(8,128)S(1)}, f32[4,16,4096]{2,1,0:T(8,128)}, f32[4,16,4096]{2,1,0:T(8,128)S(1)}) custom-call(f32[4,16,4096]{2,1,0:T(8,128)S(1)} %get-tuple-element.30.field, f32[4,16,4096]{2,1,0:T(8,128)S(1)} %get-tuple-element.31.momentum, s32[1,32768]{1,0:T(1,128)S(1)} %get-tuple-element.32.depth.refs_6_, ...), custom_call_target="tpu_custom_call" | custom-call | tf_op jit(solution)/shard_map/project_kept/pallas_call | solution.py:261
  10.2 1.9 %collective-permute-start.2 = (f32[40,2048]{1,0:T(8,128)S(1)}, f32[40,2048]{1,0:T(8,128)S(1)}, u32[]{:S(2)}, u32[]{:S(2)}) collective-permute-start(f32[40,2048]{1,0:T(8,128)S(1)} %get-tuple-element.40), channel_id=1, source_target_pairs={{0,4},{1,5},{2,6},{3,7},{4,0},{5,1},{6,2},{7,3},{8,12},{9,13},{10,... | collective-permute-start | bytes 983048 | tf_op jit(solution)/shard_map/ppermute | solution.py:672
  12.2 1.2 %collective-permute-start.3 = (f32[40,2048]{1,0:T(8,128)S(1)}, f32[40,2048]{1,0:T(8,128)S(1)}, u32[]{:S(2)}, u32[]{:S(2)}) collective-permute-start(f32[40,2048]{1,0:T(8,128)S(1)} %get-tuple-element.41), channel_id=1, source_target_pairs={{0,6},{1,7},{2,0},{3,1},{4,2},{5,3},{6,4},{7,5},{8,14},{9,15},{10,... | collective-permute-start | bytes 983048 | tf_op jit(solution)/shard_map/ppermute | solution.py:672
  13.3 3.2 %collective-permute-start.4 = (f32[16,2048]{1,0:T(8,128)S(1)}, f32[16,2048]{1,0:T(8,128)S(1)}, u32[]{:S(2)}, u32[]{:S(2)}) collective-permute-start(f32[16,2048]{1,0:T(8,128)S(1)} %get-tuple-element.45), channel_id=1, source_target_pairs={{0,8},{8,16},{16,24},{24,32},{32,40},{40,48},{48,56},{56,64},{64,7... | collective-permute-start | bytes 393224 | tf_op jit(solution)/shard_map/ppermute | solution.py:678
  16.5 1.3 %collective-permute-start.5 = (f32[16,2048]{1,0:T(8,128)S(1)}, f32[16,2048]{1,0:T(8,128)S(1)}, u32[]{:S(2)}, u32[]{:S(2)}) collective-permute-start(f32[16,2048]{1,0:T(8,128)S(1)} %get-tuple-element.42.after), channel_id=1, source_target_pairs={{8,0},{16,8},{24,16},{32,24},{40,32},{48,40},{56,48},{64,56},{72,6... | collective-permute-start | bytes 393224 | tf_op jit(solution)/shard_map/ppermute | solution.py:678
  17.9 1.2 %prepare.1 = (f32[40,2048]{1,0:T(8,128)S(1)}, bf16[128,144]{1,0:T(8,128)(2,1)S(1)}, f32[16,128]{1,0:T(8,128)S(1)}, f32[1,20]{1,0:T(1,128)S(1)}, f32[64,20]{1,0:T...) custom-call(s32[20,32768]{1,0:T(8,128)} %counts.1, f32[4,16,4096]{2,1,0:T(8,128)S(1)} %get-tuple-element.36.given_place.given, ...), custom_call_target="tpu_custom_call" | custom-call | tf_op jit(solution)/shard_map/prepare/pallas_call | solution.py:362
  19.1 3.4 %collective-permute-done.5.after = f32[16,2048]{1,0:T(8,128)S(1)} collective-permute-done((f32[16,2048]{1,0:T(8,128)S(1)}, f32[16,2048]{1,0:T(8,128)S(1)}, u32[]{:S(2)}, u32[]{:S(2)}) %collective-permute-start.5) | collective-permute-done | bytes 131104 | tf_op jit(solution)/shard_map/ppermute | solution.py:678
  22.5 3.5 %stencil.1.later.refs_5_ = f32[16,32768]{1,0:T(8,128)} custom-call(f32[4,16,4096]{2,1,0:T(8,128)S(1)} %get-tuple-element.36.given_place.given, f32[4,16,4096]{2,1,0:T(8,128)S(1)} %get-tuple-element.37.kept_place.kept, f32[16,2048]{1,0:T(8,128)S(1)} %collective-permute-done.4.before, f32[16,2048]{1,0:T(8,128)S(1)} %collective-permute-done.5.after, ...), custom_call_target="tpu_custom_call" | custom-call | tf_op jit(solution)/shard_map/stencil/pallas_call | solution.py:427
  27.7 1.0 %ratio.1 = (f32[40,2048]{1,0:T(8,128)S(1)}, f32[256,1,128]{2,1,0:T(1,128)}) custom-call(f32[40,2048]{1,0:T(8,128)S(1)} %get-tuple-element.38.own, f32[40,2048]{1,0:T(8,128)S(1)} %collective-permute-done.1.first, f32[40,2048]{1,0:T(8,128)S(1)} %collective-permute-done.2.second, f32[40,2048]{1,0:T(8,128)S(1)} %collective-permute-done.3.third, ...), custom_call_target="tpu_custom_call" | custom-call | tf_op jit(solution)/shard_map/ratio/pallas_call | solution.py:475
  28.7 1.4 %collective-permute-start.8 = (f32[40,2048]{1,0:T(8,128)S(1)}, f32[40,2048]{1,0:T(8,128)S(1)}, u32[]{:S(2)}, u32[]{:S(2)}) collective-permute-start(f32[40,2048]{1,0:T(8,128)S(1)} %get-tuple-element.50.refs_0_), channel_id=1, source_target_pairs={{0,2},{1,3},{2,4},{3,5},{4,6},{5,7},{6,0},{7,1},{8,10},{9,11},{10,... | collective-permute-start | bytes 983048 | tf_op jit(solution)/shard_map/ppermute | solution.py:672
  30.1 3.1 %collective-permute-start.7 = (f32[40,2048]{1,0:T(8,128)S(1)}, f32[40,2048]{1,0:T(8,128)S(1)}, u32[]{:S(2)}, u32[]{:S(2)}) collective-permute-start(f32[40,2048]{1,0:T(8,128)S(1)} %get-tuple-element.50.refs_0_), channel_id=1, source_target_pairs={{0,4},{1,5},{2,6},{3,7},{4,0},{5,1},{6,2},{7,3},{8,12},{9,13},{10,... | collective-permute-start | bytes 983048 | tf_op jit(solution)/shard_map/ppermute | solution.py:672
  33.3 1.1 %collective-permute-start.11 = (f32[40,2048]{1,0:T(8,128)S(1)}, f32[40,2048]{1,0:T(8,128)S(1)}, u32[]{:S(2)}, u32[]{:S(2)}) collective-permute-start(f32[40,2048]{1,0:T(8,128)S(1)} %get-tuple-element.50.refs_0_), channel_id=1, source_target_pairs={{0,1},{1,0},{2,3},{3,2},{4,5},{5,4},{6,7},{7,6},{8,9},{9,8},{10,11... | collective-permute-start | bytes 983048 | tf_op jit(solution)/shard_map/ppermute | solution.py:661
  34.3 4.7 %collective-permute-done.8.refs_3_ = f32[40,2048]{1,0:T(8,128)S(1)} collective-permute-done((f32[40,2048]{1,0:T(8,128)S(1)}, f32[40,2048]{1,0:T(8,128)S(1)}, u32[]{:S(2)}, u32[]{:S(2)}) %collective-permute-start.8) | collective-permute-done | bytes 327712 | tf_op jit(solution)/shard_map/ppermute | solution.py:672
  39.1 1.7 %collective-permute-start.14 = (f32[40,2048]{1,0:T(8,128)S(1)}, f32[40,2048]{1,0:T(8,128)}, u32[]{:S(2)}, u32[]{:S(2)}) collective-permute-start(f32[40,2048]{1,0:T(8,128)S(1)} %collective-permute-done.8.refs_3_), channel_id=1, source_target_pairs={{0,1},{1,0},{2,3},{3,2},{4,5},{5,4},{6,7},{7,6},{8,9},{9,8},{10,11... | collective-permute-start | bytes 983048 | tf_op jit(solution)/shard_map/ppermute | solution.py:661
  40.7 6.9 %collective-permute-done.7.refs_2_ = f32[40,2048]{1,0:T(8,128)S(1)} collective-permute-done((f32[40,2048]{1,0:T(8,128)S(1)}, f32[40,2048]{1,0:T(8,128)S(1)}, u32[]{:S(2)}, u32[]{:S(2)}) %collective-permute-start.7) | collective-permute-done | bytes 327712 | tf_op jit(solution)/shard_map/ppermute | solution.py:672
  47.6 1.3 %collective-permute-start.13 = (f32[40,2048]{1,0:T(8,128)S(1)}, f32[40,2048]{1,0:T(8,128)}, u32[]{:S(2)}, u32[]{:S(2)}) collective-permute-start(f32[40,2048]{1,0:T(8,128)S(1)} %collective-permute-done.7.refs_2_), channel_id=1, source_target_pairs={{0,1},{1,0},{2,3},{3,2},{4,5},{5,4},{6,7},{7,6},{8,9},{9,8},{10,11... | collective-permute-start | bytes 983048 | tf_op jit(solution)/shard_map/ppermute | solution.py:661
  49.5 12.1 %all-to-all-start = ((f32[256,1,128]{2,1,0:T(1,128)}), f32[256,1,128]{2,1,0:T(1,128)S(1)}, u32[]{:S(2)}, u32[]{:S(2)}) async-start(f32[256,1,128]{2,1,0:T(1,128)} %get-tuple-element.47), calls=%async_computation | async-start | bytes 262144 | tf_op jit(solution)/shard_map/all_to_all | solution.py:725
  61.6 3.5 %collective-permute-start.10 = (f32[1,32768]{1,0:T(1,128)S(1)}, f32[1,32768]{1,0:T(1,128)S(1)}, u32[]{:S(2)}, u32[]{:S(2)}) collective-permute-start(f32[1,32768]{1,0:T(1,128)S(1)} %get-tuple-element.54), channel_id=1, source_target_pairs={{1,2},{3,4},{5,6},{2,1},{4,3},{6,5},{9,10},{11,12},{13,14},{10,9},... | collective-permute-start | bytes 393224 | tf_op jit(solution)/shard_map/ppermute | solution.py:667
  65.2 3.5 %collective-permute-done.10.refs_9_ = f32[1,32768]{1,0:T(1,128)S(1)} collective-permute-done((f32[1,32768]{1,0:T(1,128)S(1)}, f32[1,32768]{1,0:T(1,128)S(1)}, u32[]{:S(2)}, u32[]{:S(2)}) %collective-permute-start.10) | collective-permute-done | bytes 131104 | tf_op jit(solution)/shard_map/ppermute | solution.py:667
  68.6 2.3 %gradient_kept.1.kept = f32[4,16,4096]{2,1,0:T(8,128)S(1)} custom-call(f32[40,2048]{1,0:T(8,128)S(1)} %get-tuple-element.50.refs_0_, f32[40,2048]{1,0:T(8,128)S(1)} %collective-permute-done.6.refs_1_, f32[40,2048]{1,0:T(8,128)S(1)} %collective-permute-done.7.refs_2_, f32[40,2048]{1,0:T(8,128)S(1)} %collective-permute-done.8.refs_3_, ...), custom_call_target="tpu_custom_call" | custom-call | tf_op jit(solution)/shard_map/gradient_kept/pallas_call | solution.py:644
  71.0 3.5 %gradient_given.1.given = f32[4,16,4096]{2,1,0:T(8,128)S(1)} custom-call(f32[40,2048]{1,0:T(8,128)S(1)} %collective-permute-done.11.refs_0_, f32[40,2048]{1,0:T(8,128)} %collective-permute-done.12.refs_1_, f32[40,2048]{1,0:T(8,128)} %collective-permute-done.13.refs_2_, f32[40,2048]{1,0:T(8,128)} %collective-permute-done.14.refs_3_, ...), custom_call_target="tpu_custom_call" | custom-call | tf_op jit(solution)/shard_map/gradient_given/pallas_call | solution.py:644
  74.6 3.2 %finish.1 = (f32[16,32768]{1,0:T(8,128)}, f32[1,1]{1,0:T(1,128)}) custom-call(f32[256,1,128]{2,1,0:T(1,128)S(1)} %all-to-all-done.gathered, f32[1,20]{1,0:T(1,128)S(1)} %get-tuple-element.48.mean, f32[64,20]{1,0:T(8,128)S(1)} %get-tuple-element.49.table, s32[1,32768]{1,0:T(1,128)S(1)} %get-tuple-element.32.depth.refs_6_, ...), custom_call_target="tpu_custom_call" | custom-call | tf_op jit(solution)/shard_map/finish/pallas_call | solution.py:570
  (23 shorter events, 3.5 us)
Async XLA Ops:
  4.0 6.0 %collective-permute-start = (f32[4,40,2048]{2,1,0:T(8,128)S(1)}, f32[4,40,2048]{2,1,0:T(8,128)S(1)}, u32[]{:S(2)}, u32[]{:S(2)}) collective-permute-start(f32[4,40,2048]{2,1,0:T(8,128)S(1)} %get-tuple-element.35), channel_id=1, source_target_pairs={{0,1},{1,0},{2,3},{3,2},{4,5},{5,4},{6,7},{7,6},{8,9},{9,8},{10,11... | collective-permute-start | bytes 3932168 | tf_op jit(solution)/shard_map/ppermute | solution.py:661
  9.9 7.9 %copy-start = (f32[4,20,16]{1,2,0:T(8,128)S(1)}, f32[4,20,16]{1,2,0:T(8,128)}, u32[]{:S(2)}) copy-start(f32[4,20,16]{1,2,0:T(8,128)} %param.10) | copy-start | bytes 15364
  9.9 7.9 %copy-start.1 = (f32[16]{0:T(128)S(1)}, f32[16]{0:T(128)}, u32[]{:S(2)}) copy-start(f32[16]{0:T(128)} %param.15) | copy-start | bytes 196
  10.0 7.9 %copy-start.2 = (f32[20]{0:T(128)S(1)}, f32[20]{0:T(128)}, u32[]{:S(2)}) copy-start(f32[20]{0:T(128)} %param.14) | copy-start | bytes 244
  10.1 15.9 %collective-permute-start.1 = (f32[40,2048]{1,0:T(8,128)S(1)}, f32[40,2048]{1,0:T(8,128)S(1)}, u32[]{:S(2)}, u32[]{:S(2)}) collective-permute-start(f32[40,2048]{1,0:T(8,128)S(1)} %get-tuple-element.39), channel_id=1, source_target_pairs={{0,2},{1,3},{2,4},{3,5},{4,6},{5,7},{6,0},{7,1},{8,10},{9,11},{10,... | collective-permute-start | bytes 983048 | tf_op jit(solution)/shard_map/ppermute | solution.py:672
  10.2 16.4 %collective-permute-start.2 = (f32[40,2048]{1,0:T(8,128)S(1)}, f32[40,2048]{1,0:T(8,128)S(1)}, u32[]{:S(2)}, u32[]{:S(2)}) collective-permute-start(f32[40,2048]{1,0:T(8,128)S(1)} %get-tuple-element.40), channel_id=1, source_target_pairs={{0,4},{1,5},{2,6},{3,7},{4,0},{5,1},{6,2},{7,3},{8,12},{9,13},{10,... | collective-permute-start | bytes 983048 | tf_op jit(solution)/shard_map/ppermute | solution.py:672
  12.2 15.5 %collective-permute-start.3 = (f32[40,2048]{1,0:T(8,128)S(1)}, f32[40,2048]{1,0:T(8,128)S(1)}, u32[]{:S(2)}, u32[]{:S(2)}) collective-permute-start(f32[40,2048]{1,0:T(8,128)S(1)} %get-tuple-element.41), channel_id=1, source_target_pairs={{0,6},{1,7},{2,0},{3,1},{4,2},{5,3},{6,4},{7,5},{8,14},{9,15},{10,... | collective-permute-start | bytes 983048 | tf_op jit(solution)/shard_map/ppermute | solution.py:672
  13.3 5.8 %collective-permute-start.4 = (f32[16,2048]{1,0:T(8,128)S(1)}, f32[16,2048]{1,0:T(8,128)S(1)}, u32[]{:S(2)}, u32[]{:S(2)}) collective-permute-start(f32[16,2048]{1,0:T(8,128)S(1)} %get-tuple-element.45), channel_id=1, source_target_pairs={{0,8},{8,16},{16,24},{24,32},{32,40},{40,48},{48,56},{56,64},{64,7... | collective-permute-start | bytes 393224 | tf_op jit(solution)/shard_map/ppermute | solution.py:678
  16.5 6.0 %collective-permute-start.5 = (f32[16,2048]{1,0:T(8,128)S(1)}, f32[16,2048]{1,0:T(8,128)S(1)}, u32[]{:S(2)}, u32[]{:S(2)}) collective-permute-start(f32[16,2048]{1,0:T(8,128)S(1)} %get-tuple-element.42.after), channel_id=1, source_target_pairs={{8,0},{16,8},{24,16},{32,24},{40,32},{48,40},{56,48},{64,56},{72,6... | collective-permute-start | bytes 393224 | tf_op jit(solution)/shard_map/ppermute | solution.py:678
  28.7 10.4 %collective-permute-start.8 = (f32[40,2048]{1,0:T(8,128)S(1)}, f32[40,2048]{1,0:T(8,128)S(1)}, u32[]{:S(2)}, u32[]{:S(2)}) collective-permute-start(f32[40,2048]{1,0:T(8,128)S(1)} %get-tuple-element.50.refs_0_), channel_id=1, source_target_pairs={{0,2},{1,3},{2,4},{3,5},{4,6},{5,7},{6,0},{7,1},{8,10},{9,11},{10,... | collective-permute-start | bytes 983048 | tf_op jit(solution)/shard_map/ppermute | solution.py:672
  30.1 17.5 %collective-permute-start.7 = (f32[40,2048]{1,0:T(8,128)S(1)}, f32[40,2048]{1,0:T(8,128)S(1)}, u32[]{:S(2)}, u32[]{:S(2)}) collective-permute-start(f32[40,2048]{1,0:T(8,128)S(1)} %get-tuple-element.50.refs_0_), channel_id=1, source_target_pairs={{0,4},{1,5},{2,6},{3,7},{4,0},{5,1},{6,2},{7,3},{8,12},{9,13},{10,... | collective-permute-start | bytes 983048 | tf_op jit(solution)/shard_map/ppermute | solution.py:672
  33.3 15.7 %collective-permute-start.6 = (f32[40,2048]{1,0:T(8,128)S(1)}, f32[40,2048]{1,0:T(8,128)S(1)}, u32[]{:S(2)}, u32[]{:S(2)}) collective-permute-start(f32[40,2048]{1,0:T(8,128)S(1)} %get-tuple-element.50.refs_0_), channel_id=1, source_target_pairs={{0,6},{1,7},{2,0},{3,1},{4,2},{5,3},{6,4},{7,5},{8,14},{9,15},{10,... | collective-permute-start | bytes 983048 | tf_op jit(solution)/shard_map/ppermute | solution.py:672
  33.3 37.7 %collective-permute-start.11 = (f32[40,2048]{1,0:T(8,128)S(1)}, f32[40,2048]{1,0:T(8,128)S(1)}, u32[]{:S(2)}, u32[]{:S(2)}) collective-permute-start(f32[40,2048]{1,0:T(8,128)S(1)} %get-tuple-element.50.refs_0_), channel_id=1, source_target_pairs={{0,1},{1,0},{2,3},{3,2},{4,5},{5,4},{6,7},{7,6},{8,9},{9,8},{10,11... | collective-permute-start | bytes 983048 | tf_op jit(solution)/shard_map/ppermute | solution.py:661
  39.1 31.9 %collective-permute-start.14 = (f32[40,2048]{1,0:T(8,128)S(1)}, f32[40,2048]{1,0:T(8,128)}, u32[]{:S(2)}, u32[]{:S(2)}) collective-permute-start(f32[40,2048]{1,0:T(8,128)S(1)} %collective-permute-done.8.refs_3_), channel_id=1, source_target_pairs={{0,1},{1,0},{2,3},{3,2},{4,5},{5,4},{6,7},{7,6},{8,9},{9,8},{10,11... | collective-permute-start | bytes 983048 | tf_op jit(solution)/shard_map/ppermute | solution.py:661
  47.6 23.4 %collective-permute-start.13 = (f32[40,2048]{1,0:T(8,128)S(1)}, f32[40,2048]{1,0:T(8,128)}, u32[]{:S(2)}, u32[]{:S(2)}) collective-permute-start(f32[40,2048]{1,0:T(8,128)S(1)} %collective-permute-done.7.refs_2_), channel_id=1, source_target_pairs={{0,1},{1,0},{2,3},{3,2},{4,5},{5,4},{6,7},{7,6},{8,9},{9,8},{10,11... | collective-permute-start | bytes 983048 | tf_op jit(solution)/shard_map/ppermute | solution.py:661
  48.9 22.0 %collective-permute-start.12 = (f32[40,2048]{1,0:T(8,128)S(1)}, f32[40,2048]{1,0:T(8,128)}, u32[]{:S(2)}, u32[]{:S(2)}) collective-permute-start(f32[40,2048]{1,0:T(8,128)S(1)} %collective-permute-done.6.refs_1_), channel_id=1, source_target_pairs={{0,1},{1,0},{2,3},{3,2},{4,5},{5,4},{6,7},{7,6},{8,9},{9,8},{10,11... | collective-permute-start | bytes 983048 | tf_op jit(solution)/shard_map/ppermute | solution.py:661
  49.0 12.6 %collective-permute-start.9 = (f32[1,32768]{1,0:T(1,128)S(1)}, f32[1,32768]{1,0:T(1,128)S(1)}, u32[]{:S(2)}, u32[]{:S(2)}) collective-permute-start(f32[1,32768]{1,0:T(1,128)S(1)} %get-tuple-element.53), channel_id=1, source_target_pairs={{0,1},{1,0},{2,3},{3,2},{4,5},{5,4},{6,7},{7,6},{8,9},{9,8},{10,11... | collective-permute-start | bytes 393224 | tf_op jit(solution)/shard_map/ppermute | solution.py:661
  49.5 25.1 %all-to-all-start = ((f32[256,1,128]{2,1,0:T(1,128)}), f32[256,1,128]{2,1,0:T(1,128)S(1)}, u32[]{:S(2)}, u32[]{:S(2)}) async-start(f32[256,1,128]{2,1,0:T(1,128)} %get-tuple-element.47), calls=%async_computation | async-start | bytes 262144 | tf_op jit(solution)/shard_map/all_to_all | solution.py:725
  61.6 7.0 %collective-permute-start.10 = (f32[1,32768]{1,0:T(1,128)S(1)}, f32[1,32768]{1,0:T(1,128)S(1)}, u32[]{:S(2)}, u32[]{:S(2)}) collective-permute-start(f32[1,32768]{1,0:T(1,128)S(1)} %get-tuple-element.54), channel_id=1, source_target_pairs={{1,2},{3,4},{5,6},{2,1},{4,3},{6,5},{9,10},{11,12},{13,14},{10,9},... | collective-permute-start | bytes 393224 | tf_op jit(solution)/shard_map/ppermute | solution.py:667

commit v3 on v2

--- a/solution.py
+++ b/solution.py
@@ -269,22 +269,21 @@
     )(*in_vmem(field, momentum, depth, weights))
 
 
-def combine_body(kept, partner, given_place, kept_place, own, first, second, third, head, tail):
+def combine_body(kept, partner, given_place, kept_place, own, first, second, third, near, beyond):
     chip, core = position_of()
     for d, out in enumerate((own, first, second, third)):
         out[...] = kept[d] + partner[d]
     front, back = (4 - chip) % 4, (7 - chip) % 4
     edge = given_place.shape[2] - CYCLE
-
-    @pl.when(core == 0)
-    def _():
-        head[...] = kept_place[front, :, :CYCLE]
-        tail[...] = given_place[back, :, edge:]
-
-    @pl.when(core == 1)
-    def _():
-        head[...] = given_place[front, :, :CYCLE]
-        tail[...] = kept_place[back, :, edge:]
+    even = lax.axis_index("pix") % 2 == 0
+
+    def ends(low, high):
+        head, tail = low[front, :, :CYCLE], high[back, :, edge:]
+        near[...] = jnp.where(even, tail, head)
+        beyond[...] = jnp.where(even, head, tail)
+
+    pl.when(core == 0)(lambda: ends(kept_place, given_place))
+    pl.when(core == 1)(lambda: ends(given_place, kept_place))
 
 
 def combine(kept, partner, given_place, kept_place):
@@ -379,13 +378,14 @@
 
 
 def stencil_body(
-    given, kept, before, after, scale, away, position, out, marks
+    given, kept, near, beyond, scale, away, position, out, marks
 ):
     _, shells, width = given.shape
     pixels = 8 * width
     chip, core = position_of()
-    position[:, :CYCLE] = before[...]
-    position[:, CYCLE + pixels :] = after[...]
+    even = lax.axis_index("pix") % 2 == 0
+    position[:, :CYCLE] = jnp.where(even, beyond[...], near[...])
+    position[:, CYCLE + pixels :] = jnp.where(even, near[...], beyond[...])
     for d in range(4):
         for source, half in ((given, 1 - core), (kept, core)):
             base = offset_of(half, d, chip, width)
@@ -672,10 +672,9 @@
     return lax.ppermute(values, "shell", [(i, (i + 2 * step) % count) for i in range(count)])
 
 
-def halo(values, axis, step):
-    count = lax.axis_size(axis)
-    pairs = [(i, i + step) for i in range(count) if 0 <= i + step < count]
-    return lax.ppermute(values, axis, pairs)
+def across(values, start):
+    pairs = [(i, i + 1) for i in range(start, lax.axis_size("pix") - 1, 2)]
+    return lax.ppermute(values, "pix", pairs + [(b, a) for a, b in pairs])
 
 
 def shards(field, momentum, kernels, depth_class, counts, mask, mean_counts, shell_scale):
@@ -698,34 +697,33 @@
     proj_kept, density_kept, place_kept = project_kept(
         field_kept, momentum_kept, depth, weights, classes, bins
     )
-    own, first, second, third, head, tail = combine(
+    own, first, second, third, near, beyond = combine(
         proj_kept, proj_partner, place_given, place_kept
     )
+    second = along(second, 2)
     first = along(first, 1)
     third = along(third, 3)
-    second = along(second, 2)
-    after = halo(head, "pix", -1)
-    before = halo(tail, "pix", 1)
+    near = across(near, 0)
+    beyond = across(beyond, 1)
     own_counts, weights, square, mean, table, to_partner, to_side = prepare(
         counts,
         place_given,
         place_kept,
-        head,
+        own,
         table,
         shell_scale.reshape(1, shells),
         mean_counts.reshape(1, bins),
     )
     partner_row = swap(to_partner)
     side_row = beside(to_side)
-    rest = stencil(place_given, place_kept, before, after, square)
+    rest = stencil(place_given, place_kept, near, beyond, square)
     quotient, stats = ratio(own, first, second, third, own_counts, cover, rest)
+    from_far = along(quotient, 2)
     from_back = along(quotient, 1)
     from_front = along(quotient, 3)
-    from_far = along(quotient, 2)
     gathered = lax.all_to_all(stats, ("pix", "shell"), 0, 0)
     mine = [quotient, from_front, from_far, from_back]
-    theirs = [swap(q) for q in mine[1:]]
-    theirs = [swap(quotient), *theirs]
+    theirs = [swap(q) for q in mine]
 
     common = (rest, depth, weights, partner_row, side_row, classes, bins)
     kept = gradient(mine, density_kept, *common, True)

time: 78.3 us -> 77.6 us (level)
  starting transfers between devices: 35.8 us -> 32.6 us
  waiting for transfers between devices: 21.2 us -> 23.7 us
    ppermute x6, waiting for transfers between devices: 13.2 us -> 18.3 us  [along(): lax.ppermute(values, 'shell', [(i, (i + 2 * step) % count) for i in range...]
    ppermute x2, waiting for transfers between devices: 3.44 us -> 0.9 us  [across(): return lax.ppermute(values, 'pix', pairs + [(b, a) for a, b in pairs])]
    ppermute x2, starting transfers between devices: 4.49 us -> 1.95 us  [across(): return lax.ppermute(values, 'pix', pairs + [(b, a) for a, b in pairs])]
where the time goes in v3:
time: 77.6 us; the launch traced here: 77.3 us
  starting transfers between devices  32.6 us (42%)
  waiting for transfers between devices  23.7 us (31%)
  Pallas kernels  20.1 us (26%)
  between operations  0.95 us (1%)
    ppermute x6, waiting for transfers between devices, along(): lax.ppermute(values, 'shell', [(i, (i + 2 * step) % count) for i in range...  18.3 us
    all_to_all x1, starting transfers between devices, shards(): gathered = lax.all_to_all(stats, ('pix', 'shell'), 0, 0)  11.5 us
    ppermute x6, starting transfers between devices, swap(): return lax.ppermute(values, 'shell', [(i, i ^ 1) for i in range(count)])  7.88 us
    ppermute x6, starting transfers between devices, along(): lax.ppermute(values, 'shell', [(i, (i + 2 * step) % count) for i in range...  7.73 us
    pallas_call x2, Pallas kernels, gradient(): pl.pallas_call(functools.partial(gradient_body, classes=classes, bins=bin...  5.74 us
    pallas_call x1, Pallas kernels, stencil(): pl.pallas_call(stencil_body, in_specs=[HERE] * 5, out_specs=AWAY, out_sha...  3.54 us
    ppermute x1, starting transfers between devices, beside(): return lax.ppermute(values, 'shell', pairs + [(b, a) for a, b in pairs])  3.54 us
    ppermute x1, waiting for transfers between devices, beside(): return lax.ppermute(values, 'shell', pairs + [(b, a) for a, b in pairs])  3.49 us
  transfers between devices with their start and end apart: 16, of which 8 were waited for; matrix products, arithmetic and copies ran while one was open for 0% of the time, Pallas kernels for 16%

profile of v3, /device:TPU:1, one launch (start us, length us, event | category | flops | bytes accessed | tf_op | source)
XLA Modules:
  0.0 77.3 jit_solution(1550302398837709222)
XLA Ops:
  0.6 3.4 %project_given.1 = (f32[4,40,2048]{2,1,0:T(8,128)S(1)}, f32[4,16,4096]{2,1,0:T(8,128)}, f32[4,16,4096]{2,1,0:T(8,128)S(1)}, f32[4,16,4096]{2,1,0:T(8,128)S(1)}, ...) custom-call(f32[16,32768]{1,0:T(8,128)} %field.1, ...), custom_call_target="tpu_custom_call" | custom-call | tf_op jit(solution)/shard_map/project_given/pallas_call | solution.py:211
  4.0 3.3 %collective-permute-start = (f32[4,40,2048]{2,1,0:T(8,128)S(1)}, f32[4,40,2048]{2,1,0:T(8,128)S(1)}, u32[]{:S(2)}, u32[]{:S(2)}) collective-permute-start(f32[4,40,2048]{2,1,0:T(8,128)S(1)} %get-tuple-element.35), channel_id=1, source_target_pairs={{0,1},{1,0},{2,3},{3,2},{4,5},{5,4},{6,7},{7,6},{8,9},{9,8},{10,11... | collective-permute-start | bytes 3932168 | tf_op jit(solution)/shard_map/ppermute | solution.py:661
  7.3 1.8 %project_kept.1 = (f32[4,40,2048]{2,1,0:T(8,128)S(1)}, f32[4,16,4096]{2,1,0:T(8,128)}, f32[4,16,4096]{2,1,0:T(8,128)S(1)}) custom-call(f32[4,16,4096]{2,1,0:T(8,128)S(1)} %get-tuple-element.30.field, f32[4,16,4096]{2,1,0:T(8,128)S(1)} %get-tuple-element.31.momentum, s32[1,32768]{1,0:T(1,128)S(1)} %get-tuple-element.32.depth.refs_6_, ...), custom_call_target="tpu_custom_call" | custom-call | tf_op jit(solution)/shard_map/project_kept/pallas_call | solution.py:261
  10.2 1.9 %collective-permute-start.2 = (f32[40,2048]{1,0:T(8,128)S(1)}, f32[40,2048]{1,0:T(8,128)S(1)}, u32[]{:S(2)}, u32[]{:S(2)}) collective-permute-start(f32[40,2048]{1,0:T(8,128)S(1)} %get-tuple-element.40), channel_id=1, source_target_pairs={{0,4},{1,5},{2,6},{3,7},{4,0},{5,1},{6,2},{7,3},{8,12},{9,13},{10,... | collective-permute-start | bytes 983048 | tf_op jit(solution)/shard_map/ppermute | solution.py:672
  12.2 1.2 %collective-permute-start.3 = (f32[40,2048]{1,0:T(8,128)S(1)}, f32[40,2048]{1,0:T(8,128)S(1)}, u32[]{:S(2)}, u32[]{:S(2)}) collective-permute-start(f32[40,2048]{1,0:T(8,128)S(1)} %get-tuple-element.41), channel_id=1, source_target_pairs={{0,6},{1,7},{2,0},{3,1},{4,2},{5,3},{6,4},{7,5},{8,14},{9,15},{10,... | collective-permute-start | bytes 983048 | tf_op jit(solution)/shard_map/ppermute | solution.py:672
  13.3 1.3 %collective-permute-start.4 = (f32[16,2048]{1,0:T(8,128)S(1)}, f32[16,2048]{1,0:T(8,128)S(1)}, u32[]{:S(2)}, u32[]{:S(2)}) collective-permute-start(f32[16,2048]{1,0:T(8,128)S(1)} %get-tuple-element.44), channel_id=1, source_target_pairs={{0,8},{16,24},{32,40},{48,56},{64,72},{80,88},{96,104},{112,120},{... | collective-permute-start | bytes 393224 | tf_op jit(solution)/shard_map/ppermute | solution.py:677
  15.3 1.2 %prepare.1 = (f32[40,2048]{1,0:T(8,128)S(1)}, bf16[128,144]{1,0:T(8,128)(2,1)S(1)}, f32[16,128]{1,0:T(8,128)S(1)}, f32[1,20]{1,0:T(1,128)S(1)}, f32[64,20]{1,0:T...) custom-call(s32[20,32768]{1,0:T(8,128)} %counts.1, f32[4,16,4096]{2,1,0:T(8,128)S(1)} %get-tuple-element.36.given_place.given, ...), custom_call_target="tpu_custom_call" | custom-call | tf_op jit(solution)/shard_map/prepare/pallas_call | solution.py:361
  17.5 3.5 %stencil.1.later.refs_5_ = f32[16,32768]{1,0:T(8,128)} custom-call(f32[4,16,4096]{2,1,0:T(8,128)S(1)} %get-tuple-element.36.given_place.given, f32[4,16,4096]{2,1,0:T(8,128)S(1)} %get-tuple-element.37.kept_place.kept, f32[16,2048]{1,0:T(8,128)S(1)} %collective-permute-done.4.near, f32[16,2048]{1,0:T(8,128)S(1)} %collective-permute-done.5.beyond, ...), custom_call_target="tpu_custom_call" | custom-call | tf_op jit(solution)/shard_map/stencil/pallas_call | solution.py:427
  21.0 5.6 %collective-permute-done.2.second = f32[40,2048]{1,0:T(8,128)S(1)} collective-permute-done((f32[40,2048]{1,0:T(8,128)S(1)}, f32[40,2048]{1,0:T(8,128)S(1)}, u32[]{:S(2)}, u32[]{:S(2)}) %collective-permute-start.2) | collective-permute-done | bytes 327712 | tf_op jit(solution)/shard_map/ppermute | solution.py:672
  26.7 1.0 %collective-permute-done.3.third = f32[40,2048]{1,0:T(8,128)S(1)} collective-permute-done((f32[40,2048]{1,0:T(8,128)S(1)}, f32[40,2048]{1,0:T(8,128)S(1)}, u32[]{:S(2)}, u32[]{:S(2)}) %collective-permute-start.3) | collective-permute-done | bytes 327712 | tf_op jit(solution)/shard_map/ppermute | solution.py:672
  27.7 1.0 %ratio.1 = (f32[40,2048]{1,0:T(8,128)S(1)}, f32[256,1,128]{2,1,0:T(1,128)}) custom-call(f32[40,2048]{1,0:T(8,128)S(1)} %get-tuple-element.38.after.own, f32[40,2048]{1,0:T(8,128)S(1)} %collective-permute-done.1.first, f32[40,2048]{1,0:T(8,128)S(1)} %collective-permute-done.2.second, f32[40,2048]{1,0:T(8,128)S(1)} %collective-permute-done.3.third, ...), custom_call_target="tpu_custom_call" | custom-call | tf_op jit(solution)/shard_map/ratio/pallas_call | solution.py:475
  28.7 1.4 %collective-permute-start.8 = (f32[40,2048]{1,0:T(8,128)S(1)}, f32[40,2048]{1,0:T(8,128)S(1)}, u32[]{:S(2)}, u32[]{:S(2)}) collective-permute-start(f32[40,2048]{1,0:T(8,128)S(1)} %get-tuple-element.50.refs_0_), channel_id=1, source_target_pairs={{0,2},{1,3},{2,4},{3,5},{4,6},{5,7},{6,0},{7,1},{8,10},{9,11},{10,... | collective-permute-start | bytes 983048 | tf_op jit(solution)/shard_map/ppermute | solution.py:672
  30.1 3.1 %collective-permute-start.7 = (f32[40,2048]{1,0:T(8,128)S(1)}, f32[40,2048]{1,0:T(8,128)S(1)}, u32[]{:S(2)}, u32[]{:S(2)}) collective-permute-start(f32[40,2048]{1,0:T(8,128)S(1)} %get-tuple-element.50.refs_0_), channel_id=1, source_target_pairs={{0,4},{1,5},{2,6},{3,7},{4,0},{5,1},{6,2},{7,3},{8,12},{9,13},{10,... | collective-permute-start | bytes 983048 | tf_op jit(solution)/shard_map/ppermute | solution.py:672
  33.3 1.1 %collective-permute-start.11 = (f32[40,2048]{1,0:T(8,128)S(1)}, f32[40,2048]{1,0:T(8,128)S(1)}, u32[]{:S(2)}, u32[]{:S(2)}) collective-permute-start(f32[40,2048]{1,0:T(8,128)S(1)} %get-tuple-element.50.refs_0_), channel_id=1, source_target_pairs={{0,1},{1,0},{2,3},{3,2},{4,5},{5,4},{6,7},{7,6},{8,9},{9,8},{10,11... | collective-permute-start | bytes 983048 | tf_op jit(solution)/shard_map/ppermute | solution.py:661
  34.3 4.7 %collective-permute-done.8.refs_3_ = f32[40,2048]{1,0:T(8,128)S(1)} collective-permute-done((f32[40,2048]{1,0:T(8,128)S(1)}, f32[40,2048]{1,0:T(8,128)S(1)}, u32[]{:S(2)}, u32[]{:S(2)}) %collective-permute-start.8) | collective-permute-done | bytes 327712 | tf_op jit(solution)/shard_map/ppermute | solution.py:672
  39.1 1.7 %collective-permute-start.14 = (f32[40,2048]{1,0:T(8,128)S(1)}, f32[40,2048]{1,0:T(8,128)}, u32[]{:S(2)}, u32[]{:S(2)}) collective-permute-start(f32[40,2048]{1,0:T(8,128)S(1)} %collective-permute-done.8.refs_3_), channel_id=1, source_target_pairs={{0,1},{1,0},{2,3},{3,2},{4,5},{5,4},{6,7},{7,6},{8,9},{9,8},{10,11... | collective-permute-start | bytes 983048 | tf_op jit(solution)/shard_map/ppermute | solution.py:661
  40.8 6.9 %collective-permute-done.7.refs_2_ = f32[40,2048]{1,0:T(8,128)S(1)} collective-permute-done((f32[40,2048]{1,0:T(8,128)S(1)}, f32[40,2048]{1,0:T(8,128)S(1)}, u32[]{:S(2)}, u32[]{:S(2)}) %collective-permute-start.7) | collective-permute-done | bytes 327712 | tf_op jit(solution)/shard_map/ppermute | solution.py:672
  47.6 1.3 %collective-permute-start.13 = (f32[40,2048]{1,0:T(8,128)S(1)}, f32[40,2048]{1,0:T(8,128)}, u32[]{:S(2)}, u32[]{:S(2)}) collective-permute-start(f32[40,2048]{1,0:T(8,128)S(1)} %collective-permute-done.7.refs_2_), channel_id=1, source_target_pairs={{0,1},{1,0},{2,3},{3,2},{4,5},{5,4},{6,7},{7,6},{8,9},{9,8},{10,11... | collective-permute-start | bytes 983048 | tf_op jit(solution)/shard_map/ppermute | solution.py:661
  49.5 11.5 %all-to-all-start = ((f32[256,1,128]{2,1,0:T(1,128)}), f32[256,1,128]{2,1,0:T(1,128)S(1)}, u32[]{:S(2)}, u32[]{:S(2)}) async-start(f32[256,1,128]{2,1,0:T(1,128)} %get-tuple-element.47), calls=%async_computation | async-start | bytes 262144 | tf_op jit(solution)/shard_map/all_to_all | solution.py:724
  61.0 3.5 %collective-permute-start.10 = (f32[1,32768]{1,0:T(1,128)S(1)}, f32[1,32768]{1,0:T(1,128)S(1)}, u32[]{:S(2)}, u32[]{:S(2)}) collective-permute-start(f32[1,32768]{1,0:T(1,128)S(1)} %get-tuple-element.54), channel_id=1, source_target_pairs={{1,2},{3,4},{5,6},{2,1},{4,3},{6,5},{9,10},{11,12},{13,14},{10,9},... | collective-permute-start | bytes 393224 | tf_op jit(solution)/shard_map/ppermute | solution.py:667
  64.5 3.5 %collective-permute-done.10.refs_9_ = f32[1,32768]{1,0:T(1,128)S(1)} collective-permute-done((f32[1,32768]{1,0:T(1,128)S(1)}, f32[1,32768]{1,0:T(1,128)S(1)}, u32[]{:S(2)}, u32[]{:S(2)}) %collective-permute-start.10) | collective-permute-done | bytes 131104 | tf_op jit(solution)/shard_map/ppermute | solution.py:667
  68.0 2.3 %gradient_kept.1.kept = f32[4,16,4096]{2,1,0:T(8,128)S(1)} custom-call(f32[40,2048]{1,0:T(8,128)S(1)} %get-tuple-element.50.refs_0_, f32[40,2048]{1,0:T(8,128)S(1)} %collective-permute-done.6.refs_1_, f32[40,2048]{1,0:T(8,128)S(1)} %collective-permute-done.7.refs_2_, f32[40,2048]{1,0:T(8,128)S(1)} %collective-permute-done.8.refs_3_, ...), custom_call_target="tpu_custom_call" | custom-call | tf_op jit(solution)/shard_map/gradient_kept/pallas_call | solution.py:644
  70.4 3.5 %gradient_given.1.given = f32[4,16,4096]{2,1,0:T(8,128)S(1)} custom-call(f32[40,2048]{1,0:T(8,128)S(1)} %collective-permute-done.11.refs_0_, f32[40,2048]{1,0:T(8,128)} %collective-permute-done.12.refs_1_, f32[40,2048]{1,0:T(8,128)} %collective-permute-done.13.refs_2_, f32[40,2048]{1,0:T(8,128)} %collective-permute-done.14.refs_3_, ...), custom_call_target="tpu_custom_call" | custom-call | tf_op jit(solution)/shard_map/gradient_given/pallas_call | solution.py:644
  74.0 3.2 %finish.1 = (f32[16,32768]{1,0:T(8,128)}, f32[1,1]{1,0:T(1,128)}) custom-call(f32[256,1,128]{2,1,0:T(1,128)S(1)} %all-to-all-done.gathered, f32[1,20]{1,0:T(1,128)S(1)} %get-tuple-element.48.mean, f32[64,20]{1,0:T(8,128)S(1)} %get-tuple-element.49.table, s32[1,32768]{1,0:T(1,128)S(1)} %get-tuple-element.32.depth.refs_6_, ...), custom_call_target="tpu_custom_call" | custom-call | tf_op jit(solution)/shard_map/finish/pallas_call | solution.py:570
  (23 shorter events, 3.4 us)
Async XLA Ops:
  4.0 6.0 %collective-permute-start = (f32[4,40,2048]{2,1,0:T(8,128)S(1)}, f32[4,40,2048]{2,1,0:T(8,128)S(1)}, u32[]{:S(2)}, u32[]{:S(2)}) collective-permute-start(f32[4,40,2048]{2,1,0:T(8,128)S(1)} %get-tuple-element.35), channel_id=1, source_target_pairs={{0,1},{1,0},{2,3},{3,2},{4,5},{5,4},{6,7},{7,6},{8,9},{9,8},{10,11... | collective-permute-start | bytes 3932168 | tf_op jit(solution)/shard_map/ppermute | solution.py:661
  9.9 5.4 %copy-start = (f32[4,20,16]{1,2,0:T(8,128)S(1)}, f32[4,20,16]{1,2,0:T(8,128)}, u32[]{:S(2)}) copy-start(f32[4,20,16]{1,2,0:T(8,128)} %param.10) | copy-start | bytes 15364
  9.9 5.4 %copy-start.1 = (f32[16]{0:T(128)S(1)}, f32[16]{0:T(128)}, u32[]{:S(2)}) copy-start(f32[16]{0:T(128)} %param.15) | copy-start | bytes 196
  10.0 5.4 %copy-start.2 = (f32[20]{0:T(128)S(1)}, f32[20]{0:T(128)}, u32[]{:S(2)}) copy-start(f32[20]{0:T(128)} %param.14) | copy-start | bytes 244
  10.1 10.9 %collective-permute-start.1 = (f32[40,2048]{1,0:T(8,128)S(1)}, f32[40,2048]{1,0:T(8,128)S(1)}, u32[]{:S(2)}, u32[]{:S(2)}) collective-permute-start(f32[40,2048]{1,0:T(8,128)S(1)} %get-tuple-element.39), channel_id=1, source_target_pairs={{0,2},{1,3},{2,4},{3,5},{4,6},{5,7},{6,0},{7,1},{8,10},{9,11},{10,... | collective-permute-start | bytes 983048 | tf_op jit(solution)/shard_map/ppermute | solution.py:672
  10.2 16.4 %collective-permute-start.2 = (f32[40,2048]{1,0:T(8,128)S(1)}, f32[40,2048]{1,0:T(8,128)S(1)}, u32[]{:S(2)}, u32[]{:S(2)}) collective-permute-start(f32[40,2048]{1,0:T(8,128)S(1)} %get-tuple-element.40), channel_id=1, source_target_pairs={{0,4},{1,5},{2,6},{3,7},{4,0},{5,1},{6,2},{7,3},{8,12},{9,13},{10,... | collective-permute-start | bytes 983048 | tf_op jit(solution)/shard_map/ppermute | solution.py:672
  12.2 15.5 %collective-permute-start.3 = (f32[40,2048]{1,0:T(8,128)S(1)}, f32[40,2048]{1,0:T(8,128)S(1)}, u32[]{:S(2)}, u32[]{:S(2)}) collective-permute-start(f32[40,2048]{1,0:T(8,128)S(1)} %get-tuple-element.41), channel_id=1, source_target_pairs={{0,6},{1,7},{2,0},{3,1},{4,2},{5,3},{6,4},{7,5},{8,14},{9,15},{10,... | collective-permute-start | bytes 983048 | tf_op jit(solution)/shard_map/ppermute | solution.py:672
  13.3 4.1 %collective-permute-start.4 = (f32[16,2048]{1,0:T(8,128)S(1)}, f32[16,2048]{1,0:T(8,128)S(1)}, u32[]{:S(2)}, u32[]{:S(2)}) collective-permute-start(f32[16,2048]{1,0:T(8,128)S(1)} %get-tuple-element.44), channel_id=1, source_target_pairs={{0,8},{16,24},{32,40},{48,56},{64,72},{80,88},{96,104},{112,120},{... | collective-permute-start | bytes 393224 | tf_op jit(solution)/shard_map/ppermute | solution.py:677
  14.6 2.8 %collective-permute-start.5 = (f32[16,2048]{1,0:T(8,128)S(1)}, f32[16,2048]{1,0:T(8,128)S(1)}, u32[]{:S(2)}, u32[]{:S(2)}) collective-permute-start(f32[16,2048]{1,0:T(8,128)S(1)} %get-tuple-element.45), channel_id=1, source_target_pairs={{8,16},{24,32},{40,48},{56,64},{72,80},{88,96},{104,112},{120,128}... | collective-permute-start | bytes 393224 | tf_op jit(solution)/shard_map/ppermute | solution.py:677
  28.7 10.4 %collective-permute-start.8 = (f32[40,2048]{1,0:T(8,128)S(1)}, f32[40,2048]{1,0:T(8,128)S(1)}, u32[]{:S(2)}, u32[]{:S(2)}) collective-permute-start(f32[40,2048]{1,0:T(8,128)S(1)} %get-tuple-element.50.refs_0_), channel_id=1, source_target_pairs={{0,2},{1,3},{2,4},{3,5},{4,6},{5,7},{6,0},{7,1},{8,10},{9,11},{10,... | collective-permute-start | bytes 983048 | tf_op jit(solution)/shard_map/ppermute | solution.py:672
  30.1 17.5 %collective-permute-start.7 = (f32[40,2048]{1,0:T(8,128)S(1)}, f32[40,2048]{1,0:T(8,128)S(1)}, u32[]{:S(2)}, u32[]{:S(2)}) collective-permute-start(f32[40,2048]{1,0:T(8,128)S(1)} %get-tuple-element.50.refs_0_), channel_id=1, source_target_pairs={{0,4},{1,5},{2,6},{3,7},{4,0},{5,1},{6,2},{7,3},{8,12},{9,13},{10,... | collective-permute-start | bytes 983048 | tf_op jit(solution)/shard_map/ppermute | solution.py:672
  33.3 15.7 %collective-permute-start.6 = (f32[40,2048]{1,0:T(8,128)S(1)}, f32[40,2048]{1,0:T(8,128)S(1)}, u32[]{:S(2)}, u32[]{:S(2)}) collective-permute-start(f32[40,2048]{1,0:T(8,128)S(1)} %get-tuple-element.50.refs_0_), channel_id=1, source_target_pairs={{0,6},{1,7},{2,0},{3,1},{4,2},{5,3},{6,4},{7,5},{8,14},{9,15},{10,... | collective-permute-start | bytes 983048 | tf_op jit(solution)/shard_map/ppermute | solution.py:672
  33.3 37.0 %collective-permute-start.11 = (f32[40,2048]{1,0:T(8,128)S(1)}, f32[40,2048]{1,0:T(8,128)S(1)}, u32[]{:S(2)}, u32[]{:S(2)}) collective-permute-start(f32[40,2048]{1,0:T(8,128)S(1)} %get-tuple-element.50.refs_0_), channel_id=1, source_target_pairs={{0,1},{1,0},{2,3},{3,2},{4,5},{5,4},{6,7},{7,6},{8,9},{9,8},{10,11... | collective-permute-start | bytes 983048 | tf_op jit(solution)/shard_map/ppermute | solution.py:661
  39.1 31.2 %collective-permute-start.14 = (f32[40,2048]{1,0:T(8,128)S(1)}, f32[40,2048]{1,0:T(8,128)}, u32[]{:S(2)}, u32[]{:S(2)}) collective-permute-start(f32[40,2048]{1,0:T(8,128)S(1)} %collective-permute-done.8.refs_3_), channel_id=1, source_target_pairs={{0,1},{1,0},{2,3},{3,2},{4,5},{5,4},{6,7},{7,6},{8,9},{9,8},{10,11... | collective-permute-start | bytes 983048 | tf_op jit(solution)/shard_map/ppermute | solution.py:661
  47.6 22.7 %collective-permute-start.13 = (f32[40,2048]{1,0:T(8,128)S(1)}, f32[40,2048]{1,0:T(8,128)}, u32[]{:S(2)}, u32[]{:S(2)}) collective-permute-start(f32[40,2048]{1,0:T(8,128)S(1)} %collective-permute-done.7.refs_2_), channel_id=1, source_target_pairs={{0,1},{1,0},{2,3},{3,2},{4,5},{5,4},{6,7},{7,6},{8,9},{9,8},{10,11... | collective-permute-start | bytes 983048 | tf_op jit(solution)/shard_map/ppermute | solution.py:661
  49.0 21.4 %collective-permute-start.12 = (f32[40,2048]{1,0:T(8,128)S(1)}, f32[40,2048]{1,0:T(8,128)}, u32[]{:S(2)}, u32[]{:S(2)}) collective-permute-start(f32[40,2048]{1,0:T(8,128)S(1)} %collective-permute-done.6.refs_1_), channel_id=1, source_target_pairs={{0,1},{1,0},{2,3},{3,2},{4,5},{5,4},{6,7},{7,6},{8,9},{9,8},{10,11... | collective-permute-start | bytes 983048 | tf_op jit(solution)/shard_map/ppermute | solution.py:661
  49.0 12.0 %collective-permute-start.9 = (f32[1,32768]{1,0:T(1,128)S(1)}, f32[1,32768]{1,0:T(1,128)S(1)}, u32[]{:S(2)}, u32[]{:S(2)}) collective-permute-start(f32[1,32768]{1,0:T(1,128)S(1)} %get-tuple-element.53), channel_id=1, source_target_pairs={{0,1},{1,0},{2,3},{3,2},{4,5},{5,4},{6,7},{7,6},{8,9},{9,8},{10,11... | collective-permute-start | bytes 393224 | tf_op jit(solution)/shard_map/ppermute | solution.py:661
  49.5 24.5 %all-to-all-start = ((f32[256,1,128]{2,1,0:T(1,128)}), f32[256,1,128]{2,1,0:T(1,128)S(1)}, u32[]{:S(2)}, u32[]{:S(2)}) async-start(f32[256,1,128]{2,1,0:T(1,128)} %get-tuple-element.47), calls=%async_computation | async-start | bytes 262144 | tf_op jit(solution)/shard_map/all_to_all | solution.py:724
  61.0 7.0 %collective-permute-start.10 = (f32[1,32768]{1,0:T(1,128)S(1)}, f32[1,32768]{1,0:T(1,128)S(1)}, u32[]{:S(2)}, u32[]{:S(2)}) collective-permute-start(f32[1,32768]{1,0:T(1,128)S(1)} %get-tuple-element.54), channel_id=1, source_target_pairs={{1,2},{3,4},{5,6},{2,1},{4,3},{6,5},{9,10},{11,12},{13,14},{10,9},... | collective-permute-start | bytes 393224 | tf_op jit(solution)/shard_map/ppermute | solution.py:667

commit v4 on v3

--- a/solution.py
+++ b/solution.py
@@ -5,7 +5,7 @@
 from jax import lax
 from jax.experimental import pallas as pl
 from jax.experimental.pallas import tpu as pltpu
-from jax.sharding import PartitionSpec as P
+from jax.sharding import Mesh, PartitionSpec as P
 
 
 CYCLE = 2048
@@ -69,8 +69,7 @@
 
 
 def position_of():
-    place = lax.axis_index("shell")
-    return place // 2, place % 2
+    return lax.axis_index("x"), lax.axis_index("core")
 
 
 def offset_of(half, turn, chip, width):
@@ -465,10 +464,20 @@
             weighted = weighted + covered[:, lane : lane + 128]
             logs = logs + term[:, lane : lane + 128]
             totals = totals + some[:, lane : lane + 128]
-    filler = jnp.zeros((128 - 3 * rows, 128), jnp.float32)
-    sums = jnp.concatenate([weighted, logs, totals, filler], axis=0)
+    gap = jnp.zeros((32 - bins, 128), jnp.float32)
+    sums = jnp.concatenate(
+        [
+            weighted[:bins] + weighted[bins:],
+            gap,
+            totals[:bins] + totals[bins:],
+            gap,
+            logs,
+            jnp.zeros((64 - rows, 128), jnp.float32),
+        ],
+        axis=0,
+    )
     row = exact_rows(sums, jnp.ones((8, 128), jnp.bfloat16))[:1]
-    stats[...] = jnp.broadcast_to(row[:, None], stats.shape)
+    stats[...] = jnp.broadcast_to(row.reshape((1,) * (stats.ndim - 1) + (128,)), stats.shape)
 
 
 def ratio(own, first, second, third, counts, mask, later):
@@ -478,23 +487,11 @@
         out_specs=[HERE, HERE],
         out_shape=[
             vmem(*own.shape),
-            vmem(lax.axis_size("pix") * lax.axis_size("shell"), 1, 128),
+            vmem(1, 128),
         ],
         compiler_params=LIMIT,
         name="ratio",
     )(*in_vmem(own, first, second, third, counts, mask), *in_hbm(later))
-
-
-def lanes_of(row, low, high, bins):
-    at, lane = iota((bins, 128), 0), iota((bins, 128), 1)
-    pick = (lane >= low) & (lane < high) & (lane % bins == at)
-    pick = jnp.where(pick, 1.0, 0.0).astype(jnp.bfloat16)
-    total = 0.0
-    for _ in range(3):
-        part = row.astype(jnp.bfloat16)
-        row = row - part.astype(jnp.float32)
-        total = total + dot_nt(part, pick)
-    return total
 
 
 def finish_body(
@@ -528,16 +525,10 @@
             copies.append(pltpu.make_async_copy(away.at[d], density.at[slot], marks.at[slot]))
             copies[-1].start()
     row = jnp.broadcast_to(jnp.sum(gathered[...], axis=0), (8, 128))
-    weighted = lanes_of(row, 0, 2 * bins, bins)[:1]
-    total = lanes_of(row, 4 * bins, 6 * bins, bins)[:1]
+    weighted = row[:1, :bins]
+    total = pltpu.roll(row, 96, 1)[:1, :bins]
     norm = weighted / total_pix
     level = total / (total_pix * norm)
-    average = mean[...]
-    terms = total * jnp.log(average / norm) - average * (weighted / norm)
-    lane = iota((1, 128), 1)
-    logs = jnp.where((lane >= 2 * bins) & (lane < 4 * bins), row[:1], 0.0)
-    value = jnp.sum(terms, axis=1, keepdims=True) + jnp.sum(logs, axis=1, keepdims=True)
-    loglik[...] = value / (bins * total_pix)
     drop = jnp.sum(table[...] * level, axis=1, keepdims=True)
     drop = jnp.broadcast_to(drop, (drop.shape[0], WIDE))
     for slot, (side, d, base) in enumerate(pieces):
@@ -556,6 +547,12 @@
             )
         )
         copies[-1].start()
+    average = mean[...]
+    terms = total * jnp.log(average / norm) - average * (weighted / norm)
+    lane = iota((1, 128), 1)
+    logs = jnp.where(lane >= 64, row[:1], 0.0)
+    value = jnp.sum(terms, axis=1, keepdims=True) + jnp.sum(logs, axis=1, keepdims=True)
+    loglik[...] = value / (bins * total_pix)
     for copy in copies[8:]:
         copy.wait()
 
@@ -656,20 +653,35 @@
     )(*operands)
 
 
+def pair_body(mine, partner, out):
+    row = mine[...] + partner[...]
+    out[...] = jnp.broadcast_to(row[None], out.shape)
+
+
+def pair(mine, partner):
+    return pl.pallas_call(
+        pair_body,
+        in_specs=[HERE] * 2,
+        out_specs=HERE,
+        out_shape=vmem(lax.axis_size("pix") * lax.axis_size("x"), 1, 128),
+        compiler_params=LIMIT,
+        name="pair",
+    )(*in_vmem(mine, partner))
+
+
 def swap(values):
-    count = lax.axis_size("shell")
-    return lax.ppermute(values, "shell", [(i, i ^ 1) for i in range(count)])
+    return lax.ppermute(values, "core", [(0, 1), (1, 0)])
 
 
 def beside(values):
-    count = lax.axis_size("shell")
+    count = lax.axis_size("x") * lax.axis_size("core")
     pairs = [(i, i + 1) for i in range(1, count - 1, 2)]
-    return lax.ppermute(values, "shell", pairs + [(b, a) for a, b in pairs])
+    return lax.ppermute(values, ("x", "core"), pairs + [(b, a) for a, b in pairs])
 
 
 def along(values, step):
-    count = lax.axis_size("shell")
-    return lax.ppermute(values, "shell", [(i, (i + 2 * step) % count) for i in range(count)])
+    count = lax.axis_size("x")
+    return lax.ppermute(values, "x", [(i, (i + step) % count) for i in range(count)])
 
 
 def across(values, start):
@@ -721,7 +733,9 @@
     from_far = along(quotient, 2)
     from_back = along(quotient, 1)
     from_front = along(quotient, 3)
-    gathered = lax.all_to_all(stats, ("pix", "shell"), 0, 0)
+    partner_stats = swap(stats)
+    stats = pair(stats, partner_stats)
+    gathered = lax.all_to_all(stats, ("pix", "x"), 0, 0)
     mine = [quotient, from_front, from_far, from_back]
     theirs = [swap(q) for q in mine]
 
@@ -735,20 +749,23 @@
 
 
 def solution(mesh):
+    grid = mesh.devices.reshape(mesh.devices.shape[0], -1, 2)
+    split_mesh = Mesh(grid, ("pix", "x", "core"))
+    shell = ("x", "core")
     placed = (
-        P("shell", "pix"),
-        P("shell", "pix"),
-        P(None, None, "shell"),
+        P(shell, "pix"),
+        P(shell, "pix"),
+        P(None, None, shell),
         P("pix"),
         P(None, "pix"),
         P("pix"),
         P(),
-        P("shell"),
+        P(shell),
     )
     return jax.shard_map(
         shards,
-        mesh=mesh,
+        mesh=split_mesh,
         in_specs=placed,
-        out_specs=(P("shell", "pix"), P()),
+        out_specs=(P(shell, "pix"), P()),
         check_vma=False,
     )

time: 77.6 us -> 82.2 us (1.059)
  waiting for transfers between devices: 23.7 us -> 27.4 us
  starting transfers between devices: 32.6 us -> 33.7 us
    all_to_all x1, waiting for transfers between devices: 0.14 us -> 5.07 us  [shards(): gathered = lax.all_to_all(stats, ('pix', 'x'), 0, 0)]
    all_to_all x1, starting transfers between devices: 11.5 us -> 13.8 us  [shards(): gathered = lax.all_to_all(stats, ('pix', 'x'), 0, 0)]
    ppermute x13 -> x14, waiting for transfers between devices: 22.7 us -> 21.4 us  [the longest x6 18.3 us: along(): lax.ppermute(values, 'x', [(i, (i + step) % count) for i in range(count)])]
    ppermute x13 -> x14, starting transfers between devices: 19.2 us -> 17.9 us  [the longest x7 8.26 us: swap(): return lax.ppermute(values, 'core', [(0, 1), (1, 0)])]
  transfers between devices with their start and end apart: 16 -> 17, of which waited for: 8 -> 10; matrix products, arithmetic and copies ran while one was open for 0% -> 0% of each run, Pallas kernels for 16% -> 16%
where the time goes in v4:
time: 82.2 us; the launch traced here: 81.9 us
  starting transfers between devices  33.7 us (41%)
  waiting for transfers between devices  27.4 us (33%)
  Pallas kernels  19.9 us (24%)
  between operations  0.95 us (1%)
    ppermute x6, waiting for transfers between devices, along(): lax.ppermute(values, 'x', [(i, (i + step) % count) for i in range(count)])  18.3 us
    all_to_all x1, starting transfers between devices, shards(): gathered = lax.all_to_all(stats, ('pix', 'x'), 0, 0)  13.8 us
    ppermute x7, starting transfers between devices, swap(): return lax.ppermute(values, 'core', [(0, 1), (1, 0)])  8.26 us
    ppermute x6, starting transfers between devices, along(): lax.ppermute(values, 'x', [(i, (i + step) % count) for i in range(count)])  7.78 us
    pallas_call x2, Pallas kernels, gradient(): pl.pallas_call(functools.partial(gradient_body, classes=classes, bins=bin...  5.75 us
    all_to_all x1, waiting for transfers between devices, shards(): gathered = lax.all_to_all(stats, ('pix', 'x'), 0, 0)  5.07 us
    pallas_call x1, Pallas kernels, stencil(): pl.pallas_call(stencil_body, in_specs=[HERE] * 5, out_specs=AWAY, out_sha...  3.53 us
    pallas_call x1, Pallas kernels, project_given(): pl.pallas_call(functools.partial(project_given_body, classes=classes, bin...  3.35 us
  transfers between devices with their start and end apart: 17, of which 10 were waited for; matrix products, arithmetic and copies ran while one was open for 0% of the time, Pallas kernels for 16%

profile of v4, /device:TPU:1, one launch (start us, length us, event | category | flops | bytes accessed | tf_op | source)
XLA Modules:
  0.0 81.9 jit_solution(5125261539575248886)
XLA Ops:
  0.6 3.3 %project_given.1 = (f32[4,40,2048]{2,1,0:T(8,128)S(1)}, f32[4,16,4096]{2,1,0:T(8,128)}, f32[4,16,4096]{2,1,0:T(8,128)S(1)}, f32[4,16,4096]{2,1,0:T(8,128)S(1)}, ...) custom-call(f32[16,32768]{1,0:T(8,128)} %field.1, ...), custom_call_target="tpu_custom_call" | custom-call | tf_op jit(solution)/shard_map/project_given/pallas_call | solution.py:210
  4.0 3.3 %collective-permute-start = (f32[4,40,2048]{2,1,0:T(8,128)S(1)}, f32[4,40,2048]{2,1,0:T(8,128)S(1)}, u32[]{:S(2)}, u32[]{:S(2)}) collective-permute-start(f32[4,40,2048]{2,1,0:T(8,128)S(1)} %get-tuple-element.35), channel_id=1, source_target_pairs={{0,1},{1,0},{2,3},{3,2},{4,5},{5,4},{6,7},{7,6},{8,9},{9,8},{10,11... | collective-permute-start | bytes 3932168 | tf_op jit(solution)/shard_map/ppermute | solution.py:673
  7.3 1.8 %project_kept.1 = (f32[4,40,2048]{2,1,0:T(8,128)S(1)}, f32[4,16,4096]{2,1,0:T(8,128)}, f32[4,16,4096]{2,1,0:T(8,128)S(1)}) custom-call(f32[4,16,4096]{2,1,0:T(8,128)S(1)} %get-tuple-element.30.field, f32[4,16,4096]{2,1,0:T(8,128)S(1)} %get-tuple-element.31.momentum, s32[1,32768]{1,0:T(1,128)S(1)} %get-tuple-element.32.depth.refs_6_, ...), custom_call_target="tpu_custom_call" | custom-call | tf_op jit(solution)/shard_map/project_kept/pallas_call | solution.py:260
  10.2 1.9 %collective-permute-start.2 = (f32[40,2048]{1,0:T(8,128)S(1)}, f32[40,2048]{1,0:T(8,128)S(1)}, u32[]{:S(2)}, u32[]{:S(2)}) collective-permute-start(f32[40,2048]{1,0:T(8,128)S(1)} %get-tuple-element.40), channel_id=1, source_target_pairs={{0,4},{2,6},{4,0},{6,2},{1,5},{3,7},{5,1},{7,3},{8,12},{10,14},{12... | collective-permute-start | bytes 983048 | tf_op jit(solution)/shard_map/ppermute | solution.py:684
  12.2 1.2 %collective-permute-start.3 = (f32[40,2048]{1,0:T(8,128)S(1)}, f32[40,2048]{1,0:T(8,128)S(1)}, u32[]{:S(2)}, u32[]{:S(2)}) collective-permute-start(f32[40,2048]{1,0:T(8,128)S(1)} %get-tuple-element.41), channel_id=1, source_target_pairs={{0,6},{2,0},{4,2},{6,4},{1,7},{3,1},{5,3},{7,5},{8,14},{10,8},{12,... | collective-permute-start | bytes 983048 | tf_op jit(solution)/shard_map/ppermute | solution.py:684
  13.3 1.3 %collective-permute-start.4 = (f32[16,2048]{1,0:T(8,128)S(1)}, f32[16,2048]{1,0:T(8,128)S(1)}, u32[]{:S(2)}, u32[]{:S(2)}) collective-permute-start(f32[16,2048]{1,0:T(8,128)S(1)} %get-tuple-element.44), channel_id=1, source_target_pairs={{0,8},{16,24},{32,40},{48,56},{64,72},{80,88},{96,104},{112,120},{... | collective-permute-start | bytes 393224 | tf_op jit(solution)/shard_map/ppermute | solution.py:689
  15.3 1.2 %prepare.1 = (f32[40,2048]{1,0:T(8,128)S(1)}, bf16[128,144]{1,0:T(8,128)(2,1)S(1)}, f32[16,128]{1,0:T(8,128)S(1)}, f32[1,20]{1,0:T(1,128)S(1)}, f32[64,20]{1,0:T...) custom-call(s32[20,32768]{1,0:T(8,128)} %counts.1, f32[4,16,4096]{2,1,0:T(8,128)S(1)} %get-tuple-element.36.given_place.given, ...), custom_call_target="tpu_custom_call" | custom-call | tf_op jit(solution)/shard_map/prepare/pallas_call | solution.py:360
  17.5 3.5 %stencil.1.later.refs_5_ = f32[16,32768]{1,0:T(8,128)} custom-call(f32[4,16,4096]{2,1,0:T(8,128)S(1)} %get-tuple-element.36.given_place.given, f32[4,16,4096]{2,1,0:T(8,128)S(1)} %get-tuple-element.37.kept_place.kept, f32[16,2048]{1,0:T(8,128)S(1)} %collective-permute-done.4.near, f32[16,2048]{1,0:T(8,128)S(1)} %collective-permute-done.5.beyond, ...), custom_call_target="tpu_custom_call" | custom-call | tf_op jit(solution)/shard_map/stencil/pallas_call | solution.py:426
  21.0 5.6 %collective-permute-done.2.second = f32[40,2048]{1,0:T(8,128)S(1)} collective-permute-done((f32[40,2048]{1,0:T(8,128)S(1)}, f32[40,2048]{1,0:T(8,128)S(1)}, u32[]{:S(2)}, u32[]{:S(2)}) %collective-permute-start.2) | collective-permute-done | bytes 327712 | tf_op jit(solution)/shard_map/ppermute | solution.py:684
  26.7 1.0 %collective-permute-done.3.third = f32[40,2048]{1,0:T(8,128)S(1)} collective-permute-done((f32[40,2048]{1,0:T(8,128)S(1)}, f32[40,2048]{1,0:T(8,128)S(1)}, u32[]{:S(2)}, u32[]{:S(2)}) %collective-permute-start.3) | collective-permute-done | bytes 327712 | tf_op jit(solution)/shard_map/ppermute | solution.py:684
  28.0 1.5 %collective-permute-start.9 = (f32[40,2048]{1,0:T(8,128)S(1)}, f32[40,2048]{1,0:T(8,128)S(1)}, u32[]{:S(2)}, u32[]{:S(2)}) collective-permute-start(f32[40,2048]{1,0:T(8,128)S(1)} %get-tuple-element.50.refs_0_), channel_id=1, source_target_pairs={{0,2},{2,4},{4,6},{6,0},{1,3},{3,5},{5,7},{7,1},{8,10},{10,12},{12... | collective-permute-start | bytes 983048 | tf_op jit(solution)/shard_map/ppermute | solution.py:684
  29.4 3.1 %collective-permute-start.8 = (f32[40,2048]{1,0:T(8,128)S(1)}, f32[40,2048]{1,0:T(8,128)S(1)}, u32[]{:S(2)}, u32[]{:S(2)}) collective-permute-start(f32[40,2048]{1,0:T(8,128)S(1)} %get-tuple-element.50.refs_0_), channel_id=1, source_target_pairs={{0,4},{2,6},{4,0},{6,2},{1,5},{3,7},{5,1},{7,3},{8,12},{10,14},{12... | collective-permute-start | bytes 983048 | tf_op jit(solution)/shard_map/ppermute | solution.py:684
  32.6 1.1 %collective-permute-start.12 = (f32[40,2048]{1,0:T(8,128)S(1)}, f32[40,2048]{1,0:T(8,128)S(1)}, u32[]{:S(2)}, u32[]{:S(2)}) collective-permute-start(f32[40,2048]{1,0:T(8,128)S(1)} %get-tuple-element.50.refs_0_), channel_id=1, source_target_pairs={{0,1},{1,0},{2,3},{3,2},{4,5},{5,4},{6,7},{7,6},{8,9},{9,8},{10,11... | collective-permute-start | bytes 983048 | tf_op jit(solution)/shard_map/ppermute | solution.py:673
  33.6 4.7 %collective-permute-done.9.refs_3_ = f32[40,2048]{1,0:T(8,128)S(1)} collective-permute-done((f32[40,2048]{1,0:T(8,128)S(1)}, f32[40,2048]{1,0:T(8,128)S(1)}, u32[]{:S(2)}, u32[]{:S(2)}) %collective-permute-start.9) | collective-permute-done | bytes 327712 | tf_op jit(solution)/shard_map/ppermute | solution.py:684
  38.4 1.7 %collective-permute-start.15 = (f32[40,2048]{1,0:T(8,128)S(1)}, f32[40,2048]{1,0:T(8,128)}, u32[]{:S(2)}, u32[]{:S(2)}) collective-permute-start(f32[40,2048]{1,0:T(8,128)S(1)} %collective-permute-done.9.refs_3_), channel_id=1, source_target_pairs={{0,1},{1,0},{2,3},{3,2},{4,5},{5,4},{6,7},{7,6},{8,9},{9,8},{10,11... | collective-permute-start | bytes 983048 | tf_op jit(solution)/shard_map/ppermute | solution.py:673
  40.1 6.9 %collective-permute-done.8.refs_2_ = f32[40,2048]{1,0:T(8,128)S(1)} collective-permute-done((f32[40,2048]{1,0:T(8,128)S(1)}, f32[40,2048]{1,0:T(8,128)S(1)}, u32[]{:S(2)}, u32[]{:S(2)}) %collective-permute-start.8) | collective-permute-done | bytes 327712 | tf_op jit(solution)/shard_map/ppermute | solution.py:684
  46.9 1.3 %collective-permute-start.14 = (f32[40,2048]{1,0:T(8,128)S(1)}, f32[40,2048]{1,0:T(8,128)}, u32[]{:S(2)}, u32[]{:S(2)}) collective-permute-start(f32[40,2048]{1,0:T(8,128)S(1)} %collective-permute-done.8.refs_2_), channel_id=1, source_target_pairs={{0,1},{1,0},{2,3},{3,2},{4,5},{5,4},{6,7},{7,6},{8,9},{9,8},{10,11... | collective-permute-start | bytes 983048 | tf_op jit(solution)/shard_map/ppermute | solution.py:673
  48.8 1.4 %collective-permute-done.10.refs_8_ = f32[1,32768]{1,0:T(1,128)S(1)} collective-permute-done((f32[1,32768]{1,0:T(1,128)S(1)}, f32[1,32768]{1,0:T(1,128)S(1)}, u32[]{:S(2)}, u32[]{:S(2)}) %collective-permute-start.10) | collective-permute-done | bytes 131104 | tf_op jit(solution)/shard_map/ppermute | solution.py:673
  51.4 1.9 %collective-permute-start.11 = (f32[1,32768]{1,0:T(1,128)S(1)}, f32[1,32768]{1,0:T(1,128)S(1)}, u32[]{:S(2)}, u32[]{:S(2)}) collective-permute-start(f32[1,32768]{1,0:T(1,128)S(1)} %get-tuple-element.54), channel_id=1, source_target_pairs={{1,2},{3,4},{5,6},{2,1},{4,3},{6,5},{9,10},{11,12},{13,14},{10,9},... | collective-permute-start | bytes 393224 | tf_op jit(solution)/shard_map/ppermute | solution.py:679
  54.0 13.8 %all-to-all-start = ((f32[128,1,128]{2,1,0:T(1,128)}), f32[128,1,128]{2,1,0:T(1,128)S(1)}, u32[]{:S(2)}, u32[]{:S(2)}) async-start(f32[128,1,128]{2,1,0:T(1,128)} %pair.1), calls=%async_computation | async-start | bytes 131072 | tf_op jit(solution)/shard_map/all_to_all | solution.py:738
  67.8 2.3 %gradient_kept.1.kept = f32[4,16,4096]{2,1,0:T(8,128)S(1)} custom-call(f32[40,2048]{1,0:T(8,128)S(1)} %get-tuple-element.50.refs_0_, f32[40,2048]{1,0:T(8,128)S(1)} %collective-permute-done.7.refs_1_, f32[40,2048]{1,0:T(8,128)S(1)} %collective-permute-done.8.refs_2_, f32[40,2048]{1,0:T(8,128)S(1)} %collective-permute-done.9.refs_3_, ...), custom_call_target="tpu_custom_call" | custom-call | tf_op jit(solution)/shard_map/gradient_kept/pallas_call | solution.py:641
  70.1 3.5 %gradient_given.1.given = f32[4,16,4096]{2,1,0:T(8,128)S(1)} custom-call(f32[40,2048]{1,0:T(8,128)S(1)} %collective-permute-done.12.refs_0_, f32[40,2048]{1,0:T(8,128)} %collective-permute-done.13.refs_1_, f32[40,2048]{1,0:T(8,128)} %collective-permute-done.14.refs_2_, f32[40,2048]{1,0:T(8,128)} %collective-permute-done.15.refs_3_, ...), custom_call_target="tpu_custom_call" | custom-call | tf_op jit(solution)/shard_map/gradient_given/pallas_call | solution.py:641
  73.6 5.1 %all-to-all-done.gathered = f32[128,1,128]{2,1,0:T(1,128)S(1)} async-done(((f32[128,1,128]{2,1,0:T(1,128)}), f32[128,1,128]{2,1,0:T(1,128)S(1)}, u32[]{:S(2)}, u32[]{:S(2)}) %all-to-all-start) | async-done | bytes 65568 | tf_op jit(solution)/shard_map/all_to_all | solution.py:738
  78.7 3.1 %finish.1 = (f32[16,32768]{1,0:T(8,128)}, f32[1,1]{1,0:T(1,128)}) custom-call(f32[128,1,128]{2,1,0:T(1,128)S(1)} %all-to-all-done.gathered, f32[1,20]{1,0:T(1,128)S(1)} %get-tuple-element.48.mean, f32[64,20]{1,0:T(8,128)S(1)} %get-tuple-element.49.table, s32[1,32768]{1,0:T(1,128)S(1)} %get-tuple-element.32.depth.refs_6_, ...), custom_call_target="tpu_custom_call" | custom-call | tf_op jit(solution)/shard_map/finish/pallas_call | solution.py:567
  (26 shorter events, 5.5 us)
Async XLA Ops:
  4.0 6.0 %collective-permute-start = (f32[4,40,2048]{2,1,0:T(8,128)S(1)}, f32[4,40,2048]{2,1,0:T(8,128)S(1)}, u32[]{:S(2)}, u32[]{:S(2)}) collective-permute-start(f32[4,40,2048]{2,1,0:T(8,128)S(1)} %get-tuple-element.35), channel_id=1, source_target_pairs={{0,1},{1,0},{2,3},{3,2},{4,5},{5,4},{6,7},{7,6},{8,9},{9,8},{10,11... | collective-permute-start | bytes 3932168 | tf_op jit(solution)/shard_map/ppermute | solution.py:673
  9.9 5.4 %copy-start = (f32[4,20,16]{1,2,0:T(8,128)S(1)}, f32[4,20,16]{1,2,0:T(8,128)}, u32[]{:S(2)}) copy-start(f32[4,20,16]{1,2,0:T(8,128)} %param.10) | copy-start | bytes 15364
  9.9 5.4 %copy-start.1 = (f32[16]{0:T(128)S(1)}, f32[16]{0:T(128)}, u32[]{:S(2)}) copy-start(f32[16]{0:T(128)} %param.15) | copy-start | bytes 196
  9.9 5.4 %copy-start.2 = (f32[20]{0:T(128)S(1)}, f32[20]{0:T(128)}, u32[]{:S(2)}) copy-start(f32[20]{0:T(128)} %param.14) | copy-start | bytes 244
  10.1 10.9 %collective-permute-start.1 = (f32[40,2048]{1,0:T(8,128)S(1)}, f32[40,2048]{1,0:T(8,128)S(1)}, u32[]{:S(2)}, u32[]{:S(2)}) collective-permute-start(f32[40,2048]{1,0:T(8,128)S(1)} %get-tuple-element.39), channel_id=1, source_target_pairs={{0,2},{2,4},{4,6},{6,0},{1,3},{3,5},{5,7},{7,1},{8,10},{10,12},{12... | collective-permute-start | bytes 983048 | tf_op jit(solution)/shard_map/ppermute | solution.py:684
  10.2 16.4 %collective-permute-start.2 = (f32[40,2048]{1,0:T(8,128)S(1)}, f32[40,2048]{1,0:T(8,128)S(1)}, u32[]{:S(2)}, u32[]{:S(2)}) collective-permute-start(f32[40,2048]{1,0:T(8,128)S(1)} %get-tuple-element.40), channel_id=1, source_target_pairs={{0,4},{2,6},{4,0},{6,2},{1,5},{3,7},{5,1},{7,3},{8,12},{10,14},{12... | collective-permute-start | bytes 983048 | tf_op jit(solution)/shard_map/ppermute | solution.py:684
  12.2 15.5 %collective-permute-start.3 = (f32[40,2048]{1,0:T(8,128)S(1)}, f32[40,2048]{1,0:T(8,128)S(1)}, u32[]{:S(2)}, u32[]{:S(2)}) collective-permute-start(f32[40,2048]{1,0:T(8,128)S(1)} %get-tuple-element.41), channel_id=1, source_target_pairs={{0,6},{2,0},{4,2},{6,4},{1,7},{3,1},{5,3},{7,5},{8,14},{10,8},{12,... | collective-permute-start | bytes 983048 | tf_op jit(solution)/shard_map/ppermute | solution.py:684
  13.3 4.1 %collective-permute-start.4 = (f32[16,2048]{1,0:T(8,128)S(1)}, f32[16,2048]{1,0:T(8,128)S(1)}, u32[]{:S(2)}, u32[]{:S(2)}) collective-permute-start(f32[16,2048]{1,0:T(8,128)S(1)} %get-tuple-element.44), channel_id=1, source_target_pairs={{0,8},{16,24},{32,40},{48,56},{64,72},{80,88},{96,104},{112,120},{... | collective-permute-start | bytes 393224 | tf_op jit(solution)/shard_map/ppermute | solution.py:689
  14.6 2.8 %collective-permute-start.5 = (f32[16,2048]{1,0:T(8,128)S(1)}, f32[16,2048]{1,0:T(8,128)S(1)}, u32[]{:S(2)}, u32[]{:S(2)}) collective-permute-start(f32[16,2048]{1,0:T(8,128)S(1)} %get-tuple-element.45), channel_id=1, source_target_pairs={{8,16},{24,32},{40,48},{56,64},{72,80},{88,96},{104,112},{120,128}... | collective-permute-start | bytes 393224 | tf_op jit(solution)/shard_map/ppermute | solution.py:689
  28.0 10.4 %collective-permute-start.9 = (f32[40,2048]{1,0:T(8,128)S(1)}, f32[40,2048]{1,0:T(8,128)S(1)}, u32[]{:S(2)}, u32[]{:S(2)}) collective-permute-start(f32[40,2048]{1,0:T(8,128)S(1)} %get-tuple-element.50.refs_0_), channel_id=1, source_target_pairs={{0,2},{2,4},{4,6},{6,0},{1,3},{3,5},{5,7},{7,1},{8,10},{10,12},{12... | collective-permute-start | bytes 983048 | tf_op jit(solution)/shard_map/ppermute | solution.py:684
  29.4 17.5 %collective-permute-start.8 = (f32[40,2048]{1,0:T(8,128)S(1)}, f32[40,2048]{1,0:T(8,128)S(1)}, u32[]{:S(2)}, u32[]{:S(2)}) collective-permute-start(f32[40,2048]{1,0:T(8,128)S(1)} %get-tuple-element.50.refs_0_), channel_id=1, source_target_pairs={{0,4},{2,6},{4,0},{6,2},{1,5},{3,7},{5,1},{7,3},{8,12},{10,14},{12... | collective-permute-start | bytes 983048 | tf_op jit(solution)/shard_map/ppermute | solution.py:684
  32.6 15.7 %collective-permute-start.7 = (f32[40,2048]{1,0:T(8,128)S(1)}, f32[40,2048]{1,0:T(8,128)S(1)}, u32[]{:S(2)}, u32[]{:S(2)}) collective-permute-start(f32[40,2048]{1,0:T(8,128)S(1)} %get-tuple-element.50.refs_0_), channel_id=1, source_target_pairs={{0,6},{2,0},{4,2},{6,4},{1,7},{3,1},{5,3},{7,5},{8,14},{10,8},{12,... | collective-permute-start | bytes 983048 | tf_op jit(solution)/shard_map/ppermute | solution.py:684
  32.6 37.5 %collective-permute-start.12 = (f32[40,2048]{1,0:T(8,128)S(1)}, f32[40,2048]{1,0:T(8,128)S(1)}, u32[]{:S(2)}, u32[]{:S(2)}) collective-permute-start(f32[40,2048]{1,0:T(8,128)S(1)} %get-tuple-element.50.refs_0_), channel_id=1, source_target_pairs={{0,1},{1,0},{2,3},{3,2},{4,5},{5,4},{6,7},{7,6},{8,9},{9,8},{10,11... | collective-permute-start | bytes 983048 | tf_op jit(solution)/shard_map/ppermute | solution.py:673
  38.4 31.7 %collective-permute-start.15 = (f32[40,2048]{1,0:T(8,128)S(1)}, f32[40,2048]{1,0:T(8,128)}, u32[]{:S(2)}, u32[]{:S(2)}) collective-permute-start(f32[40,2048]{1,0:T(8,128)S(1)} %collective-permute-done.9.refs_3_), channel_id=1, source_target_pairs={{0,1},{1,0},{2,3},{3,2},{4,5},{5,4},{6,7},{7,6},{8,9},{9,8},{10,11... | collective-permute-start | bytes 983048 | tf_op jit(solution)/shard_map/ppermute | solution.py:673
  46.9 23.2 %collective-permute-start.14 = (f32[40,2048]{1,0:T(8,128)S(1)}, f32[40,2048]{1,0:T(8,128)}, u32[]{:S(2)}, u32[]{:S(2)}) collective-permute-start(f32[40,2048]{1,0:T(8,128)S(1)} %collective-permute-done.8.refs_2_), channel_id=1, source_target_pairs={{0,1},{1,0},{2,3},{3,2},{4,5},{5,4},{6,7},{7,6},{8,9},{9,8},{10,11... | collective-permute-start | bytes 983048 | tf_op jit(solution)/shard_map/ppermute | solution.py:673
  48.3 21.9 %collective-permute-start.13 = (f32[40,2048]{1,0:T(8,128)S(1)}, f32[40,2048]{1,0:T(8,128)}, u32[]{:S(2)}, u32[]{:S(2)}) collective-permute-start(f32[40,2048]{1,0:T(8,128)S(1)} %collective-permute-done.7.refs_1_), channel_id=1, source_target_pairs={{0,1},{1,0},{2,3},{3,2},{4,5},{5,4},{6,7},{7,6},{8,9},{9,8},{10,11... | collective-permute-start | bytes 983048 | tf_op jit(solution)/shard_map/ppermute | solution.py:673
  48.3 1.9 %collective-permute-start.10 = (f32[1,32768]{1,0:T(1,128)S(1)}, f32[1,32768]{1,0:T(1,128)S(1)}, u32[]{:S(2)}, u32[]{:S(2)}) collective-permute-start(f32[1,32768]{1,0:T(1,128)S(1)} %get-tuple-element.53), channel_id=1, source_target_pairs={{0,1},{1,0},{2,3},{3,2},{4,5},{5,4},{6,7},{7,6},{8,9},{9,8},{10,11... | collective-permute-start | bytes 393224 | tf_op jit(solution)/shard_map/ppermute | solution.py:673
  50.2 1.2 %collective-permute-start.6 = (f32[1,128]{1,0:T(1,128)S(1)}, f32[1,128]{1,0:T(1,128)S(1)}, u32[]{:S(2)}, u32[]{:S(2)}) collective-permute-start(f32[1,128]{1,0:T(1,128)S(1)} %get-tuple-element.47.mine), channel_id=1, source_target_pairs={{0,1},{1,0},{2,3},{3,2},{4,5},{5,4},{6,7},{7,6},{8,9},{9,8},{10,11... | collective-permute-start | bytes 1544 | tf_op jit(solution)/shard_map/ppermute | solution.py:673
  51.4 16.4 %collective-permute-start.11 = (f32[1,32768]{1,0:T(1,128)S(1)}, f32[1,32768]{1,0:T(1,128)S(1)}, u32[]{:S(2)}, u32[]{:S(2)}) collective-permute-start(f32[1,32768]{1,0:T(1,128)S(1)} %get-tuple-element.54), channel_id=1, source_target_pairs={{1,2},{3,4},{5,6},{2,1},{4,3},{6,5},{9,10},{11,12},{13,14},{10,9},... | collective-permute-start | bytes 393224 | tf_op jit(solution)/shard_map/ppermute | solution.py:679
  54.0 24.7 %all-to-all-start = ((f32[128,1,128]{2,1,0:T(1,128)}), f32[128,1,128]{2,1,0:T(1,128)S(1)}, u32[]{:S(2)}, u32[]{:S(2)}) async-start(f32[128,1,128]{2,1,0:T(1,128)} %pair.1), calls=%async_computation | async-start | bytes 131072 | tf_op jit(solution)/shard_map/all_to_all | solution.py:738

commit v5 on v4

--- a/solution.py
+++ b/solution.py
@@ -99,10 +99,13 @@
         picked = every[: 2 * bins]
         for k in range(1, classes):
             picked = jnp.where(chosen == k, every[2 * bins * k : 2 * bins * (k + 1)], picked)
-        proj[d, :, start : start + WIDE] = picked
-
-
-def project_given_body(
+        proj[:, start : start + WIDE] = picked
+
+
+FAR, REST = 2, (0, 1, 3)
+
+
+def load_body(
     field,
     momentum,
     depth,
@@ -111,13 +114,13 @@
     proj,
     density,
     position,
+    field_given,
+    momentum_given,
     field_kept,
     momentum_kept,
     depth_here,
     mask_here,
     weights,
-    field_given,
-    momentum_given,
     stage,
     table,
     marks,
@@ -126,12 +129,11 @@
 ):
     _, shells, width = field_given.shape
     chip, core = position_of()
-    copies = [
+    small = [
+        pltpu.make_async_copy(table_away, table, marks.at[18]),
         pltpu.make_async_copy(depth, depth_here, marks.at[16]),
         pltpu.make_async_copy(mask, mask_here, marks.at[17]),
     ]
-    load_table = pltpu.make_async_copy(table_away, table, marks.at[18])
-    load_table.start()
 
     def fetch(half, d, source, target, mark):
         begin = offset_of(half, d, chip, width)
@@ -139,39 +141,37 @@
             source.at[:, pl.ds(begin, width)], target.at[d], marks.at[mark]
         )
 
-    for d in range(4):
-        copies.append(fetch(1 - core, d, field, field_given, 2 * d))
-        copies.append(fetch(1 - core, d, momentum, momentum_given, 2 * d + 1))
-    for d in range(4):
-        copies.append(fetch(core, d, field, field_kept, 8 + 2 * d))
-        copies.append(fetch(core, d, momentum, momentum_kept, 9 + 2 * d))
-    for copy in copies:
+    first, later = [], []
+    for d in (FAR, *REST):
+        group = first if d == FAR else later
+        group.append(fetch(1 - core, d, field, field_given, 2 * d))
+        group.append(fetch(1 - core, d, momentum, momentum_given, 2 * d + 1))
+    for d in (FAR, *REST):
+        later.append(fetch(core, d, field, field_kept, 8 + 2 * d))
+        later.append(fetch(core, d, momentum, momentum_kept, 9 + 2 * d))
+    for copy in small[:2] + first + later + small[2:]:
         copy.start()
-    load_table.wait()
+    small[0].wait()
     weights[...] = forward_weights(table[...], classes, bins, shells)
-    copies[0].wait()
-    copies[1].wait()
-    for d in range(4):
-        copies[2 + 2 * d].wait()
-        copies[3 + 2 * d].wait()
-        project_piece(
-            d,
-            offset_of(1 - core, d, chip, width),
-            field_given,
-            momentum_given,
-            depth_here,
-            weights,
-            proj,
-            stage,
-            position,
-            classes,
-            bins,
-        )
-        copies.append(
-            pltpu.make_async_copy(stage.at[d], density.at[d], marks.at[19 + d])
-        )
-        copies[-1].start()
-    for copy in copies[10:]:
+    small[1].wait()
+    for copy in first:
+        copy.wait()
+    project_piece(
+        FAR,
+        offset_of(1 - core, FAR, chip, width),
+        field_given,
+        momentum_given,
+        depth_here,
+        weights,
+        proj,
+        stage,
+        position,
+        classes,
+        bins,
+    )
+    out = pltpu.make_async_copy(stage.at[FAR], density.at[FAR], marks.at[19])
+    out.start()
+    for copy in later + small[2:] + [out]:
         copy.wait()
 
 
@@ -194,12 +194,14 @@
     return pltpu.VMEM(shape, dtype)
 
 
-def project_given(field, momentum, depth, mask, table, classes, bins):
+def load(field, momentum, depth, mask, table, classes, bins):
     shells, pixels = field.shape
     width = pixels // 8
     outs = [
-        vmem(4, 2 * bins, width // 2),
+        vmem(2 * bins, width // 2),
         pltpu.HBM((4, shells, width), jnp.float32),
+        vmem(4, shells, width),
+        vmem(4, shells, width),
         vmem(4, shells, width),
         vmem(4, shells, width),
         vmem(4, shells, width),
@@ -208,69 +210,138 @@
         vmem(classes * 2 * bins, 6 * shells, dtype=jnp.bfloat16),
     ]
     return pl.pallas_call(
-        functools.partial(project_given_body, classes=classes, bins=bins),
+        functools.partial(load_body, classes=classes, bins=bins),
         in_specs=[AWAY] * 5,
         out_specs=[HERE, AWAY] + [HERE] * (len(outs) - 2),
         out_shape=outs,
         scratch_shapes=[
             vmem(4, shells, width),
-            vmem(4, shells, width),
-            vmem(4, shells, width),
             vmem(*table.shape),
-            pltpu.SemaphoreType.DMA((23,)),
-        ],
-        compiler_params=LIMIT,
-        name="project_given",
+            pltpu.SemaphoreType.DMA((20,)),
+        ],
+        compiler_params=LIMIT,
+        name="load",
     )(*in_hbm(field, momentum, depth, mask, table))
 
 
-def project_kept_body(
-    field, momentum, depth, weights, proj, density, position, stage, marks, classes, bins
+def project_rest_body(
+    field,
+    momentum,
+    depth,
+    weights,
+    density_before,
+    position_before,
+    proj,
+    density,
+    position,
+    stage,
+    marks,
+    mine,
+    classes,
+    bins,
 ):
     width = field.shape[2]
     chip, core = position_of()
+    half = core if mine else 1 - core
     copies = []
-    for d in range(4):
+    for k, d in enumerate(REST):
         project_piece(
             d,
-            offset_of(core, d, chip, width),
+            offset_of(half, d, chip, width),
             field,
             momentum,
             depth,
             weights,
-            proj,
+            proj.at[k],
             stage,
             position,
             classes,
             bins,
         )
-        copies.append(pltpu.make_async_copy(stage.at[d], density.at[d], marks.at[d]))
+        copies.append(pltpu.make_async_copy(stage.at[d], density.at[d], marks.at[k]))
         copies[-1].start()
     for copy in copies:
         copy.wait()
 
 
-def project_kept(field, momentum, depth, weights, classes, bins):
+def project_rest(field, momentum, depth, weights, density, position, mine, classes, bins):
     _, shells, width = field.shape
-    outs = [
-        vmem(4, 2 * bins, width // 2),
-        pltpu.HBM((4, shells, width), jnp.float32),
-        vmem(4, shells, width),
-    ]
-    return pl.pallas_call(
-        functools.partial(project_kept_body, classes=classes, bins=bins),
-        in_specs=[HERE] * 4,
+    return pl.pallas_call(
+        functools.partial(project_rest_body, mine=mine, classes=classes, bins=bins),
+        in_specs=[HERE] * 4 + [AWAY, HERE],
         out_specs=[HERE, AWAY, HERE],
-        out_shape=outs,
-        scratch_shapes=[vmem(4, shells, width), pltpu.SemaphoreType.DMA((4,))],
-        compiler_params=LIMIT,
-        name="project_kept",
-    )(*in_vmem(field, momentum, depth, weights))
-
-
-def combine_body(kept, partner, given_place, kept_place, own, first, second, third, near, beyond):
+        out_shape=[
+            vmem(len(REST), 2 * bins, width // 2),
+            pltpu.HBM((4, shells, width), jnp.float32),
+            vmem(4, shells, width),
+        ],
+        scratch_shapes=[vmem(4, shells, width), pltpu.SemaphoreType.DMA((len(REST),))],
+        input_output_aliases={4: 1, 5: 2},
+        compiler_params=LIMIT,
+        name="rest_kept" if mine else "rest_given",
+    )(*in_vmem(field, momentum, depth, weights), *in_hbm(density), *in_vmem(position))
+
+
+def project_far_body(
+    field,
+    momentum,
+    depth,
+    weights,
+    partner,
+    total,
+    density,
+    position,
+    stage,
+    proj,
+    mark,
+    classes,
+    bins,
+):
+    width = field.shape[2]
     chip, core = position_of()
-    for d, out in enumerate((own, first, second, third)):
+    project_piece(
+        FAR,
+        offset_of(core, FAR, chip, width),
+        field,
+        momentum,
+        depth,
+        weights,
+        proj,
+        stage,
+        position,
+        classes,
+        bins,
+    )
+    copy = pltpu.make_async_copy(stage.at[FAR], density.at[FAR], mark)
+    copy.start()
+    total[...] = proj[...] + partner[...]
+    copy.wait()
+
+
+def project_far(field, momentum, depth, weights, partner, classes, bins):
+    _, shells, width = field.shape
+    return pl.pallas_call(
+        functools.partial(project_far_body, classes=classes, bins=bins),
+        in_specs=[HERE] * 5,
+        out_specs=[HERE, AWAY, HERE],
+        out_shape=[
+            vmem(*partner.shape),
+            pltpu.HBM((4, shells, width), jnp.float32),
+            vmem(4, shells, width),
+        ],
+        scratch_shapes=[
+            vmem(4, shells, width),
+            vmem(*partner.shape),
+            pltpu.SemaphoreType.DMA,
+        ],
+        compiler_params=LIMIT,
+        name="far_kept",
+    )(*in_vmem(field, momentum, depth, weights, partner))
+
+
+def combine_body(kept, partner, given_place, kept_place, own, first, third, near, beyond):
+    chip, core = position_of()
+    for d, out in enumerate((own, first, third)):
         out[...] = kept[d] + partner[d]
     front, back = (4 - chip) % 4, (7 - chip) % 4
     edge = given_place.shape[2] - CYCLE
@@ -288,11 +359,11 @@
 def combine(kept, partner, given_place, kept_place):
     _, rows, sub = kept.shape
     shells = given_place.shape[1]
-    outs = [vmem(rows, sub)] * 4 + [vmem(shells, CYCLE)] * 2
+    outs = [vmem(rows, sub)] * 3 + [vmem(shells, CYCLE)] * 2
     return pl.pallas_call(
         combine_body,
         in_specs=[HERE] * 4,
-        out_specs=[HERE] * 6,
+        out_specs=[HERE] * 5,
         out_shape=outs,
         compiler_params=LIMIT,
         name="combine",
@@ -584,24 +655,35 @@
 
 def gradient_body(*refs, classes, bins, mine):
     quotients, refs = refs[:4], refs[4:]
-    density_away, rest_away, depth, weights, partner, side = refs[:6]
-    out, density, rest, marks = refs[6:]
+    if mine:
+        density_away, rest_away, density_next, depth, weights, partner, side = refs[:7]
+        out, density_there, rest_there, density, rest, marks = refs[7:]
+    else:
+        density, rest, depth, weights, partner, side, out = refs
     _, shells, width = out.shape
     sub = width // 2
     chip, core = position_of()
     half = core if mine else 1 - core
-    loads = []
-    for d in range(4):
-        base = offset_of(half, d, chip, width)
-        loads.append(
-            (
+    loads = [()] * 4
+    later = []
+    if mine:
+
+        def fetch(half, d, source, target, mark):
+            base = offset_of(half, d, chip, width)
+            return pltpu.make_async_copy(
+                source.at[:, pl.ds(base, width)], target.at[d], marks.at[mark]
+            )
+
+        for d in range(4):
+            loads[d] = (
                 pltpu.make_async_copy(density_away.at[d], density.at[d], marks.at[d]),
-                pltpu.make_async_copy(
-                    rest_away.at[:, pl.ds(base, width)], rest.at[d], marks.at[4 + d]
-                ),
+                fetch(half, d, rest_away, rest, 4 + d),
             )
-        )
-        for load in loads[-1]:
+            later.append(
+                pltpu.make_async_copy(density_next.at[d], density_there.at[d], marks.at[8 + d])
+            )
+            later.append(fetch(1 - half, d, rest_away, rest_there, 12 + d))
+        for load in [load for pair in loads for load in pair] + later:
             load.start()
     row = iota((shells, WIDE), 0)
     beside_partner = (row == 0) & (core == 1) | (row == shells - 1) & (core == 0)
@@ -631,26 +713,36 @@
                 near = jnp.where(beside_partner, partner[:, away], 0.0)
                 near = jnp.where(outside, side[:, away], near)
                 out[d, :, here] = density[d, :, here] * back + (rest[d, :, here] + RADIAL * near)
-
-
-def gradient(quotients, density, rest, depth, weights, partner, side, classes, bins, mine):
-    shells, pixels = rest.shape
-    width = pixels // 8
-    operands = in_vmem(*quotients) + in_hbm(density, rest)
-    operands += in_vmem(depth, weights, partner, side)
-    return pl.pallas_call(
-        functools.partial(gradient_body, classes=classes, bins=bins, mine=mine),
-        in_specs=[HERE] * 4 + [AWAY] * 2 + [HERE] * 4,
-        out_specs=HERE,
-        out_shape=vmem(4, shells, width),
+    for load in later:
+        load.wait()
+
+
+def gradient_kept(quotients, density, rest, next_density, common, classes, bins):
+    _, shells, width = density.shape
+    return pl.pallas_call(
+        functools.partial(gradient_body, classes=classes, bins=bins, mine=True),
+        in_specs=[HERE] * 4 + [AWAY] * 3 + [HERE] * 4,
+        out_specs=[HERE] * 3,
+        out_shape=[vmem(4, shells, width)] * 3,
         scratch_shapes=[
             vmem(4, shells, width),
             vmem(4, shells, width),
-            pltpu.SemaphoreType.DMA((8,)),
-        ],
-        compiler_params=LIMIT,
-        name="gradient_kept" if mine else "gradient_given",
-    )(*operands)
+            pltpu.SemaphoreType.DMA((16,)),
+        ],
+        compiler_params=LIMIT,
+        name="gradient_kept",
+    )(*in_vmem(*quotients), *in_hbm(density, rest, next_density), *in_vmem(*common))
+
+
+def gradient_given(quotients, density, rest, common, classes, bins):
+    return pl.pallas_call(
+        functools.partial(gradient_body, classes=classes, bins=bins, mine=False),
+        in_specs=[HERE] * 10,
+        out_specs=HERE,
+        out_shape=vmem(*density.shape),
+        compiler_params=LIMIT,
+        name="gradient_given",
+    )(*in_vmem(*quotients, density, rest, *common))
 
 
 def pair_body(mine, partner, out):
@@ -695,7 +787,7 @@
     total_pix = pixels * lax.axis_size("pix")
     table = jnp.transpose(kernels, (0, 2, 1)).reshape(classes * shells, bins)
 
-    given = project_given(
+    loaded = load(
         field,
         momentum,
         depth_class.reshape(1, pixels),
@@ -704,15 +796,29 @@
         classes,
         bins,
     )
-    proj, density_given, place_given, field_kept, momentum_kept, depth, cover, weights = given
-    proj_partner = swap(proj)
-    proj_kept, density_kept, place_kept = project_kept(
-        field_kept, momentum_kept, depth, weights, classes, bins
-    )
-    own, first, second, third, near, beyond = combine(
-        proj_kept, proj_partner, place_given, place_kept
+    proj, density_given, place_given, field_given, momentum_given = loaded[:5]
+    field_kept, momentum_kept, depth, cover, weights = loaded[5:]
+    partner_far = swap(proj)
+    proj, density_given, place_given = project_rest(
+        field_given,
+        momentum_given,
+        depth,
+        weights,
+        density_given,
+        place_given,
+        False,
+        classes,
+        bins,
+    )
+    partner = swap(proj)
+    second, density_kept, place_kept = project_far(
+        field_kept, momentum_kept, depth, weights, partner_far, classes, bins
     )
     second = along(second, 2)
+    proj, density_kept, place_kept = project_rest(
+        field_kept, momentum_kept, depth, weights, density_kept, place_kept, True, classes, bins
+    )
+    own, first, third, near, beyond = combine(proj, partner, place_given, place_kept)
     first = along(first, 1)
     third = along(third, 3)
     near = across(near, 0)
@@ -739,9 +845,11 @@
     mine = [quotient, from_front, from_far, from_back]
     theirs = [swap(q) for q in mine]
 
-    common = (rest, depth, weights, partner_row, side_row, classes, bins)
-    kept = gradient(mine, density_kept, *common, True)
-    given = gradient(theirs, density_given, *common, False)
+    common = (depth, weights, partner_row, side_row)
+    kept, density_there, rest_there = gradient_kept(
+        mine, density_kept, rest, density_given, common, classes, bins
+    )
+    given = gradient_given(theirs, density_there, rest_there, common, classes, bins)
     out, loglik = finish(
         gathered, mean, table, depth, cover, kept, given, density_kept, density_given, total_pix
     )

time: 82.2 us -> 84.2 us (1.024)
  the two profiles are of different devices: /device:TPU:1 before, /device:TPU:8 now
where the time goes in v5:
time: 84.2 us; the launch traced here: 82.5 us
  starting transfers between devices  34.6 us (41%)
  waiting for transfers between devices  27.2 us (32%)
  Pallas kernels  19.6 us (23%)
  between operations  1.03 us (1%)
    all_to_all x1, starting transfers between devices, shards(): gathered = lax.all_to_all(stats, ('pix', 'x'), 0, 0)  16.8 us
    ppermute x6, waiting for transfers between devices, along(): lax.ppermute(values, 'x', [(i, (i + step) % count) for i in range(count)])  13.2 us
    ppermute x6, starting transfers between devices, along(): lax.ppermute(values, 'x', [(i, (i + step) % count) for i in range(count)])  11.1 us
    all_to_all x1, waiting for transfers between devices, shards(): gathered = lax.all_to_all(stats, ('pix', 'x'), 0, 0)  7.06 us
    ppermute x8, waiting for transfers between devices, swap(): return lax.ppermute(values, 'core', [(0, 1), (1, 0)])  5.33 us
    ppermute x2, starting transfers between devices, across(): return lax.ppermute(values, 'pix', pairs + [(b, a) for a, b in pairs])  4.76 us
    pallas_call x1, Pallas kernels, stencil(): pl.pallas_call(stencil_body, in_specs=[HERE] * 5, out_specs=AWAY, out_sha...  3.53 us
    pallas_call x1, Pallas kernels, finish(): pl.pallas_call(functools.partial(finish_body, classes=classes, bins=bins,...  3.11 us
  transfers between devices with their start and end apart: 18, of which 7 were waited for; matrix products, arithmetic and copies ran while one was open for 0% of the time, Pallas kernels for 15%

profile of v5, /device:TPU:8, one launch (start us, length us, event | category | flops | bytes accessed | tf_op | source)
XLA Modules:
  0.0 82.5 jit_solution(12214907796394378412)
XLA Ops:
  0.6 2.4 %load.1 = (f32[40,2048]{1,0:T(8,128)S(1)}, f32[4,16,4096]{2,1,0:T(8,128)}, f32[4,16,4096]{2,1,0:T(8,128)S(1)}, f32[4,16,4096]{2,1,0:T(8,128)S(1)}, f32[4,16,4096...) custom-call(f32[16,32768]{1,0:T(8,128)} %field.1, ...), custom_call_target="tpu_custom_call" | custom-call | tf_op jit(solution)/shard_map/load/pallas_call | solution.py:212
  3.1 1.5 %rest_given.1 = (f32[3,40,2048]{2,1,0:T(8,128)S(1)}, f32[4,16,4096]{2,1,0:T(8,128)}, f32[4,16,4096]{2,1,0:T(8,128)S(1)}) custom-call(f32[4,16,4096]{2,1,0:T(8,128)S(1)} %get-tuple-element.48.field, f32[4,16,4096]{2,1,0:T(8,128)S(1)} %get-tuple-element.49.momentum, ...), custom_call_target="tpu_custom_call", output_to_operand_aliasing={{1}: (4, {}), {2}: (5, {})} | custom-call | tf_op jit(solution)/shard_map/rest_given/pallas_call | solution.py:269
  5.2 2.5 %collective-permute-done.partner = f32[40,2048]{1,0:T(8,128)S(1)} collective-permute-done((f32[40,2048]{1,0:T(8,128)S(1)}, f32[40,2048]{1,0:T(8,128)S(1)}, u32[]{:S(2)}, u32[]{:S(2)}) %collective-permute-start) | collective-permute-done | bytes 327712 | tf_op jit(solution)/shard_map/ppermute | solution.py:765
  7.7 0.9 %far_kept.1 = (f32[40,2048]{1,0:T(8,128)S(1)}, f32[4,16,4096]{2,1,0:T(8,128)}, f32[4,16,4096]{2,1,0:T(8,128)S(1)}) custom-call(f32[4,16,4096]{2,1,0:T(8,128)S(1)} %get-tuple-element.40.field, f32[4,16,4096]{2,1,0:T(8,128)S(1)} %get-tuple-element.41.momentum, s32[1,32768]{1,0:T(1,128)S(1)} %get-tuple-element.42.depth.refs_7_.refs_6_, ...), custom_call_target="tpu_custom_call" | custom-call | tf_op jit(solution)/shard_map/far_kept/pallas_call | solution.py:323
  8.6 3.1 %collective-permute-start.3 = (f32[40,2048]{1,0:T(8,128)S(1)}, f32[40,2048]{1,0:T(8,128)S(1)}, u32[]{:S(2)}, u32[]{:S(2)}) collective-permute-start(f32[40,2048]{1,0:T(8,128)S(1)} %get-tuple-element.57), channel_id=1, source_target_pairs={{0,4},{2,6},{4,0},{6,2},{1,5},{3,7},{5,1},{7,3},{8,12},{10,14},{12... | collective-permute-start | bytes 983048 | tf_op jit(solution)/shard_map/ppermute | solution.py:776
  11.7 1.5 %rest_kept.1 = (f32[3,40,2048]{2,1,0:T(8,128)S(1)}, f32[4,16,4096]{2,1,0:T(8,128)}, f32[4,16,4096]{2,1,0:T(8,128)S(1)}) custom-call(f32[4,16,4096]{2,1,0:T(8,128)S(1)} %get-tuple-element.40.field, f32[4,16,4096]{2,1,0:T(8,128)S(1)} %get-tuple-element.41.momentum, ...), custom_call_target="tpu_custom_call", output_to_operand_aliasing={{1}: (4, {}), {2}: (5, {})} | custom-call | tf_op jit(solution)/shard_map/rest_kept/pallas_call | solution.py:269
  13.4 0.7 collective-permute-start.2
  14.1 2.6 %collective-permute-start.4 = (f32[40,2048]{1,0:T(8,128)S(1)}, f32[40,2048]{1,0:T(8,128)S(1)}, u32[]{:S(2)}, u32[]{:S(2)}) collective-permute-start(f32[40,2048]{1,0:T(8,128)S(1)} %get-tuple-element.58), channel_id=1, source_target_pairs={{0,6},{2,0},{4,2},{6,4},{1,7},{3,1},{5,3},{7,5},{8,14},{10,8},{12,... | collective-permute-start | bytes 983048 | tf_op jit(solution)/shard_map/ppermute | solution.py:776
  17.2 4.3 %collective-permute-start.6 = (f32[16,2048]{1,0:T(8,128)S(1)}, f32[16,2048]{1,0:T(8,128)S(1)}, u32[]{:S(2)}, u32[]{:S(2)}) collective-permute-start(f32[16,2048]{1,0:T(8,128)S(1)} %get-tuple-element.62), channel_id=1, source_target_pairs={{8,16},{24,32},{40,48},{56,64},{72,80},{88,96},{104,112},{120,128}... | collective-permute-start | bytes 393224 | tf_op jit(solution)/shard_map/ppermute | solution.py:781
  21.5 1.2 %prepare.1 = (f32[40,2048]{1,0:T(8,128)S(1)}, bf16[128,144]{1,0:T(8,128)(2,1)S(1)}, f32[16,128]{1,0:T(8,128)S(1)}, f32[1,20]{1,0:T(1,128)S(1)}, f32[64,20]{1,0:T...) custom-call(s32[20,32768]{1,0:T(8,128)} %counts.1, f32[4,16,4096]{2,1,0:T(8,128)S(1)} %get-tuple-element.53.given_place.given, ...), custom_call_target="tpu_custom_call" | custom-call | tf_op jit(solution)/shard_map/prepare/pallas_call | solution.py:431
  22.8 1.7 %collective-permute-done.6.beyond = f32[16,2048]{1,0:T(8,128)S(1)} collective-permute-done((f32[16,2048]{1,0:T(8,128)S(1)}, f32[16,2048]{1,0:T(8,128)S(1)}, u32[]{:S(2)}, u32[]{:S(2)}) %collective-permute-start.6) | collective-permute-done | bytes 131104 | tf_op jit(solution)/shard_map/ppermute | solution.py:781
  24.4 3.5 %stencil.1.later.refs_5_ = f32[16,32768]{1,0:T(8,128)} custom-call(f32[4,16,4096]{2,1,0:T(8,128)S(1)} %get-tuple-element.53.given_place.given, f32[4,16,4096]{2,1,0:T(8,128)S(1)} %get-tuple-element.54.kept_place.kept, f32[16,2048]{1,0:T(8,128)S(1)} %collective-permute-done.5.near, f32[16,2048]{1,0:T(8,128)S(1)} %collective-permute-done.6.beyond, ...), custom_call_target="tpu_custom_call" | custom-call | tf_op jit(solution)/shard_map/stencil/pallas_call | solution.py:497
  28.9 2.7 %collective-permute-start.9 = (f32[40,2048]{1,0:T(8,128)S(1)}, f32[40,2048]{1,0:T(8,128)S(1)}, u32[]{:S(2)}, u32[]{:S(2)}) collective-permute-start(f32[40,2048]{1,0:T(8,128)S(1)} %get-tuple-element.67.refs_0_), channel_id=1, source_target_pairs={{0,4},{2,6},{4,0},{6,2},{1,5},{3,7},{5,1},{7,3},{8,12},{10,14},{12... | collective-permute-start | bytes 983048 | tf_op jit(solution)/shard_map/ppermute | solution.py:776
  31.6 1.4 %collective-permute-start.8 = (f32[40,2048]{1,0:T(8,128)S(1)}, f32[40,2048]{1,0:T(8,128)S(1)}, u32[]{:S(2)}, u32[]{:S(2)}) collective-permute-start(f32[40,2048]{1,0:T(8,128)S(1)} %get-tuple-element.67.refs_0_), channel_id=1, source_target_pairs={{0,6},{2,0},{4,2},{6,4},{1,7},{3,1},{5,3},{7,5},{8,14},{10,8},{12,... | collective-permute-start | bytes 983048 | tf_op jit(solution)/shard_map/ppermute | solution.py:776
  33.0 5.2 %collective-permute-done.10.refs_3_ = f32[40,2048]{1,0:T(8,128)S(1)} collective-permute-done((f32[40,2048]{1,0:T(8,128)S(1)}, f32[40,2048]{1,0:T(8,128)S(1)}, u32[]{:S(2)}, u32[]{:S(2)}) %collective-permute-start.10) | collective-permute-done | bytes 327712 | tf_op jit(solution)/shard_map/ppermute | solution.py:776
  38.2 8.0 %collective-permute-done.9.refs_2_ = f32[40,2048]{1,0:T(8,128)S(1)} collective-permute-done((f32[40,2048]{1,0:T(8,128)S(1)}, f32[40,2048]{1,0:T(8,128)S(1)}, u32[]{:S(2)}, u32[]{:S(2)}) %collective-permute-start.9) | collective-permute-done | bytes 327712 | tf_op jit(solution)/shard_map/ppermute | solution.py:776
  46.7 1.8 %collective-permute-done.11.refs_9_.refs_8_ = f32[1,32768]{1,0:T(1,128)S(1)} collective-permute-done((f32[1,32768]{1,0:T(1,128)S(1)}, f32[1,32768]{1,0:T(1,128)S(1)}, u32[]{:S(2)}, u32[]{:S(2)}) %collective-permute-start.11) | collective-permute-done | bytes 131104 | tf_op jit(solution)/shard_map/ppermute | solution.py:765
  48.6 1.0 %collective-permute-done.7.partner = f32[1,128]{1,0:T(1,128)S(1)} collective-permute-done((f32[1,128]{1,0:T(1,128)S(1)}, f32[1,128]{1,0:T(1,128)S(1)}, u32[]{:S(2)}, u32[]{:S(2)}) %collective-permute-start.7) | collective-permute-done | bytes 544 | tf_op jit(solution)/shard_map/ppermute | solution.py:765
  49.6 0.7 collective-permute-start.12
  51.0 16.8 %all-to-all-start = ((f32[128,1,128]{2,1,0:T(1,128)}), f32[128,1,128]{2,1,0:T(1,128)S(1)}, u32[]{:S(2)}, u32[]{:S(2)}) async-start(f32[128,1,128]{2,1,0:T(1,128)} %pair.1), calls=%async_computation | async-start | bytes 131072 | tf_op jit(solution)/shard_map/all_to_all | solution.py:844
  67.8 2.4 %gradient_kept.1 = (f32[4,16,4096]{2,1,0:T(8,128)S(1)}, f32[4,16,4096]{2,1,0:T(8,128)S(1)}, f32[4,16,4096]{2,1,0:T(8,128)S(1)}) custom-call(f32[40,2048]{1,0:T(8,128)S(1)} %get-tuple-element.67.refs_0_, f32[40,2048]{1,0:T(8,128)S(1)} %collective-permute-done.8.refs_1_, f32[40,2048]{1,0:T(8,128)S(1)} %collective-permute-done.9.refs_2_, ...), custom_call_target="tpu_custom_call" | custom-call | tf_op jit(solution)/shard_map/gradient_kept/pallas_call | solution.py:722
  70.2 2.0 %gradient_given.1.given = f32[4,16,4096]{2,1,0:T(8,128)S(1)} custom-call(f32[40,2048]{1,0:T(8,128)S(1)} %collective-permute-done.13.refs_0_, f32[40,2048]{1,0:T(8,128)} %collective-permute-done.14.refs_1_, f32[40,2048]{1,0:T(8,128)} %collective-permute-done.15.refs_2_, f32[40,2048]{1,0:T(8,128)} %collective-permute-done.16.refs_3_, ...), custom_call_target="tpu_custom_call" | custom-call | tf_op jit(solution)/shard_map/gradient_given/pallas_call | solution.py:738
  72.2 7.1 %all-to-all-done.gathered = f32[128,1,128]{2,1,0:T(1,128)S(1)} async-done(((f32[128,1,128]{2,1,0:T(1,128)}), f32[128,1,128]{2,1,0:T(1,128)S(1)}, u32[]{:S(2)}, u32[]{:S(2)}) %all-to-all-start) | async-done | bytes 65568 | tf_op jit(solution)/shard_map/all_to_all | solution.py:844
  79.2 3.1 %finish.1 = (f32[16,32768]{1,0:T(8,128)}, f32[1,1]{1,0:T(1,128)}) custom-call(f32[128,1,128]{2,1,0:T(1,128)S(1)} %all-to-all-done.gathered, f32[1,20]{1,0:T(1,128)S(1)} %get-tuple-element.65.mean, f32[64,20]{1,0:T(8,128)S(1)} %get-tuple-element.66.table, s32[1,32768]{1,0:T(1,128)S(1)} %get-tuple-element.42.depth.refs_7_.refs_6_, ...), custom_call_target="tpu_custom_call" | custom-call | tf_op jit(solution)/shard_map/finish/pallas_call | solution.py:638
  (30 shorter events, 3.4 us)
Async XLA Ops:
  4.6 8.6 %collective-permute-start.1 = (f32[3,40,2048]{2,1,0:T(8,128)S(1)}, f32[3,40,2048]{2,1,0:T(8,128)S(1)}, u32[]{:S(2)}, u32[]{:S(2)}) collective-permute-start(f32[3,40,2048]{2,1,0:T(8,128)S(1)} %get-tuple-element.52), channel_id=1, source_target_pairs={{0,1},{1,0},{2,3},{3,2},{4,5},{5,4},{6,7},{7,6},{8,9},{9,8},{10,11... | collective-permute-start | bytes 2949128 | tf_op jit(solution)/shard_map/ppermute | solution.py:765
  4.7 3.0 %collective-permute-start = (f32[40,2048]{1,0:T(8,128)S(1)}, f32[40,2048]{1,0:T(8,128)S(1)}, u32[]{:S(2)}, u32[]{:S(2)}) collective-permute-start(f32[40,2048]{1,0:T(8,128)S(1)} %get-tuple-element.44), channel_id=1, source_target_pairs={{0,1},{1,0},{2,3},{3,2},{4,5},{5,4},{6,7},{7,6},{8,9},{9,8},{10,11... | collective-permute-start | bytes 983048 | tf_op jit(solution)/shard_map/ppermute | solution.py:765
  8.6 19.3 %collective-permute-start.3 = (f32[40,2048]{1,0:T(8,128)S(1)}, f32[40,2048]{1,0:T(8,128)S(1)}, u32[]{:S(2)}, u32[]{:S(2)}) collective-permute-start(f32[40,2048]{1,0:T(8,128)S(1)} %get-tuple-element.57), channel_id=1, source_target_pairs={{0,4},{2,6},{4,0},{6,2},{1,5},{3,7},{5,1},{7,3},{8,12},{10,14},{12... | collective-permute-start | bytes 983048 | tf_op jit(solution)/shard_map/ppermute | solution.py:776
  13.2 8.3 %copy-start = (f32[4,20,16]{1,2,0:T(8,128)S(1)}, f32[4,20,16]{1,2,0:T(8,128)}, u32[]{:S(2)}) copy-start(f32[4,20,16]{1,2,0:T(8,128)} %param.10) | copy-start | bytes 15364
  13.2 8.3 %copy-start.1 = (f32[16]{0:T(128)S(1)}, f32[16]{0:T(128)}, u32[]{:S(2)}) copy-start(f32[16]{0:T(128)} %param.15) | copy-start | bytes 196
  13.2 8.3 %copy-start.2 = (f32[20]{0:T(128)S(1)}, f32[20]{0:T(128)}, u32[]{:S(2)}) copy-start(f32[20]{0:T(128)} %param.14) | copy-start | bytes 244
  13.4 14.6 %collective-permute-start.2 = (f32[40,2048]{1,0:T(8,128)S(1)}, f32[40,2048]{1,0:T(8,128)S(1)}, u32[]{:S(2)}, u32[]{:S(2)}) collective-permute-start(f32[40,2048]{1,0:T(8,128)S(1)} %get-tuple-element.56), channel_id=1, source_target_pairs={{0,2},{2,4},{4,6},{6,0},{1,3},{3,5},{5,7},{7,1},{8,10},{10,12},{12... | collective-permute-start | bytes 983048 | tf_op jit(solution)/shard_map/ppermute | solution.py:776
  14.1 13.9 %collective-permute-start.4 = (f32[40,2048]{1,0:T(8,128)S(1)}, f32[40,2048]{1,0:T(8,128)S(1)}, u32[]{:S(2)}, u32[]{:S(2)}) collective-permute-start(f32[40,2048]{1,0:T(8,128)S(1)} %get-tuple-element.58), channel_id=1, source_target_pairs={{0,6},{2,0},{4,2},{6,4},{1,7},{3,1},{5,3},{7,5},{8,14},{10,8},{12,... | collective-permute-start | bytes 983048 | tf_op jit(solution)/shard_map/ppermute | solution.py:776
  16.7 6.0 %collective-permute-start.5 = (f32[16,2048]{1,0:T(8,128)S(1)}, f32[16,2048]{1,0:T(8,128)S(1)}, u32[]{:S(2)}, u32[]{:S(2)}) collective-permute-start(f32[16,2048]{1,0:T(8,128)S(1)} %get-tuple-element.61), channel_id=1, source_target_pairs={{0,8},{16,24},{32,40},{48,56},{64,72},{80,88},{96,104},{112,120},{... | collective-permute-start | bytes 393224 | tf_op jit(solution)/shard_map/ppermute | solution.py:781
  17.2 7.3 %collective-permute-start.6 = (f32[16,2048]{1,0:T(8,128)S(1)}, f32[16,2048]{1,0:T(8,128)S(1)}, u32[]{:S(2)}, u32[]{:S(2)}) collective-permute-start(f32[16,2048]{1,0:T(8,128)S(1)} %get-tuple-element.62), channel_id=1, source_target_pairs={{8,16},{24,32},{40,48},{56,64},{72,80},{88,96},{104,112},{120,128}... | collective-permute-start | bytes 393224 | tf_op jit(solution)/shard_map/ppermute | solution.py:781
  28.3 9.9 %collective-permute-start.10 = (f32[40,2048]{1,0:T(8,128)S(1)}, f32[40,2048]{1,0:T(8,128)S(1)}, u32[]{:S(2)}, u32[]{:S(2)}) collective-permute-start(f32[40,2048]{1,0:T(8,128)S(1)} %get-tuple-element.67.refs_0_), channel_id=1, source_target_pairs={{0,2},{2,4},{4,6},{6,0},{1,3},{3,5},{5,7},{7,1},{8,10},{10,12},{12... | collective-permute-start | bytes 983048 | tf_op jit(solution)/shard_map/ppermute | solution.py:776
  28.9 17.3 %collective-permute-start.9 = (f32[40,2048]{1,0:T(8,128)S(1)}, f32[40,2048]{1,0:T(8,128)S(1)}, u32[]{:S(2)}, u32[]{:S(2)}) collective-permute-start(f32[40,2048]{1,0:T(8,128)S(1)} %get-tuple-element.67.refs_0_), channel_id=1, source_target_pairs={{0,4},{2,6},{4,0},{6,2},{1,5},{3,7},{5,1},{7,3},{8,12},{10,14},{12... | collective-permute-start | bytes 983048 | tf_op jit(solution)/shard_map/ppermute | solution.py:776
  31.6 14.6 %collective-permute-start.8 = (f32[40,2048]{1,0:T(8,128)S(1)}, f32[40,2048]{1,0:T(8,128)S(1)}, u32[]{:S(2)}, u32[]{:S(2)}) collective-permute-start(f32[40,2048]{1,0:T(8,128)S(1)} %get-tuple-element.67.refs_0_), channel_id=1, source_target_pairs={{0,6},{2,0},{4,2},{6,4},{1,7},{3,1},{5,3},{7,5},{8,14},{10,8},{12,... | collective-permute-start | bytes 983048 | tf_op jit(solution)/shard_map/ppermute | solution.py:776
  33.0 37.1 %collective-permute-start.13 = (f32[40,2048]{1,0:T(8,128)S(1)}, f32[40,2048]{1,0:T(8,128)S(1)}, u32[]{:S(2)}, u32[]{:S(2)}) collective-permute-start(f32[40,2048]{1,0:T(8,128)S(1)} %get-tuple-element.67.refs_0_), channel_id=1, source_target_pairs={{0,1},{1,0},{2,3},{3,2},{4,5},{5,4},{6,7},{7,6},{8,9},{9,8},{10,11... | collective-permute-start | bytes 983048 | tf_op jit(solution)/shard_map/ppermute | solution.py:765
  38.2 32.0 %collective-permute-start.16 = (f32[40,2048]{1,0:T(8,128)S(1)}, f32[40,2048]{1,0:T(8,128)}, u32[]{:S(2)}, u32[]{:S(2)}) collective-permute-start(f32[40,2048]{1,0:T(8,128)S(1)} %collective-permute-done.10.refs_3_), channel_id=1, source_target_pairs={{0,1},{1,0},{2,3},{3,2},{4,5},{5,4},{6,7},{7,6},{8,9},{9,8},{10,11... | collective-permute-start | bytes 983048 | tf_op jit(solution)/shard_map/ppermute | solution.py:765
  46.2 24.0 %collective-permute-start.15 = (f32[40,2048]{1,0:T(8,128)S(1)}, f32[40,2048]{1,0:T(8,128)}, u32[]{:S(2)}, u32[]{:S(2)}) collective-permute-start(f32[40,2048]{1,0:T(8,128)S(1)} %collective-permute-done.9.refs_2_), channel_id=1, source_target_pairs={{0,1},{1,0},{2,3},{3,2},{4,5},{5,4},{6,7},{7,6},{8,9},{9,8},{10,11... | collective-permute-start | bytes 983048 | tf_op jit(solution)/shard_map/ppermute | solution.py:765
  46.2 24.0 %collective-permute-start.14 = (f32[40,2048]{1,0:T(8,128)S(1)}, f32[40,2048]{1,0:T(8,128)}, u32[]{:S(2)}, u32[]{:S(2)}) collective-permute-start(f32[40,2048]{1,0:T(8,128)S(1)} %collective-permute-done.8.refs_1_), channel_id=1, source_target_pairs={{0,1},{1,0},{2,3},{3,2},{4,5},{5,4},{6,7},{7,6},{8,9},{9,8},{10,11... | collective-permute-start | bytes 983048 | tf_op jit(solution)/shard_map/ppermute | solution.py:765
  46.7 1.8 %collective-permute-start.11 = (f32[1,32768]{1,0:T(1,128)S(1)}, f32[1,32768]{1,0:T(1,128)S(1)}, u32[]{:S(2)}, u32[]{:S(2)}) collective-permute-start(f32[1,32768]{1,0:T(1,128)S(1)} %get-tuple-element.71), channel_id=1, source_target_pairs={{0,1},{1,0},{2,3},{3,2},{4,5},{5,4},{6,7},{7,6},{8,9},{9,8},{10,11... | collective-permute-start | bytes 393224 | tf_op jit(solution)/shard_map/ppermute | solution.py:765
  48.5 1.2 %collective-permute-start.7 = (f32[1,128]{1,0:T(1,128)S(1)}, f32[1,128]{1,0:T(1,128)S(1)}, u32[]{:S(2)}, u32[]{:S(2)}) collective-permute-start(f32[1,128]{1,0:T(1,128)S(1)} %get-tuple-element.64.mine), channel_id=1, source_target_pairs={{0,1},{1,0},{2,3},{3,2},{4,5},{5,4},{6,7},{7,6},{8,9},{9,8},{10,11... | collective-permute-start | bytes 1544 | tf_op jit(solution)/shard_map/ppermute | solution.py:765
  49.6 18.1 %collective-permute-start.12 = (f32[1,32768]{1,0:T(1,128)S(1)}, f32[1,32768]{1,0:T(1,128)S(1)}, u32[]{:S(2)}, u32[]{:S(2)}) collective-permute-start(f32[1,32768]{1,0:T(1,128)S(1)} %get-tuple-element.72), channel_id=1, source_target_pairs={{1,2},{3,4},{5,6},{2,1},{4,3},{6,5},{9,10},{11,12},{13,14},{10,9},... | collective-permute-start | bytes 393224 | tf_op jit(solution)/shard_map/ppermute | solution.py:771
  51.0 28.3 %all-to-all-start = ((f32[128,1,128]{2,1,0:T(1,128)}), f32[128,1,128]{2,1,0:T(1,128)S(1)}, u32[]{:S(2)}, u32[]{:S(2)}) async-start(f32[128,1,128]{2,1,0:T(1,128)} %pair.1), calls=%async_computation | async-start | bytes 131072 | tf_op jit(solution)/shard_map/all_to_all | solution.py:844

commit v6 on v5

--- a/solution.py
+++ b/solution.py
@@ -244,6 +244,11 @@
     chip, core = position_of()
     half = core if mine else 1 - core
     copies = []
+    if mine:
+        copies.append(
+            pltpu.make_async_copy(density_before.at[FAR], density.at[FAR], marks.at[len(REST)])
+        )
+        copies[-1].start()
     for k, d in enumerate(REST):
         project_piece(
             d,
@@ -268,18 +273,22 @@
     _, shells, width = field.shape
     return pl.pallas_call(
         functools.partial(project_rest_body, mine=mine, classes=classes, bins=bins),
-        in_specs=[HERE] * 4 + [AWAY, HERE],
+        in_specs=[HERE] * 4 + [HERE if mine else AWAY, HERE],
         out_specs=[HERE, AWAY, HERE],
         out_shape=[
             vmem(len(REST), 2 * bins, width // 2),
             pltpu.HBM((4, shells, width), jnp.float32),
             vmem(4, shells, width),
         ],
-        scratch_shapes=[vmem(4, shells, width), pltpu.SemaphoreType.DMA((len(REST),))],
-        input_output_aliases={4: 1, 5: 2},
+        scratch_shapes=[vmem(4, shells, width), pltpu.SemaphoreType.DMA((4,))],
+        input_output_aliases={5: 2} if mine else {4: 1, 5: 2},
         compiler_params=LIMIT,
         name="rest_kept" if mine else "rest_given",
-    )(*in_vmem(field, momentum, depth, weights), *in_hbm(density), *in_vmem(position))
+    )(
+        *in_vmem(field, momentum, depth, weights),
+        *(in_vmem(density) if mine else in_hbm(density)),
+        *in_vmem(position),
+    )
 
 
 def project_far_body(
@@ -289,11 +298,9 @@
     weights,
     partner,
     total,
-    density,
+    stage,
     position,
-    stage,
     proj,
-    mark,
     classes,
     bins,
 ):
@@ -312,10 +319,7 @@
         classes,
         bins,
     )
-    copy = pltpu.make_async_copy(stage.at[FAR], density.at[FAR], mark)
-    copy.start()
     total[...] = proj[...] + partner[...]
-    copy.wait()
 
 
 def project_far(field, momentum, depth, weights, partner, classes, bins):
@@ -323,17 +327,13 @@
     return pl.pallas_call(
         functools.partial(project_far_body, classes=classes, bins=bins),
         in_specs=[HERE] * 5,
-        out_specs=[HERE, AWAY, HERE],
+        out_specs=[HERE] * 3,
         out_shape=[
             vmem(*partner.shape),
-            pltpu.HBM((4, shells, width), jnp.float32),
             vmem(4, shells, width),
-        ],
-        scratch_shapes=[
             vmem(4, shells, width),
-            vmem(*partner.shape),
-            pltpu.SemaphoreType.DMA,
-        ],
+        ],
+        scratch_shapes=[vmem(*partner.shape)],
         compiler_params=LIMIT,
         name="far_kept",
     )(*in_vmem(field, momentum, depth, weights, partner))

time: 84.2 us -> 83.9 us (level)
  the two profiles are of different devices: /device:TPU:8 before, /device:TPU:1 now
where the time goes in v6:
time: 83.9 us; the launch traced here: 83.6 us
  starting transfers between devices  39.8 us (47%)
  waiting for transfers between devices  23.6 us (28%)
  Pallas kernels  19.2 us (23%)
  between operations  1.01 us (1%)
    all_to_all x1, starting transfers between devices, shards(): gathered = lax.all_to_all(stats, ('pix', 'x'), 0, 0)  15.1 us
    ppermute x8, starting transfers between devices, swap(): return lax.ppermute(values, 'core', [(0, 1), (1, 0)])  13.5 us
    ppermute x6, waiting for transfers between devices, along(): lax.ppermute(values, 'x', [(i, (i + step) % count) for i in range(count)])  11.1 us
    ppermute x6, starting transfers between devices, along(): lax.ppermute(values, 'x', [(i, (i + step) % count) for i in range(count)])  7.02 us
    all_to_all x1, waiting for transfers between devices, shards(): gathered = lax.all_to_all(stats, ('pix', 'x'), 0, 0)  6.59 us
    ppermute x8, waiting for transfers between devices, swap(): return lax.ppermute(values, 'core', [(0, 1), (1, 0)])  4.98 us
    pallas_call x1, Pallas kernels, stencil(): pl.pallas_call(stencil_body, in_specs=[HERE] * 5, out_specs=AWAY, out_sha...  3.53 us
    pallas_call x2, Pallas kernels, project_rest(): pl.pallas_call(functools.partial(project_rest_body, mine=mine, classes=cl...  3.17 us
  transfers between devices with their start and end apart: 18, of which 7 were waited for; matrix products, arithmetic and copies ran while one was open for 0% of the time, Pallas kernels for 14%

profile of v6, /device:TPU:1, one launch (start us, length us, event | category | flops | bytes accessed | tf_op | source)
XLA Modules:
  0.0 83.6 jit_solution(16787046433853675572)
XLA Ops:
  0.6 2.4 %load.1 = (f32[40,2048]{1,0:T(8,128)S(1)}, f32[4,16,4096]{2,1,0:T(8,128)}, f32[4,16,4096]{2,1,0:T(8,128)S(1)}, f32[4,16,4096]{2,1,0:T(8,128)S(1)}, f32[4,16,4096...) custom-call(f32[16,32768]{1,0:T(8,128)} %field.1, ...), custom_call_target="tpu_custom_call" | custom-call | tf_op jit(solution)/shard_map/load/pallas_call | solution.py:212
  3.1 1.5 %rest_given.1 = (f32[3,40,2048]{2,1,0:T(8,128)S(1)}, f32[4,16,4096]{2,1,0:T(8,128)}, f32[4,16,4096]{2,1,0:T(8,128)S(1)}) custom-call(f32[4,16,4096]{2,1,0:T(8,128)S(1)} %get-tuple-element.48.field, f32[4,16,4096]{2,1,0:T(8,128)S(1)} %get-tuple-element.49.momentum, ...), custom_call_target="tpu_custom_call", output_to_operand_aliasing={{1}: (4, {}), {2}: (5, {})} | custom-call | tf_op jit(solution)/shard_map/rest_given/pallas_call | solution.py:274
  4.6 3.3 %collective-permute-start.1 = (f32[3,40,2048]{2,1,0:T(8,128)S(1)}, f32[3,40,2048]{2,1,0:T(8,128)S(1)}, u32[]{:S(2)}, u32[]{:S(2)}) collective-permute-start(f32[3,40,2048]{2,1,0:T(8,128)S(1)} %get-tuple-element.52), channel_id=1, source_target_pairs={{0,1},{1,0},{2,3},{3,2},{4,5},{5,4},{6,7},{7,6},{8,9},{9,8},{10,11... | collective-permute-start | bytes 2949128 | tf_op jit(solution)/shard_map/ppermute | solution.py:765
  8.0 2.6 %collective-permute-done.partner = f32[40,2048]{1,0:T(8,128)S(1)} collective-permute-done((f32[40,2048]{1,0:T(8,128)S(1)}, f32[40,2048]{1,0:T(8,128)S(1)}, u32[]{:S(2)}, u32[]{:S(2)}) %collective-permute-start) | collective-permute-done | bytes 327712 | tf_op jit(solution)/shard_map/ppermute | solution.py:765
  10.9 1.1 %collective-permute-start.3 = (f32[40,2048]{1,0:T(8,128)S(1)}, f32[40,2048]{1,0:T(8,128)S(1)}, u32[]{:S(2)}, u32[]{:S(2)}) collective-permute-start(f32[40,2048]{1,0:T(8,128)S(1)} %get-tuple-element.57), channel_id=1, source_target_pairs={{0,4},{2,6},{4,0},{6,2},{1,5},{3,7},{5,1},{7,3},{8,12},{10,14},{12... | collective-permute-start | bytes 983048 | tf_op jit(solution)/shard_map/ppermute | solution.py:776
  12.0 1.7 %rest_kept.1 = (f32[3,40,2048]{2,1,0:T(8,128)S(1)}, f32[4,16,4096]{2,1,0:T(8,128)}, f32[4,16,4096]{2,1,0:T(8,128)S(1)}) custom-call(f32[4,16,4096]{2,1,0:T(8,128)S(1)} %get-tuple-element.40.field, f32[4,16,4096]{2,1,0:T(8,128)S(1)} %get-tuple-element.41.momentum, ...), custom_call_target="tpu_custom_call", output_to_operand_aliasing={{2}: (5, {})} | custom-call | tf_op jit(solution)/shard_map/rest_kept/pallas_call | solution.py:274
  14.3 2.4 %collective-permute-start.4 = (f32[40,2048]{1,0:T(8,128)S(1)}, f32[40,2048]{1,0:T(8,128)S(1)}, u32[]{:S(2)}, u32[]{:S(2)}) collective-permute-start(f32[40,2048]{1,0:T(8,128)S(1)} %get-tuple-element.58), channel_id=1, source_target_pairs={{0,6},{2,0},{4,2},{6,4},{1,7},{3,1},{5,3},{7,5},{8,14},{10,8},{12,... | collective-permute-start | bytes 983048 | tf_op jit(solution)/shard_map/ppermute | solution.py:776
  16.6 1.3 %collective-permute-start.5 = (f32[16,2048]{1,0:T(8,128)S(1)}, f32[16,2048]{1,0:T(8,128)S(1)}, u32[]{:S(2)}, u32[]{:S(2)}) collective-permute-start(f32[16,2048]{1,0:T(8,128)S(1)} %get-tuple-element.61), channel_id=1, source_target_pairs={{0,8},{16,24},{32,40},{48,56},{64,72},{80,88},{96,104},{112,120},{... | collective-permute-start | bytes 393224 | tf_op jit(solution)/shard_map/ppermute | solution.py:781
  18.6 1.2 %prepare.1 = (f32[40,2048]{1,0:T(8,128)S(1)}, bf16[128,144]{1,0:T(8,128)(2,1)S(1)}, f32[16,128]{1,0:T(8,128)S(1)}, f32[1,20]{1,0:T(1,128)S(1)}, f32[64,20]{1,0:T...) custom-call(s32[20,32768]{1,0:T(8,128)} %counts.1, f32[4,16,4096]{2,1,0:T(8,128)S(1)} %get-tuple-element.53.given_place.given, ...), custom_call_target="tpu_custom_call" | custom-call | tf_op jit(solution)/shard_map/prepare/pallas_call | solution.py:431
  19.8 0.9 %collective-permute-done.5.near = f32[16,2048]{1,0:T(8,128)S(1)} collective-permute-done((f32[16,2048]{1,0:T(8,128)S(1)}, f32[16,2048]{1,0:T(8,128)S(1)}, u32[]{:S(2)}, u32[]{:S(2)}) %collective-permute-start.5) | collective-permute-done | bytes 131104 | tf_op jit(solution)/shard_map/ppermute | solution.py:781
  20.7 3.5 %stencil.1.later.refs_5_ = f32[16,32768]{1,0:T(8,128)} custom-call(f32[4,16,4096]{2,1,0:T(8,128)S(1)} %get-tuple-element.53.given_place.given, f32[4,16,4096]{2,1,0:T(8,128)S(1)} %get-tuple-element.54.kept_place.kept, f32[16,2048]{1,0:T(8,128)S(1)} %collective-permute-done.5.near, f32[16,2048]{1,0:T(8,128)S(1)} %collective-permute-done.6.beyond, ...), custom_call_target="tpu_custom_call" | custom-call | tf_op jit(solution)/shard_map/stencil/pallas_call | solution.py:497
  24.3 4.8 %collective-permute-done.2.first = f32[40,2048]{1,0:T(8,128)S(1)} collective-permute-done((f32[40,2048]{1,0:T(8,128)S(1)}, f32[40,2048]{1,0:T(8,128)S(1)}, u32[]{:S(2)}, u32[]{:S(2)}) %collective-permute-start.2) | collective-permute-done | bytes 327712 | tf_op jit(solution)/shard_map/ppermute | solution.py:776
  29.4 2.0 %collective-permute-start.9 = (f32[40,2048]{1,0:T(8,128)S(1)}, f32[40,2048]{1,0:T(8,128)S(1)}, u32[]{:S(2)}, u32[]{:S(2)}) collective-permute-start(f32[40,2048]{1,0:T(8,128)S(1)} %get-tuple-element.67.refs_0_), channel_id=1, source_target_pairs={{0,4},{2,6},{4,0},{6,2},{1,5},{3,7},{5,1},{7,3},{8,12},{10,14},{12... | collective-permute-start | bytes 983048 | tf_op jit(solution)/shard_map/ppermute | solution.py:776
  31.4 1.2 %collective-permute-start.8 = (f32[40,2048]{1,0:T(8,128)S(1)}, f32[40,2048]{1,0:T(8,128)S(1)}, u32[]{:S(2)}, u32[]{:S(2)}) collective-permute-start(f32[40,2048]{1,0:T(8,128)S(1)} %get-tuple-element.67.refs_0_), channel_id=1, source_target_pairs={{0,6},{2,0},{4,2},{6,4},{1,7},{3,1},{5,3},{7,5},{8,14},{10,8},{12,... | collective-permute-start | bytes 983048 | tf_op jit(solution)/shard_map/ppermute | solution.py:776
  32.6 1.3 %collective-permute-start.13 = (f32[40,2048]{1,0:T(8,128)S(1)}, f32[40,2048]{1,0:T(8,128)S(1)}, u32[]{:S(2)}, u32[]{:S(2)}) collective-permute-start(f32[40,2048]{1,0:T(8,128)S(1)} %get-tuple-element.67.refs_0_), channel_id=1, source_target_pairs={{0,1},{1,0},{2,3},{3,2},{4,5},{5,4},{6,7},{7,6},{8,9},{9,8},{10,11... | collective-permute-start | bytes 983048 | tf_op jit(solution)/shard_map/ppermute | solution.py:765
  33.9 6.3 %collective-permute-done.10.refs_3_ = f32[40,2048]{1,0:T(8,128)S(1)} collective-permute-done((f32[40,2048]{1,0:T(8,128)S(1)}, f32[40,2048]{1,0:T(8,128)S(1)}, u32[]{:S(2)}, u32[]{:S(2)}) %collective-permute-start.10) | collective-permute-done | bytes 327712 | tf_op jit(solution)/shard_map/ppermute | solution.py:776
  40.2 7.7 %collective-permute-start.16 = (f32[40,2048]{1,0:T(8,128)S(1)}, f32[40,2048]{1,0:T(8,128)}, u32[]{:S(2)}, u32[]{:S(2)}) collective-permute-start(f32[40,2048]{1,0:T(8,128)S(1)} %collective-permute-done.10.refs_3_), channel_id=1, source_target_pairs={{0,1},{1,0},{2,3},{3,2},{4,5},{5,4},{6,7},{7,6},{8,9},{9,8},{10,11... | collective-permute-start | bytes 983048 | tf_op jit(solution)/shard_map/ppermute | solution.py:765
  48.6 1.6 %collective-permute-done.11.refs_9_.refs_8_ = f32[1,32768]{1,0:T(1,128)S(1)} collective-permute-done((f32[1,32768]{1,0:T(1,128)S(1)}, f32[1,32768]{1,0:T(1,128)S(1)}, u32[]{:S(2)}, u32[]{:S(2)}) %collective-permute-start.11) | collective-permute-done | bytes 131104 | tf_op jit(solution)/shard_map/ppermute | solution.py:765
  51.4 2.2 %collective-permute-start.12 = (f32[1,32768]{1,0:T(1,128)S(1)}, f32[1,32768]{1,0:T(1,128)S(1)}, u32[]{:S(2)}, u32[]{:S(2)}) collective-permute-start(f32[1,32768]{1,0:T(1,128)S(1)} %get-tuple-element.72), channel_id=1, source_target_pairs={{1,2},{3,4},{5,6},{2,1},{4,3},{6,5},{9,10},{11,12},{13,14},{10,9},... | collective-permute-start | bytes 393224 | tf_op jit(solution)/shard_map/ppermute | solution.py:771
  54.3 15.1 %all-to-all-start = ((f32[128,1,128]{2,1,0:T(1,128)}), f32[128,1,128]{2,1,0:T(1,128)S(1)}, u32[]{:S(2)}, u32[]{:S(2)}) async-start(f32[128,1,128]{2,1,0:T(1,128)} %pair.1), calls=%async_computation | async-start | bytes 131072 | tf_op jit(solution)/shard_map/all_to_all | solution.py:844
  69.3 2.4 %gradient_kept.1 = (f32[4,16,4096]{2,1,0:T(8,128)S(1)}, f32[4,16,4096]{2,1,0:T(8,128)S(1)}, f32[4,16,4096]{2,1,0:T(8,128)S(1)}) custom-call(f32[40,2048]{1,0:T(8,128)S(1)} %get-tuple-element.67.refs_0_, f32[40,2048]{1,0:T(8,128)S(1)} %collective-permute-done.8.refs_1_, f32[40,2048]{1,0:T(8,128)S(1)} %collective-permute-done.9.refs_2_, ...), custom_call_target="tpu_custom_call" | custom-call | tf_op jit(solution)/shard_map/gradient_kept/pallas_call | solution.py:722
  71.8 2.0 %gradient_given.1.given = f32[4,16,4096]{2,1,0:T(8,128)S(1)} custom-call(f32[40,2048]{1,0:T(8,128)S(1)} %collective-permute-done.13.refs_0_, f32[40,2048]{1,0:T(8,128)} %collective-permute-done.14.refs_1_, f32[40,2048]{1,0:T(8,128)} %collective-permute-done.15.refs_2_, f32[40,2048]{1,0:T(8,128)} %collective-permute-done.16.refs_3_, ...), custom_call_target="tpu_custom_call" | custom-call | tf_op jit(solution)/shard_map/gradient_given/pallas_call | solution.py:738
  73.7 6.6 %all-to-all-done.gathered = f32[128,1,128]{2,1,0:T(1,128)S(1)} async-done(((f32[128,1,128]{2,1,0:T(1,128)}), f32[128,1,128]{2,1,0:T(1,128)S(1)}, u32[]{:S(2)}, u32[]{:S(2)}) %all-to-all-start) | async-done | bytes 65568 | tf_op jit(solution)/shard_map/all_to_all | solution.py:844
  80.3 3.1 %finish.1 = (f32[16,32768]{1,0:T(8,128)}, f32[1,1]{1,0:T(1,128)}) custom-call(f32[128,1,128]{2,1,0:T(1,128)S(1)} %all-to-all-done.gathered, f32[1,20]{1,0:T(1,128)S(1)} %get-tuple-element.65.mean, f32[64,20]{1,0:T(8,128)S(1)} %get-tuple-element.66.table, s32[1,32768]{1,0:T(1,128)S(1)} %get-tuple-element.42.depth.refs_7_.refs_6_, ...), custom_call_target="tpu_custom_call" | custom-call | tf_op jit(solution)/shard_map/finish/pallas_call | solution.py:638
  (30 shorter events, 4.6 us)
Async XLA Ops:
  4.6 9.1 %collective-permute-start.1 = (f32[3,40,2048]{2,1,0:T(8,128)S(1)}, f32[3,40,2048]{2,1,0:T(8,128)S(1)}, u32[]{:S(2)}, u32[]{:S(2)}) collective-permute-start(f32[3,40,2048]{2,1,0:T(8,128)S(1)} %get-tuple-element.52), channel_id=1, source_target_pairs={{0,1},{1,0},{2,3},{3,2},{4,5},{5,4},{6,7},{7,6},{8,9},{9,8},{10,11... | collective-permute-start | bytes 2949128 | tf_op jit(solution)/shard_map/ppermute | solution.py:765
  7.9 2.7 %collective-permute-start = (f32[40,2048]{1,0:T(8,128)S(1)}, f32[40,2048]{1,0:T(8,128)S(1)}, u32[]{:S(2)}, u32[]{:S(2)}) collective-permute-start(f32[40,2048]{1,0:T(8,128)S(1)} %get-tuple-element.44), channel_id=1, source_target_pairs={{0,1},{1,0},{2,3},{3,2},{4,5},{5,4},{6,7},{7,6},{8,9},{9,8},{10,11... | collective-permute-start | bytes 983048 | tf_op jit(solution)/shard_map/ppermute | solution.py:765
  10.9 13.4 %collective-permute-start.3 = (f32[40,2048]{1,0:T(8,128)S(1)}, f32[40,2048]{1,0:T(8,128)S(1)}, u32[]{:S(2)}, u32[]{:S(2)}) collective-permute-start(f32[40,2048]{1,0:T(8,128)S(1)} %get-tuple-element.57), channel_id=1, source_target_pairs={{0,4},{2,6},{4,0},{6,2},{1,5},{3,7},{5,1},{7,3},{8,12},{10,14},{12... | collective-permute-start | bytes 983048 | tf_op jit(solution)/shard_map/ppermute | solution.py:776
  13.7 4.9 %copy-start = (f32[4,20,16]{1,2,0:T(8,128)S(1)}, f32[4,20,16]{1,2,0:T(8,128)}, u32[]{:S(2)}) copy-start(f32[4,20,16]{1,2,0:T(8,128)} %param.10) | copy-start | bytes 15364
  13.7 4.9 %copy-start.1 = (f32[16]{0:T(128)S(1)}, f32[16]{0:T(128)}, u32[]{:S(2)}) copy-start(f32[16]{0:T(128)} %param.15) | copy-start | bytes 196
  13.7 4.9 %copy-start.2 = (f32[20]{0:T(128)S(1)}, f32[20]{0:T(128)}, u32[]{:S(2)}) copy-start(f32[20]{0:T(128)} %param.14) | copy-start | bytes 244
  13.9 15.3 %collective-permute-start.2 = (f32[40,2048]{1,0:T(8,128)S(1)}, f32[40,2048]{1,0:T(8,128)S(1)}, u32[]{:S(2)}, u32[]{:S(2)}) collective-permute-start(f32[40,2048]{1,0:T(8,128)S(1)} %get-tuple-element.56), channel_id=1, source_target_pairs={{0,2},{2,4},{4,6},{6,0},{1,3},{3,5},{5,7},{7,1},{8,10},{10,12},{12... | collective-permute-start | bytes 983048 | tf_op jit(solution)/shard_map/ppermute | solution.py:776
  14.3 14.9 %collective-permute-start.4 = (f32[40,2048]{1,0:T(8,128)S(1)}, f32[40,2048]{1,0:T(8,128)S(1)}, u32[]{:S(2)}, u32[]{:S(2)}) collective-permute-start(f32[40,2048]{1,0:T(8,128)S(1)} %get-tuple-element.58), channel_id=1, source_target_pairs={{0,6},{2,0},{4,2},{6,4},{1,7},{3,1},{5,3},{7,5},{8,14},{10,8},{12,... | collective-permute-start | bytes 983048 | tf_op jit(solution)/shard_map/ppermute | solution.py:776
  16.6 4.1 %collective-permute-start.5 = (f32[16,2048]{1,0:T(8,128)S(1)}, f32[16,2048]{1,0:T(8,128)S(1)}, u32[]{:S(2)}, u32[]{:S(2)}) collective-permute-start(f32[16,2048]{1,0:T(8,128)S(1)} %get-tuple-element.61), channel_id=1, source_target_pairs={{0,8},{16,24},{32,40},{48,56},{64,72},{80,88},{96,104},{112,120},{... | collective-permute-start | bytes 393224 | tf_op jit(solution)/shard_map/ppermute | solution.py:781
  17.9 2.8 %collective-permute-start.6 = (f32[16,2048]{1,0:T(8,128)S(1)}, f32[16,2048]{1,0:T(8,128)S(1)}, u32[]{:S(2)}, u32[]{:S(2)}) collective-permute-start(f32[16,2048]{1,0:T(8,128)S(1)} %get-tuple-element.62), channel_id=1, source_target_pairs={{8,16},{24,32},{40,48},{56,64},{72,80},{88,96},{104,112},{120,128}... | collective-permute-start | bytes 393224 | tf_op jit(solution)/shard_map/ppermute | solution.py:781
  29.4 10.8 %collective-permute-start.10 = (f32[40,2048]{1,0:T(8,128)S(1)}, f32[40,2048]{1,0:T(8,128)S(1)}, u32[]{:S(2)}, u32[]{:S(2)}) collective-permute-start(f32[40,2048]{1,0:T(8,128)S(1)} %get-tuple-element.67.refs_0_), channel_id=1, source_target_pairs={{0,2},{2,4},{4,6},{6,0},{1,3},{3,5},{5,7},{7,1},{8,10},{10,12},{12... | collective-permute-start | bytes 983048 | tf_op jit(solution)/shard_map/ppermute | solution.py:776
  29.4 18.4 %collective-permute-start.9 = (f32[40,2048]{1,0:T(8,128)S(1)}, f32[40,2048]{1,0:T(8,128)S(1)}, u32[]{:S(2)}, u32[]{:S(2)}) collective-permute-start(f32[40,2048]{1,0:T(8,128)S(1)} %get-tuple-element.67.refs_0_), channel_id=1, source_target_pairs={{0,4},{2,6},{4,0},{6,2},{1,5},{3,7},{5,1},{7,3},{8,12},{10,14},{12... | collective-permute-start | bytes 983048 | tf_op jit(solution)/shard_map/ppermute | solution.py:776
  31.4 16.4 %collective-permute-start.8 = (f32[40,2048]{1,0:T(8,128)S(1)}, f32[40,2048]{1,0:T(8,128)S(1)}, u32[]{:S(2)}, u32[]{:S(2)}) collective-permute-start(f32[40,2048]{1,0:T(8,128)S(1)} %get-tuple-element.67.refs_0_), channel_id=1, source_target_pairs={{0,6},{2,0},{4,2},{6,4},{1,7},{3,1},{5,3},{7,5},{8,14},{10,8},{12,... | collective-permute-start | bytes 983048 | tf_op jit(solution)/shard_map/ppermute | solution.py:776
  32.6 39.1 %collective-permute-start.13 = (f32[40,2048]{1,0:T(8,128)S(1)}, f32[40,2048]{1,0:T(8,128)S(1)}, u32[]{:S(2)}, u32[]{:S(2)}) collective-permute-start(f32[40,2048]{1,0:T(8,128)S(1)} %get-tuple-element.67.refs_0_), channel_id=1, source_target_pairs={{0,1},{1,0},{2,3},{3,2},{4,5},{5,4},{6,7},{7,6},{8,9},{9,8},{10,11... | collective-permute-start | bytes 983048 | tf_op jit(solution)/shard_map/ppermute | solution.py:765
  40.2 31.6 %collective-permute-start.16 = (f32[40,2048]{1,0:T(8,128)S(1)}, f32[40,2048]{1,0:T(8,128)}, u32[]{:S(2)}, u32[]{:S(2)}) collective-permute-start(f32[40,2048]{1,0:T(8,128)S(1)} %collective-permute-done.10.refs_3_), channel_id=1, source_target_pairs={{0,1},{1,0},{2,3},{3,2},{4,5},{5,4},{6,7},{7,6},{8,9},{9,8},{10,11... | collective-permute-start | bytes 983048 | tf_op jit(solution)/shard_map/ppermute | solution.py:765
  47.8 23.9 %collective-permute-start.15 = (f32[40,2048]{1,0:T(8,128)S(1)}, f32[40,2048]{1,0:T(8,128)}, u32[]{:S(2)}, u32[]{:S(2)}) collective-permute-start(f32[40,2048]{1,0:T(8,128)S(1)} %collective-permute-done.9.refs_2_), channel_id=1, source_target_pairs={{0,1},{1,0},{2,3},{3,2},{4,5},{5,4},{6,7},{7,6},{8,9},{9,8},{10,11... | collective-permute-start | bytes 983048 | tf_op jit(solution)/shard_map/ppermute | solution.py:765
  47.8 23.9 %collective-permute-start.14 = (f32[40,2048]{1,0:T(8,128)S(1)}, f32[40,2048]{1,0:T(8,128)}, u32[]{:S(2)}, u32[]{:S(2)}) collective-permute-start(f32[40,2048]{1,0:T(8,128)S(1)} %collective-permute-done.8.refs_1_), channel_id=1, source_target_pairs={{0,1},{1,0},{2,3},{3,2},{4,5},{5,4},{6,7},{7,6},{8,9},{9,8},{10,11... | collective-permute-start | bytes 983048 | tf_op jit(solution)/shard_map/ppermute | solution.py:765
  48.5 1.8 %collective-permute-start.11 = (f32[1,32768]{1,0:T(1,128)S(1)}, f32[1,32768]{1,0:T(1,128)S(1)}, u32[]{:S(2)}, u32[]{:S(2)}) collective-permute-start(f32[1,32768]{1,0:T(1,128)S(1)} %get-tuple-element.71), channel_id=1, source_target_pairs={{0,1},{1,0},{2,3},{3,2},{4,5},{5,4},{6,7},{7,6},{8,9},{9,8},{10,11... | collective-permute-start | bytes 393224 | tf_op jit(solution)/shard_map/ppermute | solution.py:765
  50.2 1.2 %collective-permute-start.7 = (f32[1,128]{1,0:T(1,128)S(1)}, f32[1,128]{1,0:T(1,128)S(1)}, u32[]{:S(2)}, u32[]{:S(2)}) collective-permute-start(f32[1,128]{1,0:T(1,128)S(1)} %get-tuple-element.64.mine), channel_id=1, source_target_pairs={{0,1},{1,0},{2,3},{3,2},{4,5},{5,4},{6,7},{7,6},{8,9},{9,8},{10,11... | collective-permute-start | bytes 1544 | tf_op jit(solution)/shard_map/ppermute | solution.py:765
  51.4 17.9 %collective-permute-start.12 = (f32[1,32768]{1,0:T(1,128)S(1)}, f32[1,32768]{1,0:T(1,128)S(1)}, u32[]{:S(2)}, u32[]{:S(2)}) collective-permute-start(f32[1,32768]{1,0:T(1,128)S(1)} %get-tuple-element.72), channel_id=1, source_target_pairs={{1,2},{3,4},{5,6},{2,1},{4,3},{6,5},{9,10},{11,12},{13,14},{10,9},... | collective-permute-start | bytes 393224 | tf_op jit(solution)/shard_map/ppermute | solution.py:771
  54.3 26.1 %all-to-all-start = ((f32[128,1,128]{2,1,0:T(1,128)}), f32[128,1,128]{2,1,0:T(1,128)S(1)}, u32[]{:S(2)}, u32[]{:S(2)}) async-start(f32[128,1,128]{2,1,0:T(1,128)} %pair.1), calls=%async_computation | async-start | bytes 131072 | tf_op jit(solution)/shard_map/all_to_all | solution.py:844
